TPU v7x, 128 devices: a whole 4x4x4 slice. The times are simulated.
128 devices in a mesh: tm: 64 (over y, z, x), sens: 2 (over core).
Axes of the slice: x: 4, y: 4, z: 4, core: 2. Of those that a mesh axis runs over, the one named last changes fastest.
Arguments:
- telemetry: float32 [32768, 512], P('tm', 'sens'), may hold values from -6 to 6
- present: int32 [2048, 8], P('tm', 'sens'), may hold values 0 or 1
- transition: float32 [128, 128], replicated, may hold values from -1 to 1, as said below
- sensing: float32 [512, 128], P('sens'), may hold values from -3 to 3, as said below
- filter_gain: float32 [128, 512], P(None, 'sens'), may hold values from -1 to 1, as said below
- smooth_gain: float32 [128, 128], replicated, may hold values from -1 to 1, as said below
- initial_state: float32 [128], replicated, may hold values from -6 to 6
Outputs:
- new_transition: float32 [128, 128], replicated
- new_sensing: float32 [512, 128], P('sens')
- smoothed: float32 [32768, 128], P('tm')
Inputs may be any that keep to these rules, and one draw needn't show every extreme that they name: `transition`: the previous iteration's estimate of the transition matrix; every entry lies between -1 and 1. `sensing`: the previous iteration's estimate of the observation matrix; every entry lies between -3 and 3. `filter_gain`: the previous iteration's steady filter gain; every entry lies between -1 and 1. `smooth_gain`: the previous iteration's steady smoother gain; every entry lies between -1 and 1.
All inputs are finite; a program needn't handle non-finite values. No bound on the sum of `present` on one device may be relied on, other than what follows from the above.
Results may differ from a plain program's by a relative error of at most 0.014.
Values sent between devices are 32-bit elements; how exact they have to be, the bound alone decides.
No kernel may reach another device: no remote copies, remote signals or barrier semaphores. Data moves between devices by JAX's collectives and lax.ppermute only.
A program may use at most 128 MiB of HBM per device.

v0:
```python
import jax
import jax.numpy as jnp
from jax import lax
from jax.sharding import PartitionSpec as P

HIGHEST = lax.Precision.HIGHEST
RIDGE = 0.001


def entering(value, axis, join, neutral, backward):
    count, mine = (lax.axis_size(axis), lax.axis_index(axis))
    pieces = jax.tree.map(lambda part: lax.all_gather(part, axis), value)
    if backward:
        pieces = jax.tree.map(lambda part: part[::-1], pieces)
        mine = count - 1 - mine
    subtotal = jax.tree.map(
        lambda part, zero: jnp.full_like(part, 0) + jnp.asarray(zero, part.dtype), value, neutral
    )

    def lap(position, subtotal):
        longer = join(subtotal, jax.tree.map(lambda part: part[position], pieces))
        return jax.tree.map(lambda new, old: jnp.where(position < mine, new, old), longer, subtotal)

    return lax.fori_loop(0, count - 1, lap, subtotal)


def solve_rows(gram, cross, ridge_term):
    factor = jnp.linalg.cholesky(gram + ridge_term * jnp.eye(gram.shape[0], dtype=jnp.float32))
    return jax.scipy.linalg.cho_solve((factor, True), cross.T).T


def combine_maps(earlier, latter):
    joined = jnp.einsum("...ab,...bc->...ac", latter[0], earlier[0], precision=HIGHEST)
    shifted = jnp.einsum("...ab,...b->...a", latter[0], earlier[1], precision=HIGHEST) + latter[1]
    return (joined, shifted)


def run_blocks(advance, inputs, starting):
    current = starting
    collected = []
    for offset in range(inputs.shape[1]):
        current = advance(current) + inputs[:, offset]
        collected.append(current)
    return jnp.stack(collected, axis=1)


def local_chain(powered, inputs, advance):
    zero_start = jnp.zeros((inputs.shape[0], inputs.shape[2]), jnp.float32)
    block_ends = run_blocks(advance, inputs, zero_start)[:, -1]
    return lax.associative_scan(combine_maps, (powered, block_ends), axis=0)


def finish_chain(prefix_maps, prefix_shifts, incoming, inputs, advance):
    reached = jnp.einsum("kab,b->ka", prefix_maps, incoming, precision=HIGHEST) + prefix_shifts
    starting = jnp.concatenate([incoming[None], reached[:-1]], axis=0)
    return run_blocks(advance, inputs, starting).reshape(-1, inputs.shape[2])


def on_device(telemetry, present, transition, sensing, filter_gain, smooth_gain, initial_state):
    state_width = transition.shape[0]
    row_count = telemetry.shape[0]
    seg_count = present.shape[0]
    seg_len = row_count // seg_count
    local_blocks = present.shape[1]
    local_sensors = telemetry.shape[1]
    block_size = local_sensors // local_blocks
    flag_values = present.astype(jnp.float32)
    masked = (
        telemetry.reshape(seg_count, seg_len, local_blocks, block_size)
        * flag_values[:, None, :, None]
    ).reshape(row_count, local_sensors)
    pushes = jnp.einsum("tn,sn->ts", masked, filter_gain, precision=HIGHEST)
    gain_blocks = filter_gain.reshape(state_width, local_blocks, block_size)
    sense_blocks = sensing.reshape(local_blocks, block_size, state_width)
    couplings = jnp.einsum("sgb,gbr->gsr", gain_blocks, sense_blocks, precision=HIGHEST)
    all_couplings, all_flags = (
        lax.all_gather(couplings, "sens", axis=0, tiled=True),
        lax.all_gather(flag_values, "sens", axis=1, tiled=True),
    )
    corrections = jnp.einsum("kg,gsr->ksr", all_flags, all_couplings, precision=HIGHEST)
    pushes = lax.psum(pushes, "sens")
    step_maps = transition[None] - jnp.einsum(
        "ksr,rq->ksq", corrections, transition, precision=HIGHEST
    )
    push_blocks = pushes.reshape(seg_count, seg_len, state_width)

    def forward_step(current):
        return jnp.einsum("kab,kb->ka", step_maps, current, precision=HIGHEST)

    powered = step_maps
    for bit_level in range(seg_len.bit_length() - 1):
        powered = jnp.einsum("kab,kbc->kac", powered, powered, precision=HIGHEST)
    prefix_maps, prefix_shifts = local_chain(powered, push_blocks, forward_step)
    identity_map = jnp.eye(state_width, dtype=jnp.float32)
    zero_shift = jnp.zeros((state_width,), jnp.float32)
    carried_map, carried_shift = entering(
        (prefix_maps[-1], prefix_shifts[-1]), "tm", combine_maps, (identity_map, zero_shift), False
    )
    incoming = jnp.dot(carried_map, initial_state, precision=HIGHEST) + carried_shift
    filtered = finish_chain(prefix_maps, prefix_shifts, incoming, push_blocks, forward_step)
    mixing = jnp.dot(smooth_gain, transition, precision=HIGHEST)
    drives = filtered - jnp.einsum("ta,ba->tb", filtered, mixing, precision=HIGHEST)
    drive_blocks = drives[::-1].reshape(seg_count, seg_len, state_width)

    def backward_step(current):
        return jnp.einsum("ab,kb->ka", smooth_gain, current, precision=HIGHEST)

    gain_power = smooth_gain
    for bit_level in range(seg_len.bit_length() - 1):
        gain_power = jnp.dot(gain_power, gain_power, precision=HIGHEST)
    back_maps, back_shifts = local_chain(
        jnp.broadcast_to(gain_power, (seg_count, state_width, state_width)),
        drive_blocks,
        backward_step,
    )
    device_map = back_maps[-1]
    device_shift = back_shifts[-1]
    is_last = lax.axis_index("tm") == lax.axis_size("tm") - 1
    final_state = jnp.dot(transition, filtered[-1], precision=HIGHEST)
    top_shift = device_shift + jnp.dot(device_map, final_state, precision=HIGHEST)
    send_shift = jnp.where(is_last, top_shift, device_shift)
    send_map = jnp.where(is_last, 0.0, device_map)
    unused_map, from_above = entering(
        (send_map, send_shift), "tm", combine_maps, (identity_map, zero_shift), True
    )
    incoming_back = jnp.where(is_last, final_state, from_above)
    smoothed = finish_chain(back_maps, back_shifts, incoming_back, drive_blocks, backward_step)[
        ::-1
    ]
    keep_last = jnp.where(is_last, 0.0, 1.0).astype(jnp.float32)
    pair_weight = jnp.concatenate(
        [jnp.ones((row_count - 1,), jnp.float32), keep_last[None]], axis=0
    )
    following = jnp.concatenate([smoothed[1:], incoming_back[None]], axis=0)
    weighted_prior = smoothed * pair_weight[:, None]
    lag_gram = jnp.einsum("ta,tb->ab", weighted_prior, smoothed, precision=HIGHEST)
    lag_cross = jnp.einsum("ta,tb->ab", following, weighted_prior, precision=HIGHEST)
    row_flags = jnp.repeat(flag_values, seg_len, axis=0)
    sensor_grams = jnp.einsum("tg,ta,tb->gab", row_flags, smoothed, smoothed, precision=HIGHEST)
    sensor_cross = jnp.einsum("tn,ta->na", masked, smoothed, precision=HIGHEST)
    grams = jnp.concatenate([lag_gram[None], sensor_grams], axis=0)
    cross = jnp.concatenate([lag_cross, sensor_cross], axis=0)
    ridge_term = RIDGE * row_count * lax.axis_size("tm")
    grams, cross = lax.psum((grams, cross), "tm")
    new_transition = solve_rows(grams[0], cross[:state_width], ridge_term)
    sensor_rows = cross[state_width:].reshape(local_blocks, block_size, state_width)
    new_sensing = jax.vmap(solve_rows, (0, 0, None))(grams[1:], sensor_rows, ridge_term).reshape(
        local_sensors, state_width
    )
    return (new_transition, new_sensing, smoothed)


def solution(mesh):
    placed = (P("tm", "sens"), P("tm", "sens"), P(), P("sens", None), P(None, "sens"), P(), P())
    return jax.shard_map(
        on_device,
        mesh=mesh,
        in_specs=placed,
        out_specs=(P(), P("sens", None), P("tm", None)),
        check_vma=False,
    )
```

profile of v0, /device:TPU:0, one launch (start us, length us, event | category | flops | bytes accessed | tf_op | source)
XLA Modules:
  0.0 1189.1 jit_solution(1447229856769241398)
XLA Ops:
  15.1 2.6 all_gather.22
  19.6 3.3 fusion.25
  29.4 11.9 fusion.235
  52.5 3.8 pad.129
  56.3 3.8 pad.130
  63.7 5.7 pad.131
  69.4 5.7 pad.132
  75.1 3.0 fusion.44
  80.4 10.1 pad.134
  90.6 10.2 pad.133
  118.6 3.8 pad.149
  122.4 3.7 pad.150
  130.9 5.7 pad.151
  136.6 5.7 pad.152
  142.4 2.8 add.561
  147.2 10.2 pad.153
  157.4 10.2 pad.154
  170.5 3.3 fusion.236
  176.8 3.3 fusion.238
  180.8 3.3 fusion.239
  184.9 3.4 fusion.240
  189.0 3.3 fusion.241
  193.1 3.5 fusion.242
  197.3 3.3 fusion.243
  201.4 3.3 fusion.244
  205.5 3.3 fusion.245
  209.6 3.3 fusion.246
  213.6 3.7 fusion.247
  218.1 3.4 fusion.248
  222.2 3.3 fusion.249
  226.3 3.3 fusion.250
  230.3 3.3 fusion.251
  234.4 3.3 fusion.252
  238.5 3.2 fusion.37
  249.2 2.8 fusion.48
  252.1 177.1 %all-gather.2 = f32[64,1,128]{2,1,0:T(1,128)S(1)} all-gather(f32[1,1,128]{2,1,0:T(1,128)S(1)} %add_bitcast_fusion.3), channel_id=1, replica_groups=mesh['tm'=64,'sens'=2] {'tm'}, dimensions={0}, use_global_device_ids=true | all-gather | bytes 33280 | tf_op jit(solution)/shard_map/all_gather | solution.py:12
  429.3 136.5 %while.30 = (s32[]{:T(128)}, f32[128,128]{1,0:T(8,128)S(1)}, f32[128]{0:T(128)S(1)}, s32[]{:T(128)}, f32[64,128,128]{2,1,0:T(8,128)}, /*index=5*/f32[64,128]{1,0:T(8,128)S(1)}, s32[]{:T(128)}, s32[]{:T(128)}) while((s32[]{:T(128)}, f32[128,128]{1,0:T(8,128)S(1)}, f32[128]{0:T(128)S(1)}, s32[]{:T(128)}, f32[64,128,128]{2,1,0:T(8,128)}, ...), condition=%wide.region_2.3_spmd.clone, body=%wide.region_1.2_spmd.clone.sunk | while | flops 25379332 | bytes 465000 | solution.py:24
  566.0 4.2 fusion.23
  570.2 3.3 fusion.253
  574.2 3.3 fusion.254
  578.3 3.3 fusion.255
  582.4 3.3 fusion.256
  586.5 3.7 fusion.257
  590.9 3.3 fusion.258
  595.0 3.3 fusion.259
  599.1 3.3 fusion.260
  603.2 3.3 fusion.261
  607.3 3.3 fusion.262
  611.3 3.5 fusion.263
  615.6 3.3 fusion.264
  619.7 3.3 fusion.265
  623.7 3.3 fusion.266
  627.8 3.3 fusion.267
  631.9 3.7 fusion.268
  645.1 2.4 fusion.58
  688.2 168.5 %all-gather.3 = f32[64,1,128]{2,1,0:T(1,128)S(1)} all-gather(f32[1,1,128]{2,1,0:T(1,128)S(1)} %fusion.33), channel_id=2, replica_groups=mesh['tm'=64,'sens'=2] {'tm'}, dimensions={0}, use_global_device_ids=true | all-gather | bytes 33280 | tf_op jit(solution)/shard_map/all_gather | solution.py:12
  856.7 4.7 rev.12
  861.4 67.3 %while.31 = (s32[]{:T(128)}, f32[128]{0:T(128)S(1)}, s32[]{:T(128)}, f32[64,128,128]{2,1,0:T(8,128)}, f32[64,128]{1,0:T(8,128)S(1)}, /*index=5*/s32[]{:T(128)}, s32[]{:T(128)}) while((s32[]{:T(128)}, f32[128]{0:T(128)S(1)}, s32[]{:T(128)}, f32[64,128,128]{2,1,0:T(8,128)}, f32[64,128]{1,0:T(8,128)S(1)}, /*index=5*/s32[]{:T(128)}, ...), condition=%wide.region_4.5_spmd.clone, body=%wide.region_3.4_spmd.clone.sunk | while | flops 197124 | bytes 71263 | solution.py:24
  928.8 3.6 fusion.21
  942.5 122.1 %all-reduce.47.cloned.1.call-done = (f32[384,128]{1,0:T(8,128)}, f32[5,128,128]{1,2,0:T(8,128)}) async-done(((f32[384,128]{1,0:T(8,128)}, f32[5,128,128]{1,2,0:T(8,128)}), (f32[384,128]{1,0:T(8,128)}, f32[5,128,128]{1,2,0:T(8,128)})) %all-reduce.47.cloned.1.call-update) | async-done | bytes 524304 | tf_op jit(solution)/shard_map/psum | solution.py:144
  1067.6 46.9 %custom-call.22 = f32[4,128,128]{2,1,0:T(8,128)S(1)} custom-call(f32[4,128,128]{2,1,0:T(8,128)S(1)} %fusion.95), custom_call_target="Cholesky" | custom-call | tf_op jit(solution)/shard_map/vmap(jit(cholesky))/cholesky | solution.py:28
  1114.8 39.5 %custom-call.23 = f32[4,1,128,128]{2,3,1,0:T(8,128)S(1)} custom-call(f32[4,1,128,128]{3,2,1,0:T(8,128)S(1)} %select_bitcast_fusion), custom_call_target="InvertDiagBlocksLowerTriangular" | custom-call | tf_op jit(solution)/shard_map/vmap(jit(_cho_solve))/triangular_solve | solution.py:29
  1157.0 11.7 cholesky.31
  1170.3 9.8 custom-call.21
  (816 shorter events, 361.3 us)
Async XLA Ops:
  8.0 6.5 copy-start
  8.0 2.3 copy-start.28
  8.0 168.0 %all-reduce.45.cloned.1.call-start = ((), (), s32[]{:S(2)}) async-start(), calls=%async_computation.1 | async-start | bytes 524288 | tf_op jit(solution)/shard_map/psum | solution.py:81
  9.5 1.7 copy-start.29
  12.6 7.0 copy-start.25
  12.6 416.6 %all-gather.7.cloned.1.call-start = ((), (), s32[]{:S(2)}) async-start(), calls=%async_computation | async-start | bytes 4259840 | tf_op jit(solution)/shard_map/all_gather | solution.py:12
  41.3 1.9 copy-start.3
  43.1 1.8 copy-start.13
  44.9 6.8 slice-start.3
  60.1 1.8 copy-start.16
  60.1 1.8 copy-start.17
  75.1 3.1 slice-start
  75.1 4.1 copy-start.9
  75.1 4.1 copy-start.10
  90.6 11.7 copy-start.2
  102.2 754.4 %all-gather.9.cloned.1.call-start = ((), (), s32[]{:S(2)}) async-start(), calls=%async_computation.2 | async-start | bytes 4259840 | tf_op jit(solution)/shard_map/all_gather | solution.py:12
  103.2 43.0 %copy-start.23 = (f32[128,128]{1,0:T(8,128)}, f32[128,128]{1,0:T(8,128)S(1)}, u32[]{:S(2)}) copy-start(f32[128,128]{1,0:T(8,128)S(1)} %fusion.272) | copy-start | bytes 196612
  107.0 10.8 slice-start.2
  122.4 7.7 slice-start.1
  142.4 2.8 copy-start.7
  142.4 2.8 copy-start.8
  157.4 12.8 %copy-start.26 = (f32[128,128]{1,0:T(8,128)S(1)}, f32[128,128]{1,0:T(8,128)}, u32[]{:S(2)}) copy-start(f32[128,128]{1,0:T(8,128)} %param.13) | copy-start | bytes 196612
  169.1 895.5 %all-reduce.47.cloned.1.call-start = ((), (), s32[]{:S(2)}) async-start(), calls=%async_computation.3 | async-start | bytes 1048576 | tf_op jit(solution)/shard_map/psum | solution.py:144
  170.4 3.4 copy-start.30
  238.5 190.7 %copy-start.67 = (f32[128]{0:T(128)S(1)}, f32[128]{0:T(128)}, u32[]{:S(2)}) copy-start(f32[128]{0:T(128)} %custom-call.24) | copy-start | bytes 1540
  246.7 319.1 %copy-start.66 = (f32[128]{0:T(128)S(1)}, f32[128]{0:T(128)}, u32[]{:S(2)}) copy-start(f32[128]{0:T(128)} %param.17) | copy-start | bytes 1540
  635.6 9.5 copy-start.24
  636.4 15.1 %copy-start.6 = (f32[16,128,128]{2,1,0:T(8,128)S(1)}, f32[16,128,128]{2,1,0:T(8,128)}, u32[]{:S(2)}) copy-start(f32[16,128,128]{2,1,0:T(8,128)} %copy-done.5) | copy-start | bytes 3145732
  637.6 33.1 %copy-start.19 = (f32[4,128,128]{2,1,0:T(8,128)S(1)}, f32[4,128,128]{2,1,0:T(8,128)}, u32[]{:S(2)}) copy-start(f32[4,128,128]{2,1,0:T(8,128)} %copy-done.18) | copy-start | bytes 786436
  638.0 3.3 copy-start.32
  638.1 3.5 copy-start.34
  638.1 3.5 copy-start.36
  638.1 3.5 copy-start.38
  638.1 3.5 copy-start.40
  638.1 3.5 copy-start.42
  638.1 3.5 copy-start.44
  638.1 3.5 copy-start.46
  638.1 3.5 copy-start.48
  638.1 3.5 copy-start.50
  638.1 3.5 copy-start.52
  638.2 3.5 copy-start.54
  638.9 48.2 %copy-start.11 = (f32[32,128,128]{2,1,0:T(8,128)S(1)}, f32[32,128,128]{2,1,0:T(8,128)}, u32[]{:S(2)}) copy-start(f32[32,128,128]{2,1,0:T(8,128)} %pad.153) | copy-start | bytes 6291460
  856.6 4.7 copy-start.65
  928.7 3.8 copy-start.61
  928.7 4.0 copy-start.59
  928.7 4.2 copy-start.57
  928.7 4.5 copy-start.55
  928.7 4.7 copy-start.53
  928.7 4.9 copy-start.51
  928.8 5.1 copy-start.49
  928.8 5.4 copy-start.47
  928.8 5.6 copy-start.45
  928.8 5.8 copy-start.43
  928.8 6.0 copy-start.41
  928.8 6.3 copy-start.39
  928.8 6.5 copy-start.37
  928.8 6.7 copy-start.35
  928.8 6.9 copy-start.33
  932.4 4.2 copy-start.15
  933.2 4.5 copy-start.63
  936.2 3.2 copy-start.62
  936.5 4.9 copy-start.4
  1064.6 89.7 %copy-start.31 = (f32[384,128]{1,0:T(8,128)S(1)}, f32[384,128]{1,0:T(8,128)}, u32[]{:S(2)}) copy-start(f32[384,128]{1,0:T(8,128)} %get-tuple-element.301) | copy-start | bytes 589828
  1066.5 114.9 %copy-start.1 = (f32[256,128]{1,0:T(8,128)S(1)}, f32[256,128]{1,0:T(8,128)}, u32[]{:S(2)}) copy-start(f32[256,128]{1,0:T(8,128)} %param.14) | copy-start | bytes 393220
  (12 other events, 9.8 us)
Sparse Core Ops, SparseCore 0:
  12.7 26.2 all-reduce.44
Sparse Core Ops, SparseCore 1:
  102.3 71.4 all-gather.6
  177.1 66.5 all-gather.8
  942.2 122.3 all-reduce.46
where the time goes:
time: 1210 us; the launch traced here: 1190 us
  matrix products  397 us (33%)
  blocking collectives  350 us (29%)
  other arithmetic  172 us (14%)
  local copies, waits for them, and re-layouts  127 us (10%)
  waiting for transfers between devices  122 us (10%)
  between operations  17.8 us (1%)
    all_gather x2, blocking collectives, entering(): pieces = jax.tree.map(lambda part: lax.all_gather(part, axis), value)  346 us
    dot_general x144, matrix products, combine_maps(): jnp.einsum('...ab,...b->...a', latter[0], earlier[1], precision=HIGHEST)  156 us
    psum x1, waiting for transfers between devices, on_device(): grams, cross = lax.psum((grams, cross), 'tm')  122 us
    dot_general x32, matrix products, forward_step(): return jnp.einsum('kab,kb->ka', step_maps, current, precision=HIGHEST)  108 us
    pad x32, local copies, waits for them, and re-layouts, local_chain(): return lax.associative_scan(combine_maps, (powered, block_ends), axis=0)  88.7 us
    dot_general x81, matrix products, combine_maps(): jnp.einsum('...ab,...bc->...ac', latter[0], earlier[0], precision=HIGHEST)  82.2 us
    another operation x7, other arithmetic, solve_rows(): jnp.linalg.cholesky(gram + ridge_term * jnp.eye(gram.shape[0], dtype=jnp....  59.5 us
    another operation x5, other arithmetic, solve_rows(): return jax.scipy.linalg.cho_solve((factor, True), cross.T).T  50.1 us
  transfers between devices with their start and end apart: 4, of which 1 were waited for; matrix products, arithmetic and copies ran while one was open for 41% of the time, Pallas kernels for 0%

commit v1 on v0

v1 whole, which is shorter than its diff:
```python
import functools

import jax
import jax.numpy as jnp
from jax import lax
from jax.experimental import pallas as pl
from jax.experimental.pallas import tpu as pltpu
from jax.sharding import PartitionSpec as P

RIDGE = 0.001
F32 = jnp.float32
BF16 = jnp.bfloat16
W = 128
SEGS = 16
LEN = 16
ROWS = SEGS * LEN
PACK = W + 8
VMEM_LIMIT = 56 * 1024 * 1024


def halves(value):
    high = value.astype(BF16)
    low = (value - high.astype(F32)).astype(BF16)
    return high, low


def wide(value):
    high, low = halves(value)
    return jnp.concatenate([high, low], axis=1)


def times(left_wide, right_wide):
    stacked = jnp.concatenate([right_wide, right_wide], axis=0)
    out = jnp.dot(left_wide, stacked, preferred_element_type=F32)
    return out[:, :W] + out[:, W:]


def moved(rows, dev):
    return rows + times(wide(rows), dev)


def chained(first, second, second_wide):
    return first + second + times(wide(first), second_wide)


def identity():
    rows = lax.broadcasted_iota(jnp.int32, (W, W), 0)
    cols = lax.broadcasted_iota(jnp.int32, (W, W), 1)
    return jnp.where(rows == cols, 1.0, 0.0).astype(F32)


def call(kernel, out_shapes, n_smem, n_in, scratch=()):
    smem = [pl.BlockSpec(memory_space=pltpu.SMEM)] * n_smem
    vmem = [pl.BlockSpec(memory_space=pltpu.VMEM)] * n_in
    single = not isinstance(out_shapes, (list, tuple))
    outs = [out_shapes] if single else list(out_shapes)
    out_specs = [pl.BlockSpec(memory_space=pltpu.VMEM)] * len(outs)
    return pl.pallas_call(
        kernel,
        out_shape=outs[0] if single else tuple(outs),
        in_specs=smem + vmem,
        out_specs=out_specs[0] if single else tuple(out_specs),
        scratch_shapes=list(scratch),
        compiler_params=pltpu.CompilerParams(vmem_limit_bytes=VMEM_LIMIT),
    )


def shape(*dims, dtype=F32):
    return jax.ShapeDtypeStruct(dims, dtype)


def mask_of(flags, rows, segs):
    cols = flags.shape[1] * 64
    spread = (
        lax.broadcasted_iota(jnp.int32, (flags.shape[1], cols), 0)
        == lax.broadcasted_iota(jnp.int32, (flags.shape[1], cols), 1) // 64
    )
    by_sensor = jnp.dot(flags.astype(BF16), spread.astype(BF16), preferred_element_type=F32)
    repeat = (
        lax.broadcasted_iota(jnp.int32, (rows, segs), 0) // LEN
        == lax.broadcasted_iota(jnp.int32, (rows, segs), 1)
    )
    return jnp.dot(repeat.astype(BF16), by_sensor.astype(BF16), preferred_element_type=F32)


def push_kernel(where, tel, flags, gain, mine, theirs):
    gain_t = gain[...].T
    packed = wide(gain_t)
    fl = flags[...]
    for out, core in ((theirs, 1 - where[3]), (mine, where[3])):
        start = pl.multiple_of(core * ROWS, ROWS)
        seg_start = pl.multiple_of(core * SEGS, SEGS)
        mask = mask_of(flags[pl.ds(seg_start, SEGS), :], ROWS, SEGS)
        high, low = halves(tel[pl.ds(start, ROWS), :] * mask)
        total = jnp.dot(high, packed, preferred_element_type=F32) + jnp.dot(
            low, packed, preferred_element_type=F32
        )
        out[...] = total[:, :W] + total[:, W:]


def maps_kernel(
    where, flags_own, flags_other, trans, gain_own, gain_other, sense_own, sense_other,
    powers, tree, whole, removed, single,
):
    a = trans[...]
    a_wide = wide(a)
    lane = lax.broadcasted_iota(jnp.int32, (W, 2 * W), 1) // 64
    for side, (gain, sense) in enumerate(((gain_own, sense_own), (gain_other, sense_other))):
        seen = times(wide(sense[...]), a_wide)
        seen_high, seen_low = halves(seen.T)
        gain_wide = wide(gain[...].T)
        for g in range(4):
            zero = jnp.zeros_like(seen_high)
            part = jnp.dot(
                jnp.where(lane == g, seen_high, zero), gain_wide, preferred_element_type=F32
            ) + jnp.dot(jnp.where(lane == g, seen_low, zero), gain_wide, preferred_element_type=F32)
            removed[side * 4 + g] = part[:, :W] + part[:, W:]
    base = a.T - identity()
    single[...] = base
    batch = 4

    def group(i, carry):
        devs = []
        for j in range(batch):
            k = i * batch + j
            row = where[3] * SEGS + k
            dev = single[...]
            for g in range(4):
                dev = dev - flags_own[row, g] * removed[g]
                dev = dev - flags_other[row, g] * removed[4 + g]
            devs.append(dev)
        for level in range(4):
            for j in range(batch):
                packed = wide(devs[j])
                powers[i * batch + j, level] = packed
                devs[j] = 2.0 * devs[j] + times(packed, packed)
        for j in range(batch):
            powers[i * batch + j, 4] = wide(devs[j])
            whole[i * batch + j] = devs[j]
        return carry

    lax.fori_loop(0, SEGS // batch, group, 0)
    count, base_at, source_at = SEGS, SEGS, 0
    while count > 1:
        for p in range(count // 2):
            second = whole[source_at + 2 * p + 1]
            joined = chained(whole[source_at + 2 * p], second, wide(second))
            whole[base_at + p] = joined
            tree[base_at - SEGS + p] = wide(joined)
        source_at = base_at
        count //= 2
        base_at += count


def seg_scan(rows, powers):
    row_at = lax.broadcasted_iota(jnp.int32, (ROWS, W), 0) % LEN
    for level in range(4):
        reach = 1 << level
        before = jnp.where(row_at >= reach, pltpu.roll(rows, reach, 0), 0.0)
        packed = wide(before)
        parts = [
            times(packed[k * LEN : (k + 1) * LEN], powers[k, level]) for k in range(SEGS)
        ]
        rows = rows + before + jnp.concatenate(parts, axis=0)
    return rows


def shift_kernel(mine, received, powers, tree, whole, inputs, ends, packed):
    rows = mine[...] + received[...]
    inputs[...] = rows
    reached = seg_scan(rows, powers)
    level = [reached[k * LEN + LEN - 1 : (k + 1) * LEN] for k in range(SEGS)]
    ends[0:SEGS] = jnp.concatenate(level, axis=0)
    maps = [powers[k, 4] for k in range(SEGS)]
    at, tree_at = SEGS, 0
    while len(level) > 1:
        level = [
            moved(jnp.broadcast_to(level[2 * p], (8, W)), maps[2 * p + 1])[0:1] + level[2 * p + 1]
            for p in range(len(level) // 2)
        ]
        maps = [tree[tree_at + p] for p in range(len(level))]
        tree_at += len(level)
        for p, row in enumerate(level):
            ends[at + p : at + p + 1] = row
        at += len(level)
    packed[0:W] = whole[2 * SEGS - 2]
    packed[W:PACK] = jnp.broadcast_to(level[0], (8, W))


def join2(first, second):
    second_dev = second[0:W]
    second_wide = wide(second_dev)
    dev = chained(first[0:W], second_dev, second_wide)
    row = moved(first[W:PACK], second_wide) + second[W:PACK]
    return dev, row


def pair_kernel(where, own, other, out):
    core = where[3]
    mine, theirs = own[...], other[...]
    first = jnp.where(core == 0, mine, theirs)
    second = jnp.where(core == 0, theirs, mine)
    dev, row = join2(first, second)
    out[0:W] = dev
    out[W:PACK] = row


def four_kernel(axis, where, own, r1, r2, r3, out, ordered):
    at = where[axis]
    for k, ref in enumerate((own, r1, r2, r3)):
        ordered[at ^ k] = ref[...]
    dev0, row0 = join2(ordered[0], ordered[1])
    dev1, row1 = join2(ordered[2], ordered[3])
    wide1 = wide(dev1)
    out[0:W] = chained(dev0, dev1, wide1)
    out[W:PACK] = moved(row0, wide1) + row1


def filter_kernel(
    where, y0, y1, y2, y3, z0, z1, z2, z3, x0, x1, x2, x3, c0, c1,
    initial, inputs, ends, powers, tree, gain_powers, drive_map, trans,
    drives, final, shift, ordered,
):
    state = jnp.broadcast_to(initial[...], (8, W))
    for axis, refs in ((0, (y0, y1, y2, y3)), (1, (z0, z1, z2, z3)), (2, (x0, x1, x2, x3)), (3, (c0, c1))):
        at = where[axis]
        for k, ref in enumerate(refs):
            ordered[4 * axis + (at ^ k)] = ref[...]
        for j in range(len(refs) - 1):
            slot = 4 * axis + j
            ahead = moved(state, wide(ordered[slot, 0:W])) + ordered[slot, W:PACK]
            state = jnp.where(j < at, ahead, state)
    starts = {0: state}
    for span, maps_at, ends_at in ((8, 12, 28), (4, 8, 24), (2, 0, 16), (1, -1, 0)):
        for begin in range(0, SEGS, 2 * span):
            p = begin // span
            dev = powers[p, 4] if span == 1 else tree[maps_at + p]
            starts[begin + span] = moved(starts[begin], dev) + ends[ends_at + p : ends_at + p + 1]
    entry = [moved(starts[k], powers[k, 0]) for k in range(SEGS)]
    spread = jnp.concatenate(
        [part for k in range(SEGS) for part in (entry[k], jnp.zeros((8, W), F32))], axis=0
    )
    row_at = lax.broadcasted_iota(jnp.int32, (ROWS, W), 0) % LEN
    rows = inputs[...] + jnp.where(row_at == 0, spread, 0.0)
    rows = seg_scan(rows, powers)
    drive = times(wide(rows), drive_map[...])
    drives[...] = drive
    last = jnp.broadcast_to(rows[ROWS - 1 : ROWS], (8, W))
    final_row = last + times(wide(last), wide(trans[...].T - identity()))
    final[...] = final_row
    top = (where[0] == 3) & (where[1] == 3) & (where[2] == 3) & (where[3] == 1)
    part = drive
    for level in (7, 6, 5, 4, 3):
        half = 1 << level
        part = part[:half] + moved(part[half:], gain_powers[level])
    for level in (2, 1, 0):
        half = 1 << level
        behind = pltpu.roll(part, 8 - half, 0)
        part = part + moved(behind, gain_powers[level])
    from_top = moved(final_row, gain_powers[8])
    shift[...] = jnp.broadcast_to(part[0:1], (8, W)) + jnp.where(top, from_top, 0.0)


def gain_kernel(smooth_gain, trans, gain_powers, drive_map):
    dev = smooth_gain[...].T - identity()
    adev = trans[...].T - identity()
    dev_wide = wide(dev)
    drive_map[...] = wide(-chained(adev, dev, dev_wide))
    for level in range(15):
        gain_powers[level] = dev_wide
        if level < 14:
            dev = 2.0 * dev + times(dev_wide, dev_wide)
            dev_wide = wide(dev)


def smooth_kernel(where, gathered, drives, final, gain_powers, smoothed, incoming):
    rows = gathered[...]
    bits = (
        where[3], where[2] & 1, where[2] >> 1, where[1] & 1, where[1] >> 1, where[0] & 1, where[0] >> 1
    )
    later = []
    for level in range(7):
        dist = 1 << level
        ahead = moved(rows, gain_powers[8 + level])
        later.append(rows[dist : dist + 1])
        other = pltpu.roll(rows, W - dist, 0)
        other_ahead = pltpu.roll(ahead, W - dist, 0)
        rows = jnp.where(bits[level] == 0, rows + other_ahead, other + ahead)
    state = jnp.zeros((8, W), F32)
    top = bits[0]
    for level in (6, 5, 4, 3, 2, 1, 0):
        nxt = moved(state, gain_powers[8 + level]) + later[level]
        state = jnp.where(bits[level] == 0, nxt, state)
        top = top & bits[level]
    state = jnp.where(top == 1, final[...], state)
    incoming[...] = state
    entry = moved(state, gain_powers[0])
    row_at = lax.broadcasted_iota(jnp.int32, (ROWS, W), 0)
    part = drives[...]
    part = part + jnp.where(row_at == ROWS - 1, jnp.broadcast_to(entry[0:1], (ROWS, W)), 0.0)
    for level in range(8):
        reach = 1 << level
        behind = jnp.where(row_at < ROWS - reach, pltpu.roll(part, ROWS - reach, 0), 0.0)
        part = part + moved(behind, gain_powers[level])
    smoothed[...] = part


def stats_kernel(where, tel, flags, own, other, smoothed, stats, full):
    core = where[3]
    full[pl.ds(pl.multiple_of(core * ROWS, ROWS), ROWS)] = own[0:ROWS]
    full[pl.ds(pl.multiple_of((1 - core) * ROWS, ROWS), ROWS)] = other[0:ROWS]
    rows = full[...]
    smoothed[...] = rows
    count = 2 * ROWS
    after = jnp.where(core == 1, own[ROWS : ROWS + 8], other[ROWS : ROWS + 8])
    row_at = lax.broadcasted_iota(jnp.int32, (count, W), 0)
    following = jnp.where(
        row_at == count - 1, jnp.broadcast_to(after[0:1], (count, W)), pltpu.roll(rows, count - 1, 0)
    )
    packed = wide(rows)
    packed_t = jnp.concatenate([rows.T.astype(BF16), (rows - rows.astype(BF16).astype(F32)).T.astype(BF16)], axis=0)
    last_chip = (where[0] == 3) & (where[1] == 3) & (where[2] == 3)
    lane_at = lax.broadcasted_iota(jnp.int32, (2 * W, count), 1)
    kept = jnp.where(last_chip & (lane_at == count - 1), jnp.zeros_like(packed_t), packed_t)

    def fold(out):
        return (out[:W, :W] + out[:W, W:]) + (out[W:, :W] + out[W:, W:])

    stats[0:W] = fold(jnp.dot(kept, packed, preferred_element_type=F32))
    stats[W : 2 * W] = fold(jnp.dot(kept, wide(following), preferred_element_type=F32))
    fl = flags[...]
    repeat = (
        lax.broadcasted_iota(jnp.int32, (2 * SEGS, count), 0)
        == lax.broadcasted_iota(jnp.int32, (2 * SEGS, count), 1) // LEN
    )
    lane_flags = lax.dot_general(
        fl.astype(BF16), repeat.astype(BF16), (((0,), (0,)), ((), ())), preferred_element_type=F32
    )
    for g in range(4):
        masked_t = packed_t * lane_flags[g : g + 1].astype(BF16)
        stats[(2 + g) * W : (3 + g) * W] = fold(jnp.dot(masked_t, packed, preferred_element_type=F32))
    high, low = halves(tel[...] * mask_of(fl, count, 2 * SEGS))
    cross = jnp.dot(packed_t, high, preferred_element_type=F32) + jnp.dot(
        packed_t, low, preferred_element_type=F32
    )
    cross = cross[:W] + cross[W:]
    stats[6 * W : 7 * W] = cross[:, :W]
    stats[7 * W : 8 * W] = cross[:, W:]


def solve_kernel(ridge, where, own, r1, r2, r3, new_transition, new_sensing, stats, left, right):
    at = where[2]
    for k, ref in enumerate((own, r1, r2, r3)):
        stats[at ^ k] = ref[...]
    eye = identity() * ridge
    left[0] = stats[0, 0:W] + eye
    right[0] = stats[0, W : 2 * W]
    for g in range(4):
        left[1 + g] = stats[1 + g // 2, (g % 2) * W : (g % 2 + 1) * W] + eye
        right[1 + g] = stats[3, (g // 2) * W : (g // 2 + 1) * W]
    row_at = lax.broadcasted_iota(jnp.int32, (W, W), 0)
    unit = 8

    def block(b, carry):
        base = pl.multiple_of(b * unit, unit)
        for j in range(unit):
            for p in range(5):
                lp, rp = left[p], right[p]
                lrow = left[p, pl.ds(base, unit)][j : j + 1]
                rrow = right[p, pl.ds(base, unit)][j : j + 1]
                scale = 1.0 / lrow[:, j : j + 1]
                lrow = lrow * scale
                rrow = rrow * scale
                column = jnp.broadcast_to(lp[:, j : j + 1], (W, W))
                here = row_at == base + j
                column = jnp.where(here, 0.0, column)
                left[p] = jnp.where(here, lrow, lp - column * lrow)
                right[p] = jnp.where(here, rrow, rp - column * rrow)
        for p in range(5):
            left[p] = pltpu.roll(left[p], W - unit, 1)
        return carry

    lax.fori_loop(0, W // unit, block, 0)
    new_transition[...] = right[0].T
    for g in range(4):
        new_sensing[g * 64 : (g + 1) * 64] = right[1 + g].T[(g % 2) * 64 : (g % 2 + 1) * 64]


STRIDE = {"x": 1, "z": 4, "y": 16}


def swap(value, axis, k):
    stride = STRIDE[axis]
    pairs = []
    for i in range(64):
        at = (i // stride) % 4
        pairs.append((i, i + ((at ^ k) - at) * stride))
    return lax.ppermute(value, "tm", pairs)


def swap_core(value):
    return lax.ppermute(value, "sens", [(0, 1), (1, 0)])


def three(value, axis):
    return [swap(value, axis, k) for k in (1, 2, 3)]


def piece(value, index, rows):
    return lax.dynamic_slice_in_dim(value, index * rows, rows, 0)


def scatter_sum(value, axis, at):
    rows = value.shape[0] // 4
    own = piece(value, at, rows)
    got = [swap(piece(value, at ^ k, rows), axis, k) for k in (1, 2, 3)]
    return (own + got[0]) + (got[1] + got[2])


def on_device(telemetry, present, transition, sensing, filter_gain, smooth_gain, initial_state):
    device = lax.axis_index("tm")
    core = lax.axis_index("sens")
    at_y, at_z, at_x = device // 16, (device // 4) % 4, device % 4
    where = jnp.stack([at_y, at_z, at_x, core]).astype(jnp.int32)
    flags = present.astype(F32)

    other_gain = swap_core(filter_gain)
    other_sensing = swap_core(sensing)
    other_flags = swap_core(flags)
    mine, theirs = call(push_kernel, [shape(ROWS, W)] * 2, 1, 3)(where, telemetry, flags, filter_gain)
    received = swap_core(theirs)
    powers, tree, whole = call(
        maps_kernel,
        [shape(SEGS, 5, W, 2 * W, dtype=BF16), shape(SEGS - 1, W, 2 * W, dtype=BF16), shape(2 * SEGS - 1, W, W)],
        3, 5,
        scratch=[pltpu.VMEM((8, W, W), F32), pltpu.VMEM((W, W), F32)],
    )(where, flags, other_flags, transition, filter_gain, other_gain, sensing, other_sensing)
    inputs, ends, packed = call(
        shift_kernel, [shape(ROWS, W), shape(32, W), shape(PACK, W)], 0, 5
    )(mine, received, powers, tree, whole)

    gain_powers, drive_map = call(
        gain_kernel, [shape(15, W, 2 * W, dtype=BF16), shape(W, 2 * W, dtype=BF16)], 0, 2
    )(smooth_gain, transition)

    by_core = [packed, swap_core(packed)]
    chip = call(pair_kernel, shape(PACK, W), 1, 2)(where, *by_core)
    ordered = [pltpu.VMEM((4, PACK, W), F32)]
    by_x = [chip] + three(chip, "x")
    row = call(functools.partial(four_kernel, 2), shape(PACK, W), 1, 4, ordered)(where, *by_x)
    by_z = [row] + three(row, "z")
    plane = call(functools.partial(four_kernel, 1), shape(PACK, W), 1, 4, ordered)(where, *by_z)
    by_y = [plane] + three(plane, "y")

    drives, final, shift = call(
        filter_kernel, [shape(ROWS, W), shape(8, W), shape(8, W)], 1, 14 + 8,
        [pltpu.VMEM((16, PACK, W), F32)],
    )(
        where, *by_y, *by_z, *by_x, *by_core, initial_state.reshape(1, W), inputs, ends, powers, tree,
        gain_powers, drive_map, transition,
    )
    gathered = shift[:1]
    gathered = jnp.concatenate([gathered, swap_core(gathered)], axis=0)
    for axis in ("x", "z", "y"):
        gathered = jnp.concatenate([gathered] + three(gathered, axis), axis=0)
    smoothed, incoming = call(smooth_kernel, [shape(ROWS, W), shape(8, W)], 1, 4)(
        where, gathered, drives, final, gain_powers
    )
    both = jnp.concatenate([smoothed, incoming], axis=0)
    other_both = swap_core(both)
    smoothed_out, stats = call(
        stats_kernel, [shape(2 * ROWS, W), shape(8 * W, W)], 1, 4, [pltpu.VMEM((2 * ROWS, W), F32)]
    )(where, telemetry, flags, both, other_both)

    part = scatter_sum(stats, "x", at_x)
    part = scatter_sum(part, "z", at_z)
    got = three(part, "y")
    part = (part + got[0]) + (got[1] + got[2])
    got = [part] + three(part, "z")
    stacked = jnp.stack(got)
    order = jnp.arange(4) ^ at_z
    part = jnp.concatenate([lax.dynamic_index_in_dim(stacked, at_z ^ j, 0, keepdims=False) for j in range(4)], axis=0)
    got = [part] + three(part, "x")
    ridge = RIDGE * telemetry.shape[0] * lax.axis_size("tm")
    new_transition, new_sensing = call(
        functools.partial(solve_kernel, ridge), [shape(W, W), shape(2 * W, W)], 1, 4,
        [pltpu.VMEM((4, 2 * W, W), F32), pltpu.VMEM((5, W, W), F32), pltpu.VMEM((5, W, W), F32)],
    )(where, *got)
    return new_transition, new_sensing, smoothed_out


def solution(mesh):
    placed = (P("tm", "sens"), P("tm", "sens"), P(), P("sens", None), P(None, "sens"), P(), P())
    return jax.shard_map(
        on_device,
        mesh=mesh,
        in_specs=placed,
        out_specs=(P(), P("sens", None), P("tm", None)),
        check_vma=False,
    )
```

time: 1210 us -> 228 us (0.19); the launches traced: 1190 us -> 228 us
  matrix products: 397 us -> 0 us
  blocking collectives: 350 us -> 0 us
  other arithmetic: 172 us -> 2.25 us
  local copies, waits for them, and re-layouts: 127 us -> 14.2 us
  Pallas kernels: 0 us -> 109 us
  waiting for transfers between devices: 122 us -> 47.3 us
  starting transfers between devices: 0.57 us -> 54.5 us
  between operations: 17.8 us -> 0.84 us
    dot_general x312 -> x0, matrix products: 394 us -> none  [the longest x144 156 us: combine_maps(): jnp.einsum('...ab,...b->...a', latter[0], earlier[1], precision=HIGHEST)]
    all_gather x4 -> x0, blocking collectives: 350 us -> none  [the longest x2 346 us: entering(): pieces = jax.tree.map(lambda part: lax.all_gather(part, axis), value)]
    psum x2 -> x0, waiting for transfers between devices: 122 us -> none  [the longest x1 122 us: on_device(): grams, cross = lax.psum((grams, cross), 'tm')]
    another operation x13 -> x2, other arithmetic: 110 us -> 0.68 us  [the longest x1 0.67 us: on_device(): where = jnp.stack([at_y, at_z, at_x, core]).astype(jnp.int32)]
    pallas_call x0 -> x11, Pallas kernels: none -> 109 us  [the longest x1 64.5 us: on_device(): call(functools.partial(solve_kernel, ridge), [shape(W, W), shape(2 * W, W...]
    pad x32 -> x0, local copies, waits for them, and re-layouts: 88.7 us -> none  [local_chain(): return lax.associative_scan(combine_maps, (powered, block_ends), axis=0)]
    ppermute x0 -> x40, starting transfers between devices: none -> 54.5 us  [the longest x33 53.1 us: swap(): return lax.ppermute(value, 'tm', pairs)]
    ppermute x0 -> x40, waiting for transfers between devices: none -> 47.3 us  [the longest x33 42.6 us: swap(): return lax.ppermute(value, 'tm', pairs)]
  transfers between devices with their start and end apart: 4 -> 40, of which waited for: 1 -> 28; matrix products, arithmetic and copies ran while one was open for 41% -> 1% of each run, Pallas kernels for 0% -> 7%
where the time goes in v1:
time: 228 us
  Pallas kernels  109 us (48%)
  starting transfers between devices  54.5 us (24%)
  waiting for transfers between devices  47.3 us (21%)
  local copies, waits for them, and re-layouts  14.2 us (6%)
    pallas_call x1, Pallas kernels, on_device(): call(functools.partial(solve_kernel, ridge), [shape(W, W), shape(2 * W, W...  64.5 us
    ppermute x33, starting transfers between devices, swap(): return lax.ppermute(value, 'tm', pairs)  53.1 us
    ppermute x33, waiting for transfers between devices, swap(): return lax.ppermute(value, 'tm', pairs)  42.6 us
    pallas_call x1, Pallas kernels, on_device(): call(maps_kernel, [shape(SEGS, 5, W, 2 * W, dtype=BF16), shape(SEGS - 1,...  9.45 us
    pallas_call x1, Pallas kernels, on_device(): call(filter_kernel, [shape(ROWS, W), shape(8, W), shape(8, W)], 1, 14 + 8...  8.43 us
    unnamed x42, local copies, waits for them, and re-layouts  7.47 us
    pallas_call x1, Pallas kernels, on_device(): call(shift_kernel, [shape(ROWS, W), shape(32, W), shape(PACK, W)], 0, 5)  5.84 us
    pallas_call x1, Pallas kernels, on_device(): call(smooth_kernel, [shape(ROWS, W), shape(8, W)], 1, 4)  4.75 us
  transfers between devices with their start and end apart: 40, of which 28 were waited for; matrix products, arithmetic and copies ran while one was open for 1% of the time, Pallas kernels for 7%

profile of v1, /device:TPU:0, one launch (start us, length us, event | category | flops | bytes accessed | tf_op | source)
XLA Modules:
  0.0 227.8 jit_solution(7874279377901588781)
XLA Ops:
  1.2 0.8 copy.10
  3.2 2.3 %shard_map.94 = (f32[256,128]{1,0:T(8,128)}, f32[256,128]{1,0:T(8,128)}) custom-call(s32[4]{0:T(128)} %pad_add_fusion.where, f32[512,256]{1,0:T(8,128)} %tel.3, f32[32,4]{1,0:T(8,128)} %convert_element_type.3.flags.flags_own, f32[128,256]{1,0:T(8,128)} %gain_own.1), custom_call_target="tpu_custom_call" | custom-call | tf_op jit(solution)/shard_map/pallas_call | solution.py:430
  6.1 1.1 collective-permute-done.1.flags_other
  8.5 9.5 %shard_map.95 = (bf16[16,5,128,256]{3,2,1,0:T(8,128)(2,1)}, bf16[15,128,256]{2,1,0:T(8,128)(2,1)}, f32[31,128,128]{2,1,0:T(8,128)}) custom-call(s32[4]{0:T(128)} %pad_add_fusion.where, f32[32,4]{1,0:T(8,128)} %convert_element_type.3.flags.flags_own, f32[32,4]{1,0:T(8,128)} %copy-done.19, f32[128,128]{1,0:T(8,128)} %trans.5, f32[128,256]{1,0:T(8,128)} %gain_own.1, ...), custom_call_target="tpu_custom_call" | custom-call | tf_op jit(solution)/shard_map/pallas_call | solution.py:432
  18.6 5.8 %shard_map.96 = (f32[256,128]{1,0:T(8,128)}, f32[32,128]{1,0:T(8,128)}, f32[136,128]{1,0:T(8,128)}) custom-call(f32[256,128]{1,0:T(8,128)} %get-tuple-element.22.mine, f32[256,128]{1,0:T(8,128)} %copy-done.10, bf16[16,5,128,256]{3,2,1,0:T(8,128)(2,1)} %get-tuple-element.24.powers, bf16[15,128,256]{2,1,0:T(8,128)(2,1)} %get-tuple-element.25.tree, ...), custom_call_target="tpu_custom_call" | custom-call | tf_op jit(solution)/shard_map/pallas_call | solution.py:438
  24.7 1.1 collective-permute-done.4.other.c1
  26.5 1.7 shard_map.97.own.x0
  28.3 1.6 collective-permute-start.5
  29.8 2.7 %collective-permute-start.6 = (f32[136,128]{1,0:T(8,128)}, f32[136,128]{1,0:T(8,128)S(1)}, u32[]{:S(2)}, u32[]{:S(2)}) collective-permute-start(f32[136,128]{1,0:T(8,128)} %shard_map.97.own.x0), channel_id=1, source_target_pairs={{0,4},{2,6},{4,0},{6,2},{8,12},{10,14},{12,8},{14,10},{16,20},{18,... | collective-permute-start | bytes 208904 | tf_op jit(solution)/shard_map/ppermute | solution.py:398
  33.0 3.7 %collective-permute-done.6.r2.x2 = f32[136,128]{1,0:T(8,128)S(1)} collective-permute-done((f32[136,128]{1,0:T(8,128)}, f32[136,128]{1,0:T(8,128)S(1)}, u32[]{:S(2)}, u32[]{:S(2)}) %collective-permute-start.6) | collective-permute-done | bytes 69664 | tf_op jit(solution)/shard_map/ppermute | solution.py:398
  36.7 1.6 collective-permute-done.7.r3.x3
  38.9 2.0 shard_map.98.own.z0
  41.0 4.0 %collective-permute-start.10 = (f32[136,128]{1,0:T(8,128)}, f32[136,128]{1,0:T(8,128)S(1)}, u32[]{:S(2)}, u32[]{:S(2)}) collective-permute-start(f32[136,128]{1,0:T(8,128)} %shard_map.98.own.z0), channel_id=1, source_target_pairs={{0,24},{2,26},{4,28},{6,30},{8,16},{10,18},{12,20},{14,22},{16,8},... | collective-permute-start | bytes 208904 | tf_op jit(solution)/shard_map/ppermute | solution.py:398
  45.0 1.5 collective-permute-start.9
  46.5 1.3 collective-permute-done.10.r3.z3
  47.8 1.7 collective-permute-done.8.r1.z1
  49.5 1.5 collective-permute-done.9.r2.z2
  51.7 2.0 shard_map.99.y0
  53.7 1.6 collective-permute-start.11
  55.3 2.9 %collective-permute-start.12 = (f32[136,128]{1,0:T(8,128)}, f32[136,128]{1,0:T(8,128)S(1)}, u32[]{:S(2)}, u32[]{:S(2)}) collective-permute-start(f32[136,128]{1,0:T(8,128)} %shard_map.99.y0), channel_id=1, source_target_pairs={{0,64},{2,66},{4,68},{6,70},{8,72},{10,74},{12,76},{14,78},{16,80}... | collective-permute-start | bytes 208904 | tf_op jit(solution)/shard_map/ppermute | solution.py:398
  58.4 4.4 %shard_map.100 = (bf16[15,128,256]{2,1,0:T(8,128)(2,1)}, bf16[128,256]{1,0:T(8,128)(2,1)}) custom-call(f32[128,128]{1,0:T(8,128)} %smooth_gain.1, f32[128,128]{1,0:T(8,128)} %trans.5), custom_call_target="tpu_custom_call" | custom-call | tf_op jit(solution)/shard_map/pallas_call | solution.py:442
  62.8 1.1 collective-permute-done.13.y3
  64.6 8.4 %shard_map.101 = (f32[256,128]{1,0:T(8,128)}, f32[8,128]{1,0:T(8,128)}, f32[8,128]{1,0:T(8,128)}) custom-call(s32[4]{0:T(128)} %pad_add_fusion.where, f32[136,128]{1,0:T(8,128)} %shard_map.99.y0, f32[136,128]{1,0:T(8,128)} %copy-done.16, f32[136,128]{1,0:T(8,128)} %copy-done.17, f32[136,128]{1,0:T(8,128)} %copy-done.18, f32[136,128]{1,0:T(8,128)} %shard_map.98.own.z0, ...), custom_call_target="tpu_custom_call" | custom-call | tf_op jit(solution)/shard_map/pallas_call | solution.py:455
  73.7 1.1 collective-permute-done.14
  74.8 2.4 %collective-permute-start.16 = (f32[2,128]{1,0:T(2,128)S(1)}, f32[2,128]{1,0:T(2,128)S(1)}, u32[]{:S(2)}, u32[]{:S(2)}) collective-permute-start(f32[2,128]{1,0:T(2,128)S(1)} %pad_maximum_fusion.2), channel_id=1, source_target_pairs={{0,4},{2,6},{4,0},{6,2},{8,12},{10,14},{12,8},{14,10},{16,20},{18,... | collective-permute-start | bytes 3080 | tf_op jit(solution)/shard_map/ppermute | solution.py:398
  77.2 2.3 collective-permute-start.17
  80.0 2.0 collective-permute-done.17
  82.0 2.1 collective-permute-start.18
  84.1 1.5 collective-permute-start.19
  85.6 1.3 collective-permute-start.20
  86.9 2.3 %collective-permute-done.19 = f32[8,128]{1,0:T(8,128)S(1)} collective-permute-done((f32[8,128]{1,0:T(8,128)S(1)}, f32[8,128]{1,0:T(8,128)S(1)}, u32[]{:S(2)}, u32[]{:S(2)}) %collective-permute-start.19) | collective-permute-done | bytes 4128 | tf_op jit(solution)/shard_map/ppermute | solution.py:398
  89.2 1.2 collective-permute-done.20
  90.6 3.4 %collective-permute-start.22 = (f32[32,128]{1,0:T(8,128)S(1)}, f32[32,128]{1,0:T(8,128)S(1)}, u32[]{:S(2)}, u32[]{:S(2)}) collective-permute-start(f32[32,128]{1,0:T(8,128)S(1)} %concatenate.23), channel_id=1, source_target_pairs={{0,64},{2,66},{4,68},{6,70},{8,72},{10,74},{12,76},{14,78},{16,80}... | collective-permute-start | bytes 49160 | tf_op jit(solution)/shard_map/ppermute | solution.py:398
  93.9 1.3 collective-permute-start.23
  95.9 3.0 %collective-permute-done.23 = f32[32,128]{1,0:T(8,128)S(1)} collective-permute-done((f32[32,128]{1,0:T(8,128)S(1)}, f32[32,128]{1,0:T(8,128)S(1)}, u32[]{:S(2)}, u32[]{:S(2)}) %collective-permute-start.23) | collective-permute-done | bytes 16416 | tf_op jit(solution)/shard_map/ppermute | solution.py:398
  98.9 4.2 %concatenate.24.gathered = f32[128,128]{1,0:T(8,128)} concatenate(f32[1,128]{1,0:T(1,128)S(1)} %slice.3, f32[1,128]{1,0:T(1,128)S(1)} %collective-permute-done.14, f32[2,128]{1,0:T(2,128)S(1)} %collective-permute-done.15, f32[2,128]{1,0:T(2,128)S(1)} %collective-permute-done.16, f32[2,128]{1,0:T(2,128)S(1)} %collective-permute-done.17, f32[8,128]{1,0:T(8,128)S(1)} %collective-permute-done.18, ...), dimensions={0} | concatenate | bytes 131072 | tf_op jit(solution)/shard_map/concatenate | solution.py:465
  103.1 4.7 %shard_map.102 = (f32[256,128]{1,0:T(8,128)}, f32[8,128]{1,0:T(8,128)}) custom-call(s32[4]{0:T(128)} %pad_add_fusion.where, f32[128,128]{1,0:T(8,128)} %concatenate.24.gathered, f32[256,128]{1,0:T(8,128)} %get-tuple-element.33.drives, f32[8,128]{1,0:T(8,128)} %get-tuple-element.34.final, bf16[15,128,256]{2,1,0:T(8,128)(2,1)} %get-tuple-element.30.gain_powers), custom_call_target="tpu_custom_call" | custom-call | tf_op jit(solution)/shard_map/pallas_call | solution.py:466
  107.8 0.9 constant_dynamic-update-slice_fusion.1
  109.4 1.4 collective-permute-done.24.other
  111.4 3.4 %shard_map.103 = (f32[512,128]{1,0:T(8,128)}, f32[1024,128]{1,0:T(8,128)}) custom-call(s32[4]{0:T(128)} %pad_add_fusion.where, f32[512,256]{1,0:T(8,128)} %tel.3, f32[32,4]{1,0:T(8,128)} %convert_element_type.3.flags.flags_own, f32[264,128]{1,0:T(8,128)} %copy-done, f32[264,128]{1,0:T(8,128)} %copy-done.9), custom_call_target="tpu_custom_call" | custom-call | tf_op jit(solution)/shard_map/pallas_call | solution.py:471
  114.8 1.1 constant_dynamic-slice_fusion.5
  116.0 3.6 %collective-permute-start.26 = (f32[256,128]{1,0:T(8,128)S(1)}, f32[256,128]{1,0:T(8,128)S(1)}, u32[]{:S(2)}, u32[]{:S(2)}) collective-permute-start(f32[256,128]{1,0:T(8,128)S(1)} %get-tuple-element.43), channel_id=1, source_target_pairs={{0,4},{2,6},{4,0},{6,2},{8,12},{10,14},{12,8},{14,10},{16,20},{18,... | collective-permute-start | bytes 393224 | tf_op jit(solution)/shard_map/ppermute | solution.py:398
  119.6 1.1 collective-permute-start.27
  120.6 1.6 collective-permute-done.25
  122.3 3.7 %collective-permute-done.26 = f32[256,128]{1,0:T(8,128)S(1)} collective-permute-done((f32[256,128]{1,0:T(8,128)S(1)}, f32[256,128]{1,0:T(8,128)S(1)}, u32[]{:S(2)}, u32[]{:S(2)}) %collective-permute-start.26) | collective-permute-done | bytes 131104 | tf_op jit(solution)/shard_map/ppermute | solution.py:398
  126.0 2.2 collective-permute-done.27
  128.3 0.9 add_add_fusion
  129.3 2.8 %collective-permute-start.29 = (f32[64,128]{1,0:T(8,128)S(1)}, f32[64,128]{1,0:T(8,128)S(1)}, u32[]{:S(2)}, u32[]{:S(2)}) collective-permute-start(f32[64,128]{1,0:T(8,128)S(1)} %get-tuple-element.50), channel_id=1, source_target_pairs={{0,16},{2,18},{4,20},{6,22},{8,24},{10,26},{12,28},{14,30},{16,0},... | collective-permute-start | bytes 98312 | tf_op jit(solution)/shard_map/ppermute | solution.py:398
  132.1 1.9 collective-permute-start.30
  134.0 0.8 collective-permute-done.29
  134.8 2.4 %collective-permute-done.30 = f32[64,128]{1,0:T(8,128)S(1)} collective-permute-done((f32[64,128]{1,0:T(8,128)S(1)}, f32[64,128]{1,0:T(8,128)S(1)}, u32[]{:S(2)}, u32[]{:S(2)}) %collective-permute-start.30) | collective-permute-done | bytes 32800 | tf_op jit(solution)/shard_map/ppermute | solution.py:398
  137.3 2.8 %collective-permute-start.32 = (f32[64,128]{1,0:T(8,128)S(1)}, f32[64,128]{1,0:T(8,128)S(1)}, u32[]{:S(2)}, u32[]{:S(2)}) collective-permute-start(f32[64,128]{1,0:T(8,128)S(1)} %add_add_fusion.2), channel_id=1, source_target_pairs={{0,64},{2,66},{4,68},{6,70},{8,72},{10,74},{12,76},{14,78},{16,80}... | collective-permute-start | bytes 98312 | tf_op jit(solution)/shard_map/ppermute | solution.py:398
  140.1 1.9 collective-permute-start.33
  142.0 0.8 collective-permute-done.32
  142.8 2.4 %collective-permute-done.33 = f32[64,128]{1,0:T(8,128)S(1)} collective-permute-done((f32[64,128]{1,0:T(8,128)S(1)}, f32[64,128]{1,0:T(8,128)S(1)}, u32[]{:S(2)}, u32[]{:S(2)}) %collective-permute-start.33) | collective-permute-done | bytes 32800 | tf_op jit(solution)/shard_map/ppermute | solution.py:398
  145.3 3.3 %collective-permute-start.35 = (f32[64,128]{1,0:T(8,128)S(1)}, f32[64,128]{1,0:T(8,128)S(1)}, u32[]{:S(2)}, u32[]{:S(2)}) collective-permute-start(f32[64,128]{1,0:T(8,128)S(1)} %add_add_fusion.1), channel_id=1, source_target_pairs={{0,16},{2,18},{4,20},{6,22},{8,24},{10,26},{12,28},{14,30},{16,0},... | collective-permute-start | bytes 98312 | tf_op jit(solution)/shard_map/ppermute | solution.py:398
  148.7 1.4 collective-permute-start.36
  150.0 0.9 collective-permute-done.35
  150.9 2.9 %collective-permute-done.36 = f32[64,128]{1,0:T(8,128)S(1)} collective-permute-done((f32[64,128]{1,0:T(8,128)S(1)}, f32[64,128]{1,0:T(8,128)S(1)}, u32[]{:S(2)}, u32[]{:S(2)}) %collective-permute-start.36) | collective-permute-done | bytes 32800 | tf_op jit(solution)/shard_map/ppermute | solution.py:398
  154.0 2.5 %collective-permute-start.38 = (f32[256,128]{1,0:T(8,128)S(1)}, f32[256,128]{1,0:T(8,128)S(1)}, u32[]{:S(2)}, u32[]{:S(2)}) collective-permute-start(f32[256,128]{1,0:T(8,128)S(1)} %pad_maximum_fusion.1.own), channel_id=1, source_target_pairs={{0,4},{2,6},{4,0},{6,2},{8,12},{10,14},{12,8},{14,10},{16,20},{18,... | collective-permute-start | bytes 393224 | tf_op jit(solution)/shard_map/ppermute | solution.py:398
  156.5 2.2 collective-permute-start.39
  158.9 1.9 collective-permute-done.38.r2
  160.8 1.8 collective-permute-done.39.r3
  163.3 64.5 %shard_map.104 = (f32[128,128]{1,0:T(8,128)}, f32[256,128]{1,0:T(8,128)}) custom-call(s32[4]{0:T(128)} %pad_add_fusion.where, f32[256,128]{1,0:T(8,128)} %copy-done.1, f32[256,128]{1,0:T(8,128)} %copy-done.11, f32[256,128]{1,0:T(8,128)} %copy-done.12, f32[256,128]{1,0:T(8,128)} %copy-done.13), custom_call_target="tpu_custom_call" | custom-call | tf_op jit(solution)/shard_map/pallas_call | solution.py:485
  (85 shorter events, 12.5 us)
Async XLA Ops:
  0.6 6.5 %collective-permute-start.2 = (f32[128,256]{1,0:T(8,128)}, f32[128,256]{1,0:T(8,128)S(1)}, u32[]{:S(2)}, u32[]{:S(2)}) collective-permute-start(f32[128,256]{1,0:T(8,128)} %gain_own.1), channel_id=1, source_target_pairs={{0,1},{1,0},{2,3},{3,2},{4,5},{5,4},{6,7},{7,6},{8,9},{9,8},{10,11... | collective-permute-start | bytes 393224 | tf_op jit(solution)/shard_map/ppermute | solution.py:402
  0.7 6.4 %collective-permute-start.3 = (f32[256,128]{1,0:T(8,128)}, f32[256,128]{1,0:T(8,128)S(1)}, u32[]{:S(2)}, u32[]{:S(2)}) collective-permute-start(f32[256,128]{1,0:T(8,128)} %sense_own.1), channel_id=1, source_target_pairs={{0,1},{1,0},{2,3},{3,2},{4,5},{5,4},{6,7},{7,6},{8,9},{9,8},{10,11... | collective-permute-start | bytes 393224 | tf_op jit(solution)/shard_map/ppermute | solution.py:402
  5.6 12.4 %collective-permute-start = (f32[256,128]{1,0:T(8,128)}, f32[256,128]{1,0:T(8,128)S(1)}, u32[]{:S(2)}, u32[]{:S(2)}) collective-permute-start(f32[256,128]{1,0:T(8,128)} %get-tuple-element.23), channel_id=1, source_target_pairs={{0,1},{1,0},{2,3},{3,2},{4,5},{5,4},{6,7},{7,6},{8,9},{9,8},{10,11... | collective-permute-start | bytes 393224 | tf_op jit(solution)/shard_map/ppermute | solution.py:402
  5.7 1.5 collective-permute-start.1
  7.2 0.6 copy-start.19
  7.2 0.7 copy-start.14
  7.8 0.7 copy-start.15
  17.9 0.7 copy-start.10
  24.4 1.5 collective-permute-start.4
  25.9 0.6 copy-start.2
  28.3 4.7 %collective-permute-start.5 = (f32[136,128]{1,0:T(8,128)}, f32[136,128]{1,0:T(8,128)S(1)}, u32[]{:S(2)}, u32[]{:S(2)}) collective-permute-start(f32[136,128]{1,0:T(8,128)} %shard_map.97.own.x0), channel_id=1, source_target_pairs={{0,2},{2,0},{4,6},{6,4},{8,10},{10,8},{12,14},{14,12},{16,18},{18,... | collective-permute-start | bytes 208904 | tf_op jit(solution)/shard_map/ppermute | solution.py:398
  29.8 6.8 %collective-permute-start.6 = (f32[136,128]{1,0:T(8,128)}, f32[136,128]{1,0:T(8,128)S(1)}, u32[]{:S(2)}, u32[]{:S(2)}) collective-permute-start(f32[136,128]{1,0:T(8,128)} %shard_map.97.own.x0), channel_id=1, source_target_pairs={{0,4},{2,6},{4,0},{6,2},{8,12},{10,14},{12,8},{14,10},{16,20},{18,... | collective-permute-start | bytes 208904 | tf_op jit(solution)/shard_map/ppermute | solution.py:398
  32.6 5.7 %collective-permute-start.7 = (f32[136,128]{1,0:T(8,128)}, f32[136,128]{1,0:T(8,128)S(1)}, u32[]{:S(2)}, u32[]{:S(2)}) collective-permute-start(f32[136,128]{1,0:T(8,128)} %shard_map.97.own.x0), channel_id=1, source_target_pairs={{0,6},{2,4},{4,2},{6,0},{8,14},{10,12},{12,10},{14,8},{16,22},{18,... | collective-permute-start | bytes 208904 | tf_op jit(solution)/shard_map/ppermute | solution.py:398
  33.0 5.3 %copy-start.3 = (f32[136,128]{1,0:T(8,128)}, f32[136,128]{1,0:T(8,128)S(1)}, u32[]{:S(2)}) copy-start(f32[136,128]{1,0:T(8,128)S(1)} %collective-permute-done.5.r1.x1) | copy-start | bytes 208900
  36.7 1.6 copy-start.4
  38.3 0.6 copy-start.5
  41.0 6.8 %collective-permute-start.10 = (f32[136,128]{1,0:T(8,128)}, f32[136,128]{1,0:T(8,128)S(1)}, u32[]{:S(2)}, u32[]{:S(2)}) collective-permute-start(f32[136,128]{1,0:T(8,128)} %shard_map.98.own.z0), channel_id=1, source_target_pairs={{0,24},{2,26},{4,28},{6,30},{8,16},{10,18},{12,20},{14,22},{16,8},... | collective-permute-start | bytes 208904 | tf_op jit(solution)/shard_map/ppermute | solution.py:398
  45.0 4.5 %collective-permute-start.8 = (f32[136,128]{1,0:T(8,128)}, f32[136,128]{1,0:T(8,128)S(1)}, u32[]{:S(2)}, u32[]{:S(2)}) collective-permute-start(f32[136,128]{1,0:T(8,128)} %shard_map.98.own.z0), channel_id=1, source_target_pairs={{0,8},{2,10},{4,12},{6,14},{8,0},{10,2},{12,4},{14,6},{16,24},{18,... | collective-permute-start | bytes 208904 | tf_op jit(solution)/shard_map/ppermute | solution.py:398
  45.0 6.0 %collective-permute-start.9 = (f32[136,128]{1,0:T(8,128)}, f32[136,128]{1,0:T(8,128)S(1)}, u32[]{:S(2)}, u32[]{:S(2)}) collective-permute-start(f32[136,128]{1,0:T(8,128)} %shard_map.98.own.z0), channel_id=1, source_target_pairs={{0,16},{2,18},{4,20},{6,22},{8,24},{10,26},{12,28},{14,30},{16,0},... | collective-permute-start | bytes 208904 | tf_op jit(solution)/shard_map/ppermute | solution.py:398
  47.8 3.2 %copy-start.6 = (f32[136,128]{1,0:T(8,128)}, f32[136,128]{1,0:T(8,128)S(1)}, u32[]{:S(2)}) copy-start(f32[136,128]{1,0:T(8,128)S(1)} %collective-permute-done.10.r3.z3) | copy-start | bytes 208900
  49.5 1.5 copy-start.7
  51.1 0.6 copy-start.8
  53.7 9.1 %collective-permute-start.11 = (f32[136,128]{1,0:T(8,128)}, f32[136,128]{1,0:T(8,128)S(1)}, u32[]{:S(2)}, u32[]{:S(2)}) collective-permute-start(f32[136,128]{1,0:T(8,128)} %shard_map.99.y0), channel_id=1, source_target_pairs={{0,32},{2,34},{4,36},{6,38},{8,40},{10,42},{12,44},{14,46},{16,48}... | collective-permute-start | bytes 208904 | tf_op jit(solution)/shard_map/ppermute | solution.py:398
  55.3 7.5 %collective-permute-start.12 = (f32[136,128]{1,0:T(8,128)}, f32[136,128]{1,0:T(8,128)S(1)}, u32[]{:S(2)}, u32[]{:S(2)}) collective-permute-start(f32[136,128]{1,0:T(8,128)} %shard_map.99.y0), channel_id=1, source_target_pairs={{0,64},{2,66},{4,68},{6,70},{8,72},{10,74},{12,76},{14,78},{16,80}... | collective-permute-start | bytes 208904 | tf_op jit(solution)/shard_map/ppermute | solution.py:398
  58.2 5.7 %collective-permute-start.13 = (f32[136,128]{1,0:T(8,128)}, f32[136,128]{1,0:T(8,128)S(1)}, u32[]{:S(2)}, u32[]{:S(2)}) collective-permute-start(f32[136,128]{1,0:T(8,128)} %shard_map.99.y0), channel_id=1, source_target_pairs={{0,96},{2,98},{4,100},{6,102},{8,104},{10,106},{12,108},{14,110},{... | collective-permute-start | bytes 208904 | tf_op jit(solution)/shard_map/ppermute | solution.py:398
  62.8 1.2 copy-start.16
  62.8 1.2 copy-start.17
  63.9 0.6 copy-start.18
  73.7 1.1 collective-permute-start.14
  74.8 4.7 %collective-permute-start.15 = (f32[2,128]{1,0:T(2,128)S(1)}, f32[2,128]{1,0:T(2,128)S(1)}, u32[]{:S(2)}, u32[]{:S(2)}) collective-permute-start(f32[2,128]{1,0:T(2,128)S(1)} %pad_maximum_fusion.2), channel_id=1, source_target_pairs={{0,2},{2,0},{4,6},{6,4},{8,10},{10,8},{12,14},{14,12},{16,18},{18,... | collective-permute-start | bytes 3080 | tf_op jit(solution)/shard_map/ppermute | solution.py:398
  74.8 5.2 %collective-permute-start.16 = (f32[2,128]{1,0:T(2,128)S(1)}, f32[2,128]{1,0:T(2,128)S(1)}, u32[]{:S(2)}, u32[]{:S(2)}) collective-permute-start(f32[2,128]{1,0:T(2,128)S(1)} %pad_maximum_fusion.2), channel_id=1, source_target_pairs={{0,4},{2,6},{4,0},{6,2},{8,12},{10,14},{12,8},{14,10},{16,20},{18,... | collective-permute-start | bytes 3080 | tf_op jit(solution)/shard_map/ppermute | solution.py:398
  77.2 4.8 %collective-permute-start.17 = (f32[2,128]{1,0:T(2,128)S(1)}, f32[2,128]{1,0:T(2,128)S(1)}, u32[]{:S(2)}, u32[]{:S(2)}) collective-permute-start(f32[2,128]{1,0:T(2,128)S(1)} %pad_maximum_fusion.2), channel_id=1, source_target_pairs={{0,6},{2,4},{4,2},{6,0},{8,14},{10,12},{12,10},{14,8},{16,22},{18,... | collective-permute-start | bytes 3080 | tf_op jit(solution)/shard_map/ppermute | solution.py:398
  82.0 4.9 %collective-permute-start.18 = (f32[8,128]{1,0:T(8,128)S(1)}, f32[8,128]{1,0:T(8,128)S(1)}, u32[]{:S(2)}, u32[]{:S(2)}) collective-permute-start(f32[8,128]{1,0:T(8,128)S(1)} %concatenate.22), channel_id=1, source_target_pairs={{0,8},{2,10},{4,12},{6,14},{8,0},{10,2},{12,4},{14,6},{16,24},{18,... | collective-permute-start | bytes 12296 | tf_op jit(solution)/shard_map/ppermute | solution.py:398
  84.1 5.1 %collective-permute-start.19 = (f32[8,128]{1,0:T(8,128)S(1)}, f32[8,128]{1,0:T(8,128)S(1)}, u32[]{:S(2)}, u32[]{:S(2)}) collective-permute-start(f32[8,128]{1,0:T(8,128)S(1)} %concatenate.22), channel_id=1, source_target_pairs={{0,16},{2,18},{4,20},{6,22},{8,24},{10,26},{12,28},{14,30},{16,0},... | collective-permute-start | bytes 12296 | tf_op jit(solution)/shard_map/ppermute | solution.py:398
  85.6 4.8 %collective-permute-start.20 = (f32[8,128]{1,0:T(8,128)S(1)}, f32[8,128]{1,0:T(8,128)S(1)}, u32[]{:S(2)}, u32[]{:S(2)}) collective-permute-start(f32[8,128]{1,0:T(8,128)S(1)} %concatenate.22), channel_id=1, source_target_pairs={{0,24},{2,26},{4,28},{6,30},{8,16},{10,18},{12,20},{14,22},{16,8},... | collective-permute-start | bytes 12296 | tf_op jit(solution)/shard_map/ppermute | solution.py:398
  90.5 4.8 %collective-permute-start.21 = (f32[32,128]{1,0:T(8,128)S(1)}, f32[32,128]{1,0:T(8,128)S(1)}, u32[]{:S(2)}, u32[]{:S(2)}) collective-permute-start(f32[32,128]{1,0:T(8,128)S(1)} %concatenate.23), channel_id=1, source_target_pairs={{0,32},{2,34},{4,36},{6,38},{8,40},{10,42},{12,44},{14,46},{16,48}... | collective-permute-start | bytes 49160 | tf_op jit(solution)/shard_map/ppermute | solution.py:398
  90.6 5.3 %collective-permute-start.22 = (f32[32,128]{1,0:T(8,128)S(1)}, f32[32,128]{1,0:T(8,128)S(1)}, u32[]{:S(2)}, u32[]{:S(2)}) collective-permute-start(f32[32,128]{1,0:T(8,128)S(1)} %concatenate.23), channel_id=1, source_target_pairs={{0,64},{2,66},{4,68},{6,70},{8,72},{10,74},{12,76},{14,78},{16,80}... | collective-permute-start | bytes 49160 | tf_op jit(solution)/shard_map/ppermute | solution.py:398
  93.9 4.9 %collective-permute-start.23 = (f32[32,128]{1,0:T(8,128)S(1)}, f32[32,128]{1,0:T(8,128)S(1)}, u32[]{:S(2)}, u32[]{:S(2)}) collective-permute-start(f32[32,128]{1,0:T(8,128)S(1)} %concatenate.23), channel_id=1, source_target_pairs={{0,96},{2,98},{4,100},{6,102},{8,104},{10,106},{12,108},{14,110},{... | collective-permute-start | bytes 49160 | tf_op jit(solution)/shard_map/ppermute | solution.py:398
  109.4 1.4 copy-start
  109.4 1.4 collective-permute-start.24
  110.8 0.7 copy-start.9
  115.9 6.4 %collective-permute-start.25 = (f32[256,128]{1,0:T(8,128)S(1)}, f32[256,128]{1,0:T(8,128)S(1)}, u32[]{:S(2)}, u32[]{:S(2)}) collective-permute-start(f32[256,128]{1,0:T(8,128)S(1)} %get-tuple-element.41), channel_id=1, source_target_pairs={{0,2},{2,0},{4,6},{6,4},{8,10},{10,8},{12,14},{14,12},{16,18},{18,... | collective-permute-start | bytes 393224 | tf_op jit(solution)/shard_map/ppermute | solution.py:398
  116.0 10.1 %collective-permute-start.26 = (f32[256,128]{1,0:T(8,128)S(1)}, f32[256,128]{1,0:T(8,128)S(1)}, u32[]{:S(2)}, u32[]{:S(2)}) collective-permute-start(f32[256,128]{1,0:T(8,128)S(1)} %get-tuple-element.43), channel_id=1, source_target_pairs={{0,4},{2,6},{4,0},{6,2},{8,12},{10,14},{12,8},{14,10},{16,20},{18,... | collective-permute-start | bytes 393224 | tf_op jit(solution)/shard_map/ppermute | solution.py:398
  119.6 8.7 %collective-permute-start.27 = (f32[256,128]{1,0:T(8,128)S(1)}, f32[256,128]{1,0:T(8,128)S(1)}, u32[]{:S(2)}, u32[]{:S(2)}) collective-permute-start(f32[256,128]{1,0:T(8,128)S(1)} %get-tuple-element.42), channel_id=1, source_target_pairs={{0,6},{2,4},{4,2},{6,0},{8,14},{10,12},{12,10},{14,8},{16,22},{18,... | collective-permute-start | bytes 393224 | tf_op jit(solution)/shard_map/ppermute | solution.py:398
  129.2 4.8 %collective-permute-start.28 = (f32[64,128]{1,0:T(8,128)S(1)}, f32[64,128]{1,0:T(8,128)S(1)}, u32[]{:S(2)}, u32[]{:S(2)}) collective-permute-start(f32[64,128]{1,0:T(8,128)S(1)} %get-tuple-element.48), channel_id=1, source_target_pairs={{0,8},{2,10},{4,12},{6,14},{8,0},{10,2},{12,4},{14,6},{16,24},{18,... | collective-permute-start | bytes 98312 | tf_op jit(solution)/shard_map/ppermute | solution.py:398
  129.3 5.5 %collective-permute-start.29 = (f32[64,128]{1,0:T(8,128)S(1)}, f32[64,128]{1,0:T(8,128)S(1)}, u32[]{:S(2)}, u32[]{:S(2)}) collective-permute-start(f32[64,128]{1,0:T(8,128)S(1)} %get-tuple-element.50), channel_id=1, source_target_pairs={{0,16},{2,18},{4,20},{6,22},{8,24},{10,26},{12,28},{14,30},{16,0},... | collective-permute-start | bytes 98312 | tf_op jit(solution)/shard_map/ppermute | solution.py:398
  132.1 5.1 %collective-permute-start.30 = (f32[64,128]{1,0:T(8,128)S(1)}, f32[64,128]{1,0:T(8,128)S(1)}, u32[]{:S(2)}, u32[]{:S(2)}) collective-permute-start(f32[64,128]{1,0:T(8,128)S(1)} %get-tuple-element.49), channel_id=1, source_target_pairs={{0,24},{2,26},{4,28},{6,30},{8,16},{10,18},{12,20},{14,22},{16,8},... | collective-permute-start | bytes 98312 | tf_op jit(solution)/shard_map/ppermute | solution.py:398
  137.3 4.8 %collective-permute-start.31 = (f32[64,128]{1,0:T(8,128)S(1)}, f32[64,128]{1,0:T(8,128)S(1)}, u32[]{:S(2)}, u32[]{:S(2)}) collective-permute-start(f32[64,128]{1,0:T(8,128)S(1)} %add_add_fusion.2), channel_id=1, source_target_pairs={{0,32},{2,34},{4,36},{6,38},{8,40},{10,42},{12,44},{14,46},{16,48}... | collective-permute-start | bytes 98312 | tf_op jit(solution)/shard_map/ppermute | solution.py:398
  137.3 5.5 %collective-permute-start.32 = (f32[64,128]{1,0:T(8,128)S(1)}, f32[64,128]{1,0:T(8,128)S(1)}, u32[]{:S(2)}, u32[]{:S(2)}) collective-permute-start(f32[64,128]{1,0:T(8,128)S(1)} %add_add_fusion.2), channel_id=1, source_target_pairs={{0,64},{2,66},{4,68},{6,70},{8,72},{10,74},{12,76},{14,78},{16,80}... | collective-permute-start | bytes 98312 | tf_op jit(solution)/shard_map/ppermute | solution.py:398
  140.1 5.1 %collective-permute-start.33 = (f32[64,128]{1,0:T(8,128)S(1)}, f32[64,128]{1,0:T(8,128)S(1)}, u32[]{:S(2)}, u32[]{:S(2)}) collective-permute-start(f32[64,128]{1,0:T(8,128)S(1)} %add_add_fusion.2), channel_id=1, source_target_pairs={{0,96},{2,98},{4,100},{6,102},{8,104},{10,106},{12,108},{14,110},{... | collective-permute-start | bytes 98312 | tf_op jit(solution)/shard_map/ppermute | solution.py:398
  145.2 4.8 %collective-permute-start.34 = (f32[64,128]{1,0:T(8,128)S(1)}, f32[64,128]{1,0:T(8,128)S(1)}, u32[]{:S(2)}, u32[]{:S(2)}) collective-permute-start(f32[64,128]{1,0:T(8,128)S(1)} %add_add_fusion.1), channel_id=1, source_target_pairs={{0,8},{2,10},{4,12},{6,14},{8,0},{10,2},{12,4},{14,6},{16,24},{18,... | collective-permute-start | bytes 98312 | tf_op jit(solution)/shard_map/ppermute | solution.py:398
  145.3 5.6 %collective-permute-start.35 = (f32[64,128]{1,0:T(8,128)S(1)}, f32[64,128]{1,0:T(8,128)S(1)}, u32[]{:S(2)}, u32[]{:S(2)}) collective-permute-start(f32[64,128]{1,0:T(8,128)S(1)} %add_add_fusion.1), channel_id=1, source_target_pairs={{0,16},{2,18},{4,20},{6,22},{8,24},{10,26},{12,28},{14,30},{16,0},... | collective-permute-start | bytes 98312 | tf_op jit(solution)/shard_map/ppermute | solution.py:398
  148.7 5.1 %collective-permute-start.36 = (f32[64,128]{1,0:T(8,128)S(1)}, f32[64,128]{1,0:T(8,128)S(1)}, u32[]{:S(2)}, u32[]{:S(2)}) collective-permute-start(f32[64,128]{1,0:T(8,128)S(1)} %add_add_fusion.1), channel_id=1, source_target_pairs={{0,24},{2,26},{4,28},{6,30},{8,16},{10,18},{12,20},{14,22},{16,8},... | collective-permute-start | bytes 98312 | tf_op jit(solution)/shard_map/ppermute | solution.py:398
  153.9 8.8 %copy-start.1 = (f32[256,128]{1,0:T(8,128)}, f32[256,128]{1,0:T(8,128)S(1)}, u32[]{:S(2)}) copy-start(f32[256,128]{1,0:T(8,128)S(1)} %pad_maximum_fusion.1.own) | copy-start | bytes 393220
  153.9 5.0 %collective-permute-start.37 = (f32[256,128]{1,0:T(8,128)S(1)}, f32[256,128]{1,0:T(8,128)S(1)}, u32[]{:S(2)}, u32[]{:S(2)}) collective-permute-start(f32[256,128]{1,0:T(8,128)S(1)} %pad_maximum_fusion.1.own), channel_id=1, source_target_pairs={{0,2},{2,0},{4,6},{6,4},{8,10},{10,8},{12,14},{14,12},{16,18},{18,... | collective-permute-start | bytes 393224 | tf_op jit(solution)/shard_map/ppermute | solution.py:398
  154.0 6.9 %collective-permute-start.38 = (f32[256,128]{1,0:T(8,128)S(1)}, f32[256,128]{1,0:T(8,128)S(1)}, u32[]{:S(2)}, u32[]{:S(2)}) collective-permute-start(f32[256,128]{1,0:T(8,128)S(1)} %pad_maximum_fusion.1.own), channel_id=1, source_target_pairs={{0,4},{2,6},{4,0},{6,2},{8,12},{10,14},{12,8},{14,10},{16,20},{18,... | collective-permute-start | bytes 393224 | tf_op jit(solution)/shard_map/ppermute | solution.py:398
  156.5 6.2 %collective-permute-start.39 = (f32[256,128]{1,0:T(8,128)S(1)}, f32[256,128]{1,0:T(8,128)S(1)}, u32[]{:S(2)}, u32[]{:S(2)}) collective-permute-start(f32[256,128]{1,0:T(8,128)S(1)} %pad_maximum_fusion.1.own), channel_id=1, source_target_pairs={{0,6},{2,4},{4,2},{6,0},{8,14},{10,12},{12,10},{14,8},{16,22},{18,... | collective-permute-start | bytes 393224 | tf_op jit(solution)/shard_map/ppermute | solution.py:398
  158.9 3.7 %copy-start.11 = (f32[256,128]{1,0:T(8,128)}, f32[256,128]{1,0:T(8,128)S(1)}, u32[]{:S(2)}) copy-start(f32[256,128]{1,0:T(8,128)S(1)} %collective-permute-done.37.r1) | copy-start | bytes 393220
  160.8 1.8 copy-start.12
  162.7 0.7 copy-start.13

commit v2 on v1

--- a/solution.py
+++ b/solution.py
@@ -15,6 +15,8 @@
 LEN = 16
 ROWS = SEGS * LEN
 PACK = W + 8
+SLAB = W // 4
+CHUNK = W + SLAB + 8
 VMEM_LIMIT = 56 * 1024 * 1024
 
 
@@ -305,7 +307,7 @@
     smoothed[...] = part
 
 
-def stats_kernel(where, tel, flags, own, other, smoothed, stats, full):
+def stats_kernel(where, tel, flags, own, other, smoothed, out0, out1, out2, out3, full, parts):
     core = where[3]
     full[pl.ds(pl.multiple_of(core * ROWS, ROWS), ROWS)] = own[0:ROWS]
     full[pl.ds(pl.multiple_of((1 - core) * ROWS, ROWS), ROWS)] = other[0:ROWS]
@@ -326,8 +328,13 @@
     def fold(out):
         return (out[:W, :W] + out[:W, W:]) + (out[W:, :W] + out[W:, W:])
 
-    stats[0:W] = fold(jnp.dot(kept, packed, preferred_element_type=F32))
-    stats[W : 2 * W] = fold(jnp.dot(kept, wide(following), preferred_element_type=F32))
+    upper = lax.broadcasted_iota(jnp.int32, (W, W), 0) - lax.broadcasted_iota(jnp.int32, (W, W), 1)
+    lag_gram = fold(jnp.dot(kept, packed, preferred_element_type=F32))
+    lag_cross_t = fold(jnp.dot(kept, wide(following), preferred_element_type=F32))
+    lag = jnp.where(jnp.logical_and(upper <= 0, core == 0), lag_gram, lag_cross_t)
+    for j in range(4):
+        parts[j, W : W + SLAB] = lag[j * SLAB : (j + 1) * SLAB]
+        parts[j, W + SLAB :] = jnp.zeros((8, W), F32)
     fl = flags[...]
     repeat = (
         lax.broadcasted_iota(jnp.int32, (2 * SEGS, count), 0)
@@ -336,54 +343,90 @@
     lane_flags = lax.dot_general(
         fl.astype(BF16), repeat.astype(BF16), (((0,), (0,)), ((), ())), preferred_element_type=F32
     )
+    grams = []
     for g in range(4):
         masked_t = packed_t * lane_flags[g : g + 1].astype(BF16)
-        stats[(2 + g) * W : (3 + g) * W] = fold(jnp.dot(masked_t, packed, preferred_element_type=F32))
+        grams.append(fold(jnp.dot(masked_t, packed, preferred_element_type=F32)))
+    for tile in range(2):
+        parts[tile, 0:W] = jnp.where(upper <= 0, grams[2 * tile], grams[2 * tile + 1])
+        parts[0, W + SLAB + tile : W + SLAB + tile + 1] = jnp.sum(
+            jnp.where(upper == 0, grams[2 * tile + 1], 0.0), axis=0, keepdims=True
+        )
     high, low = halves(tel[...] * mask_of(fl, count, 2 * SEGS))
     cross = jnp.dot(packed_t, high, preferred_element_type=F32) + jnp.dot(
         packed_t, low, preferred_element_type=F32
     )
     cross = cross[:W] + cross[W:]
-    stats[6 * W : 7 * W] = cross[:, :W]
-    stats[7 * W : 8 * W] = cross[:, W:]
-
-
-def solve_kernel(ridge, where, own, r1, r2, r3, new_transition, new_sensing, stats, left, right):
+    parts[2, 0:W] = cross[:, :W]
+    parts[3, 0:W] = cross[:, W:]
+    for k, out in enumerate((out0, out1, out2, out3)):
+        out[...] = parts[where[2] ^ k]
+
+
+def inverses(matrices):
+    unit = 8
+    lane = lax.broadcasted_iota(jnp.int32, (W, W), 1)
+    lane_head = lane[:unit]
+    row_head = lax.broadcasted_iota(jnp.int32, (unit, W), 0)
+
+    def block(b, held):
+        heads = [m[:unit] for m in held]
+        rests = [m[unit:] for m in held]
+        for j in range(unit):
+            for p in range(len(held)):
+                head, rest = heads[p], rests[p]
+                row = head[j : j + 1]
+                scale = 1.0 / row[:, j : j + 1]
+                row = jnp.where(lane_head[:1] == j, scale, row * scale)
+                head_next = jnp.where(lane_head == j, 0.0, head) - head[:, j : j + 1] * row
+                heads[p] = jnp.where(row_head == j, row, head_next)
+                rests[p] = jnp.where(lane[unit:] == j, 0.0, rest) - rest[:, j : j + 1] * row
+        return tuple(
+            pltpu.roll(jnp.concatenate([rest, head], axis=0), W - unit, 1)
+            for head, rest in zip(heads, rests)
+        )
+
+    return lax.fori_loop(0, W // unit, block, tuple(matrices))
+
+
+def exact(left, right):
+    return jnp.dot(left, right, precision=lax.Precision.HIGHEST, preferred_element_type=F32)
+
+
+def solve_kernel(ridge, where, own, r1, r2, r3, new_transition, new_sensing, parts):
     at = where[2]
+    core = where[3]
     for k, ref in enumerate((own, r1, r2, r3)):
-        stats[at ^ k] = ref[...]
-    eye = identity() * ridge
-    left[0] = stats[0, 0:W] + eye
-    right[0] = stats[0, W : 2 * W]
-    for g in range(4):
-        left[1 + g] = stats[1 + g // 2, (g % 2) * W : (g % 2 + 1) * W] + eye
-        right[1 + g] = stats[3, (g // 2) * W : (g // 2 + 1) * W]
-    row_at = lax.broadcasted_iota(jnp.int32, (W, W), 0)
-    unit = 8
-
-    def block(b, carry):
-        base = pl.multiple_of(b * unit, unit)
-        for j in range(unit):
-            for p in range(5):
-                lp, rp = left[p], right[p]
-                lrow = left[p, pl.ds(base, unit)][j : j + 1]
-                rrow = right[p, pl.ds(base, unit)][j : j + 1]
-                scale = 1.0 / lrow[:, j : j + 1]
-                lrow = lrow * scale
-                rrow = rrow * scale
-                column = jnp.broadcast_to(lp[:, j : j + 1], (W, W))
-                here = row_at == base + j
-                column = jnp.where(here, 0.0, column)
-                left[p] = jnp.where(here, lrow, lp - column * lrow)
-                right[p] = jnp.where(here, rrow, rp - column * rrow)
-        for p in range(5):
-            left[p] = pltpu.roll(left[p], W - unit, 1)
-        return carry
-
-    lax.fori_loop(0, W // unit, block, 0)
-    new_transition[...] = right[0].T
-    for g in range(4):
-        new_sensing[g * 64 : (g + 1) * 64] = right[1 + g].T[(g % 2) * 64 : (g % 2 + 1) * 64]
+        parts[at ^ k] = ref[...]
+    rows = lax.broadcasted_iota(jnp.int32, (W, W), 0)
+    lanes = lax.broadcasted_iota(jnp.int32, (W, W), 1)
+    eye = jnp.where(rows == lanes, ridge, 0.0).astype(F32)
+    slabs = [parts[j, W : W + SLAB] for j in range(4)]
+    far = [parts[j, W + SLAB + 8 :] for j in range(4)]
+    lag_here = jnp.concatenate(slabs, axis=0)
+    lag_far = jnp.concatenate(far, axis=0)
+    lag_a = jnp.where(core == 0, lag_here, lag_far)
+    lag_b = jnp.where(core == 0, lag_far, lag_here)
+
+    def upper(tile):
+        return jnp.where(rows <= lanes, tile, 0.0) + jnp.where(rows < lanes, tile, 0.0).T
+
+    def lower(tile, diagonal):
+        below = jnp.where(rows > lanes, tile, 0.0)
+        return below + below.T + jnp.where(rows == lanes, diagonal, 0.0)
+
+    grams = [upper(lag_a)]
+    for tile in range(2):
+        grams.append(upper(parts[tile, 0:W]))
+        grams.append(lower(parts[tile, 0:W], parts[0, W + SLAB + tile : W + SLAB + tile + 1]))
+    done = inverses([gram + eye for gram in grams])
+    lag_cross_t = jnp.where(rows > lanes, lag_a, lag_b)
+    new_transition[...] = exact(lag_cross_t.T, done[0])
+    for tile in range(2):
+        cross = parts[2 + tile, 0:W].T
+        for half in range(2):
+            g = 2 * tile + half
+            new_sensing[g * 64 : (g + 1) * 64] = exact(cross[half * 64 : (half + 1) * 64], done[1 + g])
 
 
 STRIDE = {"x": 1, "z": 4, "y": 16}
@@ -404,17 +447,6 @@
 
 def three(value, axis):
     return [swap(value, axis, k) for k in (1, 2, 3)]
-
-
-def piece(value, index, rows):
-    return lax.dynamic_slice_in_dim(value, index * rows, rows, 0)
-
-
-def scatter_sum(value, axis, at):
-    rows = value.shape[0] // 4
-    own = piece(value, at, rows)
-    got = [swap(piece(value, at ^ k, rows), axis, k) for k in (1, 2, 3)]
-    return (own + got[0]) + (got[1] + got[2])
 
 
 def on_device(telemetry, present, transition, sensing, filter_gain, smooth_gain, initial_state):
@@ -468,24 +500,22 @@
     )
     both = jnp.concatenate([smoothed, incoming], axis=0)
     other_both = swap_core(both)
-    smoothed_out, stats = call(
-        stats_kernel, [shape(2 * ROWS, W), shape(8 * W, W)], 1, 4, [pltpu.VMEM((2 * ROWS, W), F32)]
+    smoothed_out, *chunks = call(
+        stats_kernel, [shape(2 * ROWS, W)] + [shape(CHUNK, W)] * 4, 1, 4,
+        [pltpu.VMEM((2 * ROWS, W), F32), pltpu.VMEM((4, CHUNK, W), F32)],
     )(where, telemetry, flags, both, other_both)
 
-    part = scatter_sum(stats, "x", at_x)
-    part = scatter_sum(part, "z", at_z)
-    got = three(part, "y")
-    part = (part + got[0]) + (got[1] + got[2])
-    got = [part] + three(part, "z")
-    stacked = jnp.stack(got)
-    order = jnp.arange(4) ^ at_z
-    part = jnp.concatenate([lax.dynamic_index_in_dim(stacked, at_z ^ j, 0, keepdims=False) for j in range(4)], axis=0)
-    got = [part] + three(part, "x")
+    got = [swap(chunks[k], "x", k) for k in (1, 2, 3)]
+    part = (chunks[0] + got[0]) + (got[1] + got[2])
+    for axis in ("z", "y"):
+        got = three(part, axis)
+        part = (part + got[0]) + (got[1] + got[2])
+    part = jnp.concatenate([part, swap_core(part[W : W + SLAB])], axis=0)
     ridge = RIDGE * telemetry.shape[0] * lax.axis_size("tm")
     new_transition, new_sensing = call(
         functools.partial(solve_kernel, ridge), [shape(W, W), shape(2 * W, W)], 1, 4,
-        [pltpu.VMEM((4, 2 * W, W), F32), pltpu.VMEM((5, W, W), F32), pltpu.VMEM((5, W, W), F32)],
-    )(where, *got)
+        [pltpu.VMEM((4, CHUNK + SLAB, W), F32)],
+    )(where, part, *three(part, "x"))
     return new_transition, new_sensing, smoothed_out
 
 

time: 228 us -> 172 us (0.75)
  Pallas kernels: 109 us -> 60.9 us
  starting transfers between devices: 54.5 us -> 49.7 us
  waiting for transfers between devices: 47.3 us -> 44.5 us
    pallas_call x1, Pallas kernels: 64.5 us -> 16.6 us  [on_device(): call(functools.partial(solve_kernel, ridge), [shape(W, W), shape(2 * W, W...]
    ppermute x33 -> x30, starting transfers between devices: 53.1 us -> 48.2 us  [swap(): return lax.ppermute(value, 'tm', pairs)]
    ppermute x33 -> x30, waiting for transfers between devices: 42.6 us -> 38.6 us  [swap(): return lax.ppermute(value, 'tm', pairs)]
    ppermute x7 -> x8, waiting for transfers between devices: 4.69 us -> 5.86 us  [swap_core(): return lax.ppermute(value, 'sens', [(0, 1), (1, 0)])]
  transfers between devices with their start and end apart: 40 -> 38, of which waited for: 28 -> 28; matrix products, arithmetic and copies ran while one was open for 1% -> 1% of each run, Pallas kernels for 7% -> 9%
where the time goes in v2:
time: 172 us; the launch traced here: 171 us
  Pallas kernels  60.9 us (35%)
  starting transfers between devices  49.7 us (29%)
  waiting for transfers between devices  44.5 us (26%)
  local copies, waits for them, and re-layouts  13 us (8%)
  other arithmetic  2.16 us (1%)
    ppermute x30, starting transfers between devices, swap(): return lax.ppermute(value, 'tm', pairs)  48.2 us
    ppermute x30, waiting for transfers between devices, swap(): return lax.ppermute(value, 'tm', pairs)  38.6 us
    pallas_call x1, Pallas kernels, on_device(): call(functools.partial(solve_kernel, ridge), [shape(W, W), shape(2 * W, W...  16.6 us
    pallas_call x1, Pallas kernels, on_device(): call(maps_kernel, [shape(SEGS, 5, W, 2 * W, dtype=BF16), shape(SEGS - 1,...  9.44 us
    pallas_call x1, Pallas kernels, on_device(): call(filter_kernel, [shape(ROWS, W), shape(8, W), shape(8, W)], 1, 14 + 8...  8.44 us
    unnamed x42, local copies, waits for them, and re-layouts  7.43 us
    ppermute x8, waiting for transfers between devices, swap_core(): return lax.ppermute(value, 'sens', [(0, 1), (1, 0)])  5.86 us
    pallas_call x1, Pallas kernels, on_device(): call(shift_kernel, [shape(ROWS, W), shape(32, W), shape(PACK, W)], 0, 5)  5.84 us
  transfers between devices with their start and end apart: 38, of which 28 were waited for; matrix products, arithmetic and copies ran while one was open for 1% of the time, Pallas kernels for 9%

profile of v2, /device:TPU:0, one launch (start us, length us, event | category | flops | bytes accessed | tf_op | source)
XLA Modules:
  0.0 171.1 jit_solution(12714111639939925243)
XLA Ops:
  1.2 0.8 copy.10
  3.2 2.3 %shard_map.94 = (f32[256,128]{1,0:T(8,128)}, f32[256,128]{1,0:T(8,128)}) custom-call(s32[4]{0:T(128)} %pad_add_fusion.where, f32[512,256]{1,0:T(8,128)} %tel.3, f32[32,4]{1,0:T(8,128)} %convert_element_type.3.flags.flags_own, f32[128,256]{1,0:T(8,128)} %gain_own.1), custom_call_target="tpu_custom_call" | custom-call | tf_op jit(solution)/shard_map/pallas_call | solution.py:462
  6.0 1.1 collective-permute-done.1.flags_other
  8.4 9.4 %shard_map.95 = (bf16[16,5,128,256]{3,2,1,0:T(8,128)(2,1)}, bf16[15,128,256]{2,1,0:T(8,128)(2,1)}, f32[31,128,128]{2,1,0:T(8,128)}) custom-call(s32[4]{0:T(128)} %pad_add_fusion.where, f32[32,4]{1,0:T(8,128)} %convert_element_type.3.flags.flags_own, f32[32,4]{1,0:T(8,128)} %copy-done.19, f32[128,128]{1,0:T(8,128)} %trans.5, f32[128,256]{1,0:T(8,128)} %gain_own.1, ...), custom_call_target="tpu_custom_call" | custom-call | tf_op jit(solution)/shard_map/pallas_call | solution.py:464
  18.5 5.8 %shard_map.96 = (f32[256,128]{1,0:T(8,128)}, f32[32,128]{1,0:T(8,128)}, f32[136,128]{1,0:T(8,128)}) custom-call(f32[256,128]{1,0:T(8,128)} %get-tuple-element.25.mine, f32[256,128]{1,0:T(8,128)} %copy-done.10, bf16[16,5,128,256]{3,2,1,0:T(8,128)(2,1)} %get-tuple-element.27.powers, bf16[15,128,256]{2,1,0:T(8,128)(2,1)} %get-tuple-element.28.tree, ...), custom_call_target="tpu_custom_call" | custom-call | tf_op jit(solution)/shard_map/pallas_call | solution.py:470
  24.6 1.1 collective-permute-done.4.other.c1
  26.4 1.8 %shard_map.97.own.x0 = f32[136,128]{1,0:T(8,128)} custom-call(s32[4]{0:T(128)} %pad_add_fusion.where, f32[136,128]{1,0:T(8,128)} %get-tuple-element.30.own.c0, f32[136,128]{1,0:T(8,128)} %copy-done.2), custom_call_target="tpu_custom_call" | custom-call | tf_op jit(solution)/shard_map/pallas_call | solution.py:479
  28.2 1.6 collective-permute-start.5
  29.7 2.7 %collective-permute-start.6 = (f32[136,128]{1,0:T(8,128)}, f32[136,128]{1,0:T(8,128)S(1)}, u32[]{:S(2)}, u32[]{:S(2)}) collective-permute-start(f32[136,128]{1,0:T(8,128)} %shard_map.97.own.x0), channel_id=1, source_target_pairs={{0,4},{2,6},{4,0},{6,2},{8,12},{10,14},{12,8},{14,10},{16,20},{18,... | collective-permute-start | bytes 208904 | tf_op jit(solution)/shard_map/ppermute | solution.py:441
  32.9 3.7 %collective-permute-done.6.r2.x2 = f32[136,128]{1,0:T(8,128)S(1)} collective-permute-done((f32[136,128]{1,0:T(8,128)}, f32[136,128]{1,0:T(8,128)S(1)}, u32[]{:S(2)}, u32[]{:S(2)}) %collective-permute-start.6) | collective-permute-done | bytes 69664 | tf_op jit(solution)/shard_map/ppermute | solution.py:441
  36.6 1.6 collective-permute-done.7.r3.x3
  38.8 2.0 %shard_map.98.own.z0 = f32[136,128]{1,0:T(8,128)} custom-call(s32[4]{0:T(128)} %pad_add_fusion.where, f32[136,128]{1,0:T(8,128)} %shard_map.97.own.x0, f32[136,128]{1,0:T(8,128)} %copy-done.3, f32[136,128]{1,0:T(8,128)} %copy-done.4, f32[136,128]{1,0:T(8,128)} %copy-done.5), custom_call_target="tpu_custom_call" | custom-call | tf_op jit(solution)/shard_map/pallas_call | solution.py:482
  40.9 4.0 %collective-permute-start.10 = (f32[136,128]{1,0:T(8,128)}, f32[136,128]{1,0:T(8,128)S(1)}, u32[]{:S(2)}, u32[]{:S(2)}) collective-permute-start(f32[136,128]{1,0:T(8,128)} %shard_map.98.own.z0), channel_id=1, source_target_pairs={{0,24},{2,26},{4,28},{6,30},{8,16},{10,18},{12,20},{14,22},{16,8},... | collective-permute-start | bytes 208904 | tf_op jit(solution)/shard_map/ppermute | solution.py:441
  44.9 1.5 collective-permute-start.9
  46.4 1.3 collective-permute-done.10.r3.z3
  47.7 1.7 collective-permute-done.8.r1.z1
  49.4 1.5 collective-permute-done.9.r2.z2
  51.6 2.1 %shard_map.99.y0 = f32[136,128]{1,0:T(8,128)} custom-call(s32[4]{0:T(128)} %pad_add_fusion.where, f32[136,128]{1,0:T(8,128)} %shard_map.98.own.z0, f32[136,128]{1,0:T(8,128)} %copy-done.7, f32[136,128]{1,0:T(8,128)} %copy-done.8, f32[136,128]{1,0:T(8,128)} %copy-done.6), custom_call_target="tpu_custom_call" | custom-call | tf_op jit(solution)/shard_map/pallas_call | solution.py:484
  53.6 1.6 collective-permute-start.11
  55.2 2.9 %collective-permute-start.12 = (f32[136,128]{1,0:T(8,128)}, f32[136,128]{1,0:T(8,128)S(1)}, u32[]{:S(2)}, u32[]{:S(2)}) collective-permute-start(f32[136,128]{1,0:T(8,128)} %shard_map.99.y0), channel_id=1, source_target_pairs={{0,64},{2,66},{4,68},{6,70},{8,72},{10,74},{12,76},{14,78},{16,80}... | collective-permute-start | bytes 208904 | tf_op jit(solution)/shard_map/ppermute | solution.py:441
  58.3 4.4 %shard_map.100 = (bf16[15,128,256]{2,1,0:T(8,128)(2,1)}, bf16[128,256]{1,0:T(8,128)(2,1)}) custom-call(f32[128,128]{1,0:T(8,128)} %smooth_gain.1, f32[128,128]{1,0:T(8,128)} %trans.5), custom_call_target="tpu_custom_call" | custom-call | tf_op jit(solution)/shard_map/pallas_call | solution.py:474
  62.7 1.1 collective-permute-done.13.y3
  64.5 8.4 %shard_map.101 = (f32[256,128]{1,0:T(8,128)}, f32[8,128]{1,0:T(8,128)}, f32[8,128]{1,0:T(8,128)}) custom-call(s32[4]{0:T(128)} %pad_add_fusion.where, f32[136,128]{1,0:T(8,128)} %shard_map.99.y0, f32[136,128]{1,0:T(8,128)} %copy-done.16, f32[136,128]{1,0:T(8,128)} %copy-done.17, f32[136,128]{1,0:T(8,128)} %copy-done.18, f32[136,128]{1,0:T(8,128)} %shard_map.98.own.z0, ...), custom_call_target="tpu_custom_call" | custom-call | tf_op jit(solution)/shard_map/pallas_call | solution.py:487
  72.9 0.7 slice.6
  73.6 1.1 collective-permute-done.14
  74.7 2.4 %collective-permute-start.16 = (f32[2,128]{1,0:T(2,128)S(1)}, f32[2,128]{1,0:T(2,128)S(1)}, u32[]{:S(2)}, u32[]{:S(2)}) collective-permute-start(f32[2,128]{1,0:T(2,128)S(1)} %pad_maximum_fusion.1), channel_id=1, source_target_pairs={{0,4},{2,6},{4,0},{6,2},{8,12},{10,14},{12,8},{14,10},{16,20},{18,... | collective-permute-start | bytes 3080 | tf_op jit(solution)/shard_map/ppermute | solution.py:441
  77.1 2.3 %collective-permute-start.17 = (f32[2,128]{1,0:T(2,128)S(1)}, f32[2,128]{1,0:T(2,128)S(1)}, u32[]{:S(2)}, u32[]{:S(2)}) collective-permute-start(f32[2,128]{1,0:T(2,128)S(1)} %pad_maximum_fusion.1), channel_id=1, source_target_pairs={{0,6},{2,4},{4,2},{6,0},{8,14},{10,12},{12,10},{14,8},{16,22},{18,... | collective-permute-start | bytes 3080 | tf_op jit(solution)/shard_map/ppermute | solution.py:441
  79.9 2.1 %collective-permute-done.17 = f32[2,128]{1,0:T(2,128)S(1)} collective-permute-done((f32[2,128]{1,0:T(2,128)S(1)}, f32[2,128]{1,0:T(2,128)S(1)}, u32[]{:S(2)}, u32[]{:S(2)}) %collective-permute-start.17) | collective-permute-done | bytes 1056 | tf_op jit(solution)/shard_map/ppermute | solution.py:441
  81.9 2.1 %collective-permute-start.18 = (f32[8,128]{1,0:T(8,128)S(1)}, f32[8,128]{1,0:T(8,128)S(1)}, u32[]{:S(2)}, u32[]{:S(2)}) collective-permute-start(f32[8,128]{1,0:T(8,128)S(1)} %concatenate.22), channel_id=1, source_target_pairs={{0,8},{2,10},{4,12},{6,14},{8,0},{10,2},{12,4},{14,6},{16,24},{18,... | collective-permute-start | bytes 12296 | tf_op jit(solution)/shard_map/ppermute | solution.py:441
  84.0 1.5 collective-permute-start.19
  85.6 1.2 collective-permute-start.20
  86.8 2.3 %collective-permute-done.19 = f32[8,128]{1,0:T(8,128)S(1)} collective-permute-done((f32[8,128]{1,0:T(8,128)S(1)}, f32[8,128]{1,0:T(8,128)S(1)}, u32[]{:S(2)}, u32[]{:S(2)}) %collective-permute-start.19) | collective-permute-done | bytes 4128 | tf_op jit(solution)/shard_map/ppermute | solution.py:441
  89.2 1.2 collective-permute-done.20
  90.5 3.4 %collective-permute-start.22 = (f32[32,128]{1,0:T(8,128)S(1)}, f32[32,128]{1,0:T(8,128)S(1)}, u32[]{:S(2)}, u32[]{:S(2)}) collective-permute-start(f32[32,128]{1,0:T(8,128)S(1)} %concatenate.23), channel_id=1, source_target_pairs={{0,64},{2,66},{4,68},{6,70},{8,72},{10,74},{12,76},{14,78},{16,80}... | collective-permute-start | bytes 49160 | tf_op jit(solution)/shard_map/ppermute | solution.py:441
  93.9 1.3 collective-permute-start.23
  95.8 3.0 %collective-permute-done.23 = f32[32,128]{1,0:T(8,128)S(1)} collective-permute-done((f32[32,128]{1,0:T(8,128)S(1)}, f32[32,128]{1,0:T(8,128)S(1)}, u32[]{:S(2)}, u32[]{:S(2)}) %collective-permute-start.23) | collective-permute-done | bytes 16416 | tf_op jit(solution)/shard_map/ppermute | solution.py:441
  98.8 4.2 %concatenate.24.gathered = f32[128,128]{1,0:T(8,128)} concatenate(f32[1,128]{1,0:T(1,128)S(1)} %slice.6, f32[1,128]{1,0:T(1,128)S(1)} %collective-permute-done.14, f32[2,128]{1,0:T(2,128)S(1)} %collective-permute-done.15, f32[2,128]{1,0:T(2,128)S(1)} %collective-permute-done.16, f32[2,128]{1,0:T(2,128)S(1)} %collective-permute-done.17, f32[8,128]{1,0:T(8,128)S(1)} %collective-permute-done.18, ...), dimensions={0} | concatenate | bytes 131072 | tf_op jit(solution)/shard_map/concatenate | solution.py:497
  103.0 4.7 %shard_map.102 = (f32[256,128]{1,0:T(8,128)}, f32[8,128]{1,0:T(8,128)}) custom-call(s32[4]{0:T(128)} %pad_add_fusion.where, f32[128,128]{1,0:T(8,128)} %concatenate.24.gathered, f32[256,128]{1,0:T(8,128)} %get-tuple-element.36.drives, f32[8,128]{1,0:T(8,128)} %get-tuple-element.37.final, bf16[15,128,256]{2,1,0:T(8,128)(2,1)} %get-tuple-element.33.gain_powers), custom_call_target="tpu_custom_call" | custom-call | tf_op jit(solution)/shard_map/pallas_call | solution.py:498
  107.8 0.9 constant_dynamic-update-slice_fusion.1
  108.7 0.7 constant_dynamic-update-slice_fusion.own
  109.4 1.4 collective-permute-done.24.other
  110.7 0.7 copy-done.9
  111.4 3.3 %shard_map.103 = (f32[512,128]{1,0:T(8,128)}, f32[168,128]{1,0:T(8,128)}, f32[168,128]{1,0:T(8,128)}, f32[168,128]{1,0:T(8,128)}, f32[168,128]{1,0:T(8,128)}) custom-call(s32[4]{0:T(128)} %pad_add_fusion.where, f32[512,256]{1,0:T(8,128)} %tel.3, f32[32,4]{1,0:T(8,128)} %convert_element_type.3.flags.flags_own, f32[264,128]{1,0:T(8,128)} %copy-done, ...), custom_call_target="tpu_custom_call" | custom-call | tf_op jit(solution)/shard_map/pallas_call | solution.py:503
  114.7 3.6 %collective-permute-start.26 = (f32[168,128]{1,0:T(8,128)}, f32[168,128]{1,0:T(8,128)S(1)}, u32[]{:S(2)}, u32[]{:S(2)}) collective-permute-start(f32[168,128]{1,0:T(8,128)} %get-tuple-element.42), channel_id=1, source_target_pairs={{0,4},{2,6},{4,0},{6,2},{8,12},{10,14},{12,8},{14,10},{16,20},{18,... | collective-permute-start | bytes 258056 | tf_op jit(solution)/shard_map/ppermute | solution.py:441
  118.3 1.1 collective-permute-start.27
  119.4 0.9 collective-permute-done.25
  120.2 2.8 %collective-permute-done.26 = f32[168,128]{1,0:T(8,128)S(1)} collective-permute-done((f32[168,128]{1,0:T(8,128)}, f32[168,128]{1,0:T(8,128)S(1)}, u32[]{:S(2)}, u32[]{:S(2)}) %collective-permute-start.26) | collective-permute-done | bytes 86048 | tf_op jit(solution)/shard_map/ppermute | solution.py:441
  123.0 1.7 %collective-permute-done.27 = f32[168,128]{1,0:T(8,128)S(1)} collective-permute-done((f32[168,128]{1,0:T(8,128)}, f32[168,128]{1,0:T(8,128)S(1)}, u32[]{:S(2)}, u32[]{:S(2)}) %collective-permute-start.27) | collective-permute-done | bytes 86048 | tf_op jit(solution)/shard_map/ppermute | solution.py:441
  124.7 0.9 add_add_fusion.2
  125.7 2.8 %collective-permute-start.29 = (f32[168,128]{1,0:T(8,128)S(1)}, f32[168,128]{1,0:T(8,128)S(1)}, u32[]{:S(2)}, u32[]{:S(2)}) collective-permute-start(f32[168,128]{1,0:T(8,128)S(1)} %add_add_fusion.2), channel_id=1, source_target_pairs={{0,16},{2,18},{4,20},{6,22},{8,24},{10,26},{12,28},{14,30},{16,0},... | collective-permute-start | bytes 258056 | tf_op jit(solution)/shard_map/ppermute | solution.py:441
  128.6 1.9 %collective-permute-start.30 = (f32[168,128]{1,0:T(8,128)S(1)}, f32[168,128]{1,0:T(8,128)S(1)}, u32[]{:S(2)}, u32[]{:S(2)}) collective-permute-start(f32[168,128]{1,0:T(8,128)S(1)} %add_add_fusion.2), channel_id=1, source_target_pairs={{0,24},{2,26},{4,28},{6,30},{8,16},{10,18},{12,20},{14,22},{16,8},... | collective-permute-start | bytes 258056 | tf_op jit(solution)/shard_map/ppermute | solution.py:441
  130.8 1.8 %collective-permute-done.29 = f32[168,128]{1,0:T(8,128)S(1)} collective-permute-done((f32[168,128]{1,0:T(8,128)S(1)}, f32[168,128]{1,0:T(8,128)S(1)}, u32[]{:S(2)}, u32[]{:S(2)}) %collective-permute-start.29) | collective-permute-done | bytes 86048 | tf_op jit(solution)/shard_map/ppermute | solution.py:441
  132.6 1.7 collective-permute-done.30
  134.4 2.8 %collective-permute-start.32 = (f32[168,128]{1,0:T(8,128)S(1)}, f32[168,128]{1,0:T(8,128)S(1)}, u32[]{:S(2)}, u32[]{:S(2)}) collective-permute-start(f32[168,128]{1,0:T(8,128)S(1)} %add_add_fusion.1), channel_id=1, source_target_pairs={{0,64},{2,66},{4,68},{6,70},{8,72},{10,74},{12,76},{14,78},{16,80}... | collective-permute-start | bytes 258056 | tf_op jit(solution)/shard_map/ppermute | solution.py:441
  137.1 1.9 %collective-permute-start.33 = (f32[168,128]{1,0:T(8,128)S(1)}, f32[168,128]{1,0:T(8,128)S(1)}, u32[]{:S(2)}, u32[]{:S(2)}) collective-permute-start(f32[168,128]{1,0:T(8,128)S(1)} %add_add_fusion.1), channel_id=1, source_target_pairs={{0,96},{2,98},{4,100},{6,102},{8,104},{10,106},{12,108},{14,110},{... | collective-permute-start | bytes 258056 | tf_op jit(solution)/shard_map/ppermute | solution.py:441
  139.1 1.6 collective-permute-done.32
  140.6 2.2 %collective-permute-done.33 = f32[168,128]{1,0:T(8,128)S(1)} collective-permute-done((f32[168,128]{1,0:T(8,128)S(1)}, f32[168,128]{1,0:T(8,128)S(1)}, u32[]{:S(2)}, u32[]{:S(2)}) %collective-permute-start.33) | collective-permute-done | bytes 86048 | tf_op jit(solution)/shard_map/ppermute | solution.py:441
  143.0 1.2 collective-permute-done.34
  144.2 2.4 %collective-permute-start.36 = (f32[200,128]{1,0:T(8,128)S(1)}, f32[200,128]{1,0:T(8,128)S(1)}, u32[]{:S(2)}, u32[]{:S(2)}) collective-permute-start(f32[200,128]{1,0:T(8,128)S(1)} %pad_maximum_fusion.own), channel_id=1, source_target_pairs={{0,4},{2,6},{4,0},{6,2},{8,12},{10,14},{12,8},{14,10},{16,20},{18,... | collective-permute-start | bytes 307208 | tf_op jit(solution)/shard_map/ppermute | solution.py:441
  146.7 2.3 %collective-permute-start.37 = (f32[200,128]{1,0:T(8,128)S(1)}, f32[200,128]{1,0:T(8,128)S(1)}, u32[]{:S(2)}, u32[]{:S(2)}) collective-permute-start(f32[200,128]{1,0:T(8,128)S(1)} %pad_maximum_fusion.own), channel_id=1, source_target_pairs={{0,6},{2,4},{4,2},{6,0},{8,14},{10,12},{12,10},{14,8},{16,22},{18,... | collective-permute-start | bytes 307208 | tf_op jit(solution)/shard_map/ppermute | solution.py:441
  148.9 1.0 collective-permute-done.35.r1
  150.0 1.9 %collective-permute-done.36.r2 = f32[200,128]{1,0:T(8,128)S(1)} collective-permute-done((f32[200,128]{1,0:T(8,128)S(1)}, f32[200,128]{1,0:T(8,128)S(1)}, u32[]{:S(2)}, u32[]{:S(2)}) %collective-permute-start.36) | collective-permute-done | bytes 102432 | tf_op jit(solution)/shard_map/ppermute | solution.py:441
  151.9 1.9 %collective-permute-done.37.r3 = f32[200,128]{1,0:T(8,128)S(1)} collective-permute-done((f32[200,128]{1,0:T(8,128)S(1)}, f32[200,128]{1,0:T(8,128)S(1)}, u32[]{:S(2)}, u32[]{:S(2)}) %collective-permute-start.37) | collective-permute-done | bytes 102432 | tf_op jit(solution)/shard_map/ppermute | solution.py:441
  154.5 16.6 %shard_map.104 = (f32[128,128]{1,0:T(8,128)}, f32[256,128]{1,0:T(8,128)}) custom-call(s32[4]{0:T(128)} %pad_add_fusion.where, f32[200,128]{1,0:T(8,128)} %copy-done.1, f32[200,128]{1,0:T(8,128)} %copy-done.13, f32[200,128]{1,0:T(8,128)} %copy-done.14, f32[200,128]{1,0:T(8,128)} %copy-done.15), custom_call_target="tpu_custom_call" | custom-call | tf_op jit(solution)/shard_map/pallas_call | solution.py:515
  (78 shorter events, 10.3 us)
Async XLA Ops:
  0.6 6.4 %collective-permute-start.2 = (f32[128,256]{1,0:T(8,128)}, f32[128,256]{1,0:T(8,128)S(1)}, u32[]{:S(2)}, u32[]{:S(2)}) collective-permute-start(f32[128,256]{1,0:T(8,128)} %gain_own.1), channel_id=1, source_target_pairs={{0,1},{1,0},{2,3},{3,2},{4,5},{5,4},{6,7},{7,6},{8,9},{9,8},{10,11... | collective-permute-start | bytes 393224 | tf_op jit(solution)/shard_map/ppermute | solution.py:445
  0.7 6.4 %collective-permute-start.3 = (f32[256,128]{1,0:T(8,128)}, f32[256,128]{1,0:T(8,128)S(1)}, u32[]{:S(2)}, u32[]{:S(2)}) collective-permute-start(f32[256,128]{1,0:T(8,128)} %sense_own.1), channel_id=1, source_target_pairs={{0,1},{1,0},{2,3},{3,2},{4,5},{5,4},{6,7},{7,6},{8,9},{9,8},{10,11... | collective-permute-start | bytes 393224 | tf_op jit(solution)/shard_map/ppermute | solution.py:445
  5.5 12.3 %collective-permute-start = (f32[256,128]{1,0:T(8,128)}, f32[256,128]{1,0:T(8,128)S(1)}, u32[]{:S(2)}, u32[]{:S(2)}) collective-permute-start(f32[256,128]{1,0:T(8,128)} %get-tuple-element.26), channel_id=1, source_target_pairs={{0,1},{1,0},{2,3},{3,2},{4,5},{5,4},{6,7},{7,6},{8,9},{9,8},{10,11... | collective-permute-start | bytes 393224 | tf_op jit(solution)/shard_map/ppermute | solution.py:445
  5.6 1.5 collective-permute-start.1
  7.1 0.6 copy-start.19
  7.1 0.6 copy-start.11
  7.7 0.6 copy-start.12
  17.8 0.7 copy-start.10
  24.3 1.5 collective-permute-start.4
  25.8 0.6 copy-start.2
  28.2 4.7 %collective-permute-start.5 = (f32[136,128]{1,0:T(8,128)}, f32[136,128]{1,0:T(8,128)S(1)}, u32[]{:S(2)}, u32[]{:S(2)}) collective-permute-start(f32[136,128]{1,0:T(8,128)} %shard_map.97.own.x0), channel_id=1, source_target_pairs={{0,2},{2,0},{4,6},{6,4},{8,10},{10,8},{12,14},{14,12},{16,18},{18,... | collective-permute-start | bytes 208904 | tf_op jit(solution)/shard_map/ppermute | solution.py:441
  29.7 6.8 %collective-permute-start.6 = (f32[136,128]{1,0:T(8,128)}, f32[136,128]{1,0:T(8,128)S(1)}, u32[]{:S(2)}, u32[]{:S(2)}) collective-permute-start(f32[136,128]{1,0:T(8,128)} %shard_map.97.own.x0), channel_id=1, source_target_pairs={{0,4},{2,6},{4,0},{6,2},{8,12},{10,14},{12,8},{14,10},{16,20},{18,... | collective-permute-start | bytes 208904 | tf_op jit(solution)/shard_map/ppermute | solution.py:441
  32.5 5.7 %collective-permute-start.7 = (f32[136,128]{1,0:T(8,128)}, f32[136,128]{1,0:T(8,128)S(1)}, u32[]{:S(2)}, u32[]{:S(2)}) collective-permute-start(f32[136,128]{1,0:T(8,128)} %shard_map.97.own.x0), channel_id=1, source_target_pairs={{0,6},{2,4},{4,2},{6,0},{8,14},{10,12},{12,10},{14,8},{16,22},{18,... | collective-permute-start | bytes 208904 | tf_op jit(solution)/shard_map/ppermute | solution.py:441
  32.9 5.3 %copy-start.3 = (f32[136,128]{1,0:T(8,128)}, f32[136,128]{1,0:T(8,128)S(1)}, u32[]{:S(2)}) copy-start(f32[136,128]{1,0:T(8,128)S(1)} %collective-permute-done.5.r1.x1) | copy-start | bytes 208900
  36.6 1.6 copy-start.4
  38.2 0.6 copy-start.5
  40.9 6.8 %collective-permute-start.10 = (f32[136,128]{1,0:T(8,128)}, f32[136,128]{1,0:T(8,128)S(1)}, u32[]{:S(2)}, u32[]{:S(2)}) collective-permute-start(f32[136,128]{1,0:T(8,128)} %shard_map.98.own.z0), channel_id=1, source_target_pairs={{0,24},{2,26},{4,28},{6,30},{8,16},{10,18},{12,20},{14,22},{16,8},... | collective-permute-start | bytes 208904 | tf_op jit(solution)/shard_map/ppermute | solution.py:441
  44.9 4.5 %collective-permute-start.8 = (f32[136,128]{1,0:T(8,128)}, f32[136,128]{1,0:T(8,128)S(1)}, u32[]{:S(2)}, u32[]{:S(2)}) collective-permute-start(f32[136,128]{1,0:T(8,128)} %shard_map.98.own.z0), channel_id=1, source_target_pairs={{0,8},{2,10},{4,12},{6,14},{8,0},{10,2},{12,4},{14,6},{16,24},{18,... | collective-permute-start | bytes 208904 | tf_op jit(solution)/shard_map/ppermute | solution.py:441
  44.9 6.0 %collective-permute-start.9 = (f32[136,128]{1,0:T(8,128)}, f32[136,128]{1,0:T(8,128)S(1)}, u32[]{:S(2)}, u32[]{:S(2)}) collective-permute-start(f32[136,128]{1,0:T(8,128)} %shard_map.98.own.z0), channel_id=1, source_target_pairs={{0,16},{2,18},{4,20},{6,22},{8,24},{10,26},{12,28},{14,30},{16,0},... | collective-permute-start | bytes 208904 | tf_op jit(solution)/shard_map/ppermute | solution.py:441
  47.7 3.2 %copy-start.6 = (f32[136,128]{1,0:T(8,128)}, f32[136,128]{1,0:T(8,128)S(1)}, u32[]{:S(2)}) copy-start(f32[136,128]{1,0:T(8,128)S(1)} %collective-permute-done.10.r3.z3) | copy-start | bytes 208900
  49.4 1.5 copy-start.7
  50.9 0.6 copy-start.8
  53.6 9.1 %collective-permute-start.11 = (f32[136,128]{1,0:T(8,128)}, f32[136,128]{1,0:T(8,128)S(1)}, u32[]{:S(2)}, u32[]{:S(2)}) collective-permute-start(f32[136,128]{1,0:T(8,128)} %shard_map.99.y0), channel_id=1, source_target_pairs={{0,32},{2,34},{4,36},{6,38},{8,40},{10,42},{12,44},{14,46},{16,48}... | collective-permute-start | bytes 208904 | tf_op jit(solution)/shard_map/ppermute | solution.py:441
  55.2 7.5 %collective-permute-start.12 = (f32[136,128]{1,0:T(8,128)}, f32[136,128]{1,0:T(8,128)S(1)}, u32[]{:S(2)}, u32[]{:S(2)}) collective-permute-start(f32[136,128]{1,0:T(8,128)} %shard_map.99.y0), channel_id=1, source_target_pairs={{0,64},{2,66},{4,68},{6,70},{8,72},{10,74},{12,76},{14,78},{16,80}... | collective-permute-start | bytes 208904 | tf_op jit(solution)/shard_map/ppermute | solution.py:441
  58.1 5.7 %collective-permute-start.13 = (f32[136,128]{1,0:T(8,128)}, f32[136,128]{1,0:T(8,128)S(1)}, u32[]{:S(2)}, u32[]{:S(2)}) collective-permute-start(f32[136,128]{1,0:T(8,128)} %shard_map.99.y0), channel_id=1, source_target_pairs={{0,96},{2,98},{4,100},{6,102},{8,104},{10,106},{12,108},{14,110},{... | collective-permute-start | bytes 208904 | tf_op jit(solution)/shard_map/ppermute | solution.py:441
  62.7 1.2 copy-start.16
  62.7 1.2 copy-start.17
  63.8 0.6 copy-start.18
  73.6 1.1 collective-permute-start.14
  74.7 4.7 %collective-permute-start.15 = (f32[2,128]{1,0:T(2,128)S(1)}, f32[2,128]{1,0:T(2,128)S(1)}, u32[]{:S(2)}, u32[]{:S(2)}) collective-permute-start(f32[2,128]{1,0:T(2,128)S(1)} %pad_maximum_fusion.1), channel_id=1, source_target_pairs={{0,2},{2,0},{4,6},{6,4},{8,10},{10,8},{12,14},{14,12},{16,18},{18,... | collective-permute-start | bytes 3080 | tf_op jit(solution)/shard_map/ppermute | solution.py:441
  74.7 5.2 %collective-permute-start.16 = (f32[2,128]{1,0:T(2,128)S(1)}, f32[2,128]{1,0:T(2,128)S(1)}, u32[]{:S(2)}, u32[]{:S(2)}) collective-permute-start(f32[2,128]{1,0:T(2,128)S(1)} %pad_maximum_fusion.1), channel_id=1, source_target_pairs={{0,4},{2,6},{4,0},{6,2},{8,12},{10,14},{12,8},{14,10},{16,20},{18,... | collective-permute-start | bytes 3080 | tf_op jit(solution)/shard_map/ppermute | solution.py:441
  77.1 4.8 %collective-permute-start.17 = (f32[2,128]{1,0:T(2,128)S(1)}, f32[2,128]{1,0:T(2,128)S(1)}, u32[]{:S(2)}, u32[]{:S(2)}) collective-permute-start(f32[2,128]{1,0:T(2,128)S(1)} %pad_maximum_fusion.1), channel_id=1, source_target_pairs={{0,6},{2,4},{4,2},{6,0},{8,14},{10,12},{12,10},{14,8},{16,22},{18,... | collective-permute-start | bytes 3080 | tf_op jit(solution)/shard_map/ppermute | solution.py:441
  81.9 4.9 %collective-permute-start.18 = (f32[8,128]{1,0:T(8,128)S(1)}, f32[8,128]{1,0:T(8,128)S(1)}, u32[]{:S(2)}, u32[]{:S(2)}) collective-permute-start(f32[8,128]{1,0:T(8,128)S(1)} %concatenate.22), channel_id=1, source_target_pairs={{0,8},{2,10},{4,12},{6,14},{8,0},{10,2},{12,4},{14,6},{16,24},{18,... | collective-permute-start | bytes 12296 | tf_op jit(solution)/shard_map/ppermute | solution.py:441
  84.0 5.1 %collective-permute-start.19 = (f32[8,128]{1,0:T(8,128)S(1)}, f32[8,128]{1,0:T(8,128)S(1)}, u32[]{:S(2)}, u32[]{:S(2)}) collective-permute-start(f32[8,128]{1,0:T(8,128)S(1)} %concatenate.22), channel_id=1, source_target_pairs={{0,16},{2,18},{4,20},{6,22},{8,24},{10,26},{12,28},{14,30},{16,0},... | collective-permute-start | bytes 12296 | tf_op jit(solution)/shard_map/ppermute | solution.py:441
  85.6 4.8 %collective-permute-start.20 = (f32[8,128]{1,0:T(8,128)S(1)}, f32[8,128]{1,0:T(8,128)S(1)}, u32[]{:S(2)}, u32[]{:S(2)}) collective-permute-start(f32[8,128]{1,0:T(8,128)S(1)} %concatenate.22), channel_id=1, source_target_pairs={{0,24},{2,26},{4,28},{6,30},{8,16},{10,18},{12,20},{14,22},{16,8},... | collective-permute-start | bytes 12296 | tf_op jit(solution)/shard_map/ppermute | solution.py:441
  90.4 4.8 %collective-permute-start.21 = (f32[32,128]{1,0:T(8,128)S(1)}, f32[32,128]{1,0:T(8,128)S(1)}, u32[]{:S(2)}, u32[]{:S(2)}) collective-permute-start(f32[32,128]{1,0:T(8,128)S(1)} %concatenate.23), channel_id=1, source_target_pairs={{0,32},{2,34},{4,36},{6,38},{8,40},{10,42},{12,44},{14,46},{16,48}... | collective-permute-start | bytes 49160 | tf_op jit(solution)/shard_map/ppermute | solution.py:441
  90.5 5.3 %collective-permute-start.22 = (f32[32,128]{1,0:T(8,128)S(1)}, f32[32,128]{1,0:T(8,128)S(1)}, u32[]{:S(2)}, u32[]{:S(2)}) collective-permute-start(f32[32,128]{1,0:T(8,128)S(1)} %concatenate.23), channel_id=1, source_target_pairs={{0,64},{2,66},{4,68},{6,70},{8,72},{10,74},{12,76},{14,78},{16,80}... | collective-permute-start | bytes 49160 | tf_op jit(solution)/shard_map/ppermute | solution.py:441
  93.9 4.9 %collective-permute-start.23 = (f32[32,128]{1,0:T(8,128)S(1)}, f32[32,128]{1,0:T(8,128)S(1)}, u32[]{:S(2)}, u32[]{:S(2)}) collective-permute-start(f32[32,128]{1,0:T(8,128)S(1)} %concatenate.23), channel_id=1, source_target_pairs={{0,96},{2,98},{4,100},{6,102},{8,104},{10,106},{12,108},{14,110},{... | collective-permute-start | bytes 49160 | tf_op jit(solution)/shard_map/ppermute | solution.py:441
  109.4 1.4 copy-start
  109.4 1.4 collective-permute-start.24
  110.7 0.7 copy-start.9
  114.7 5.6 %collective-permute-start.25 = (f32[168,128]{1,0:T(8,128)}, f32[168,128]{1,0:T(8,128)S(1)}, u32[]{:S(2)}, u32[]{:S(2)}) collective-permute-start(f32[168,128]{1,0:T(8,128)} %get-tuple-element.41), channel_id=1, source_target_pairs={{0,2},{2,0},{4,6},{6,4},{8,10},{10,8},{12,14},{14,12},{16,18},{18,... | collective-permute-start | bytes 258056 | tf_op jit(solution)/shard_map/ppermute | solution.py:441
  114.7 8.3 %collective-permute-start.26 = (f32[168,128]{1,0:T(8,128)}, f32[168,128]{1,0:T(8,128)S(1)}, u32[]{:S(2)}, u32[]{:S(2)}) collective-permute-start(f32[168,128]{1,0:T(8,128)} %get-tuple-element.42), channel_id=1, source_target_pairs={{0,4},{2,6},{4,0},{6,2},{8,12},{10,14},{12,8},{14,10},{16,20},{18,... | collective-permute-start | bytes 258056 | tf_op jit(solution)/shard_map/ppermute | solution.py:441
  118.3 6.5 %collective-permute-start.27 = (f32[168,128]{1,0:T(8,128)}, f32[168,128]{1,0:T(8,128)S(1)}, u32[]{:S(2)}, u32[]{:S(2)}) collective-permute-start(f32[168,128]{1,0:T(8,128)} %get-tuple-element.43), channel_id=1, source_target_pairs={{0,6},{2,4},{4,2},{6,0},{8,14},{10,12},{12,10},{14,8},{16,22},{18,... | collective-permute-start | bytes 258056 | tf_op jit(solution)/shard_map/ppermute | solution.py:441
  125.7 5.1 %collective-permute-start.28 = (f32[168,128]{1,0:T(8,128)S(1)}, f32[168,128]{1,0:T(8,128)S(1)}, u32[]{:S(2)}, u32[]{:S(2)}) collective-permute-start(f32[168,128]{1,0:T(8,128)S(1)} %add_add_fusion.2), channel_id=1, source_target_pairs={{0,8},{2,10},{4,12},{6,14},{8,0},{10,2},{12,4},{14,6},{16,24},{18,... | collective-permute-start | bytes 258056 | tf_op jit(solution)/shard_map/ppermute | solution.py:441
  125.7 6.9 %collective-permute-start.29 = (f32[168,128]{1,0:T(8,128)S(1)}, f32[168,128]{1,0:T(8,128)S(1)}, u32[]{:S(2)}, u32[]{:S(2)}) collective-permute-start(f32[168,128]{1,0:T(8,128)S(1)} %add_add_fusion.2), channel_id=1, source_target_pairs={{0,16},{2,18},{4,20},{6,22},{8,24},{10,26},{12,28},{14,30},{16,0},... | collective-permute-start | bytes 258056 | tf_op jit(solution)/shard_map/ppermute | solution.py:441
  128.6 5.7 %collective-permute-start.30 = (f32[168,128]{1,0:T(8,128)S(1)}, f32[168,128]{1,0:T(8,128)S(1)}, u32[]{:S(2)}, u32[]{:S(2)}) collective-permute-start(f32[168,128]{1,0:T(8,128)S(1)} %add_add_fusion.2), channel_id=1, source_target_pairs={{0,24},{2,26},{4,28},{6,30},{8,16},{10,18},{12,20},{14,22},{16,8},... | collective-permute-start | bytes 258056 | tf_op jit(solution)/shard_map/ppermute | solution.py:441
  134.3 4.8 %collective-permute-start.31 = (f32[168,128]{1,0:T(8,128)S(1)}, f32[168,128]{1,0:T(8,128)S(1)}, u32[]{:S(2)}, u32[]{:S(2)}) collective-permute-start(f32[168,128]{1,0:T(8,128)S(1)} %add_add_fusion.1), channel_id=1, source_target_pairs={{0,32},{2,34},{4,36},{6,38},{8,40},{10,42},{12,44},{14,46},{16,48}... | collective-permute-start | bytes 258056 | tf_op jit(solution)/shard_map/ppermute | solution.py:441
  134.4 6.2 %collective-permute-start.32 = (f32[168,128]{1,0:T(8,128)S(1)}, f32[168,128]{1,0:T(8,128)S(1)}, u32[]{:S(2)}, u32[]{:S(2)}) collective-permute-start(f32[168,128]{1,0:T(8,128)S(1)} %add_add_fusion.1), channel_id=1, source_target_pairs={{0,64},{2,66},{4,68},{6,70},{8,72},{10,74},{12,76},{14,78},{16,80}... | collective-permute-start | bytes 258056 | tf_op jit(solution)/shard_map/ppermute | solution.py:441
  137.1 5.7 %collective-permute-start.33 = (f32[168,128]{1,0:T(8,128)S(1)}, f32[168,128]{1,0:T(8,128)S(1)}, u32[]{:S(2)}, u32[]{:S(2)}) collective-permute-start(f32[168,128]{1,0:T(8,128)S(1)} %add_add_fusion.1), channel_id=1, source_target_pairs={{0,96},{2,98},{4,100},{6,102},{8,104},{10,106},{12,108},{14,110},{... | collective-permute-start | bytes 258056 | tf_op jit(solution)/shard_map/ppermute | solution.py:441
  142.9 1.3 collective-permute-start.34
  144.1 9.7 %copy-start.1 = (f32[200,128]{1,0:T(8,128)}, f32[200,128]{1,0:T(8,128)S(1)}, u32[]{:S(2)}) copy-start(f32[200,128]{1,0:T(8,128)S(1)} %pad_maximum_fusion.own) | copy-start | bytes 307204
  144.2 5.8 %collective-permute-start.35 = (f32[200,128]{1,0:T(8,128)S(1)}, f32[200,128]{1,0:T(8,128)S(1)}, u32[]{:S(2)}, u32[]{:S(2)}) collective-permute-start(f32[200,128]{1,0:T(8,128)S(1)} %pad_maximum_fusion.own), channel_id=1, source_target_pairs={{0,2},{2,0},{4,6},{6,4},{8,10},{10,8},{12,14},{14,12},{16,18},{18,... | collective-permute-start | bytes 307208 | tf_op jit(solution)/shard_map/ppermute | solution.py:441
  144.2 7.6 %collective-permute-start.36 = (f32[200,128]{1,0:T(8,128)S(1)}, f32[200,128]{1,0:T(8,128)S(1)}, u32[]{:S(2)}, u32[]{:S(2)}) collective-permute-start(f32[200,128]{1,0:T(8,128)S(1)} %pad_maximum_fusion.own), channel_id=1, source_target_pairs={{0,4},{2,6},{4,0},{6,2},{8,12},{10,14},{12,8},{14,10},{16,20},{18,... | collective-permute-start | bytes 307208 | tf_op jit(solution)/shard_map/ppermute | solution.py:441
  146.7 7.2 %collective-permute-start.37 = (f32[200,128]{1,0:T(8,128)S(1)}, f32[200,128]{1,0:T(8,128)S(1)}, u32[]{:S(2)}, u32[]{:S(2)}) collective-permute-start(f32[200,128]{1,0:T(8,128)S(1)} %pad_maximum_fusion.own), channel_id=1, source_target_pairs={{0,6},{2,4},{4,2},{6,0},{8,14},{10,12},{12,10},{14,8},{16,22},{18,... | collective-permute-start | bytes 307208 | tf_op jit(solution)/shard_map/ppermute | solution.py:441
  150.0 3.9 %copy-start.13 = (f32[200,128]{1,0:T(8,128)}, f32[200,128]{1,0:T(8,128)S(1)}, u32[]{:S(2)}) copy-start(f32[200,128]{1,0:T(8,128)S(1)} %collective-permute-done.35.r1) | copy-start | bytes 307204
  151.9 1.9 %copy-start.14 = (f32[200,128]{1,0:T(8,128)}, f32[200,128]{1,0:T(8,128)S(1)}, u32[]{:S(2)}) copy-start(f32[200,128]{1,0:T(8,128)S(1)} %collective-permute-done.36.r2) | copy-start | bytes 307204
  153.8 0.6 copy-start.15

commit v3 on v2

--- a/solution.py
+++ b/solution.py
@@ -17,7 +17,7 @@
 PACK = W + 8
 SLAB = W // 4
 CHUNK = W + SLAB + 8
-VMEM_LIMIT = 56 * 1024 * 1024
+VMEM_LIMIT = 24 * 1024 * 1024
 
 
 def halves(value):
@@ -54,21 +54,25 @@
 def call(kernel, out_shapes, n_smem, n_in, scratch=()):
     smem = [pl.BlockSpec(memory_space=pltpu.SMEM)] * n_smem
     vmem = [pl.BlockSpec(memory_space=pltpu.VMEM)] * n_in
-    single = not isinstance(out_shapes, (list, tuple))
-    outs = [out_shapes] if single else list(out_shapes)
-    out_specs = [pl.BlockSpec(memory_space=pltpu.VMEM)] * len(outs)
-    return pl.pallas_call(
+    outs = [out if leaves else pltpu.VMEM(out.shape, out.dtype) for out, leaves in out_shapes]
+    run = pl.pallas_call(
         kernel,
-        out_shape=outs[0] if single else tuple(outs),
+        out_shape=tuple(outs),
         in_specs=smem + vmem,
-        out_specs=out_specs[0] if single else tuple(out_specs),
+        out_specs=tuple([pl.BlockSpec(memory_space=pltpu.VMEM)] * len(outs)),
         scratch_shapes=list(scratch),
         compiler_params=pltpu.CompilerParams(vmem_limit_bytes=VMEM_LIMIT),
     )
 
-
-def shape(*dims, dtype=F32):
-    return jax.ShapeDtypeStruct(dims, dtype)
+    def placed(*operands):
+        near = [pltpu.with_memory_space_constraint(v, pltpu.VMEM) for v in operands[n_smem:]]
+        return run(*operands[:n_smem], *near)
+
+    return placed
+
+
+def shape(*dims, dtype=F32, leaves=False):
+    return jax.ShapeDtypeStruct(dims, dtype), leaves
 
 
 def mask_of(flags, rows, segs):
@@ -476,12 +480,12 @@
     )(smooth_gain, transition)
 
     by_core = [packed, swap_core(packed)]
-    chip = call(pair_kernel, shape(PACK, W), 1, 2)(where, *by_core)
+    (chip,) = call(pair_kernel, [shape(PACK, W)], 1, 2)(where, *by_core)
     ordered = [pltpu.VMEM((4, PACK, W), F32)]
     by_x = [chip] + three(chip, "x")
-    row = call(functools.partial(four_kernel, 2), shape(PACK, W), 1, 4, ordered)(where, *by_x)
+    (row,) = call(functools.partial(four_kernel, 2), [shape(PACK, W)], 1, 4, ordered)(where, *by_x)
     by_z = [row] + three(row, "z")
-    plane = call(functools.partial(four_kernel, 1), shape(PACK, W), 1, 4, ordered)(where, *by_z)
+    (plane,) = call(functools.partial(four_kernel, 1), [shape(PACK, W)], 1, 4, ordered)(where, *by_z)
     by_y = [plane] + three(plane, "y")
 
     drives, final, shift = call(
@@ -501,7 +505,7 @@
     both = jnp.concatenate([smoothed, incoming], axis=0)
     other_both = swap_core(both)
     smoothed_out, *chunks = call(
-        stats_kernel, [shape(2 * ROWS, W)] + [shape(CHUNK, W)] * 4, 1, 4,
+        stats_kernel, [shape(2 * ROWS, W, leaves=True)] + [shape(CHUNK, W)] * 4, 1, 4,
         [pltpu.VMEM((2 * ROWS, W), F32), pltpu.VMEM((4, CHUNK, W), F32)],
     )(where, telemetry, flags, both, other_both)
 
@@ -513,7 +517,7 @@
     part = jnp.concatenate([part, swap_core(part[W : W + SLAB])], axis=0)
     ridge = RIDGE * telemetry.shape[0] * lax.axis_size("tm")
     new_transition, new_sensing = call(
-        functools.partial(solve_kernel, ridge), [shape(W, W), shape(2 * W, W)], 1, 4,
+        functools.partial(solve_kernel, ridge), [shape(W, W, leaves=True), shape(2 * W, W, leaves=True)], 1, 4,
         [pltpu.VMEM((4, CHUNK + SLAB, W), F32)],
     )(where, part, *three(part, "x"))
     return new_transition, new_sensing, smoothed_out

time: 172 us -> 144 us (0.84)
  Pallas kernels: 60.9 us -> 41.3 us
  local copies, waits for them, and re-layouts: 13 us -> 5.46 us
  other arithmetic: 2.16 us -> 0.17 us
    pallas_call x11, Pallas kernels: 60.9 us -> 41.3 us  [placed(): return run(*operands[:n_smem], *near)]
    concatenate x3, local copies, waits for them, and re-layouts: 4.24 us -> 0.07 us  [on_device(): gathered = jnp.concatenate([gathered] + three(gathered, axis), axis=0)]
    unnamed x42 -> x20, local copies, waits for them, and re-layouts: 7.43 us -> 5.38 us
  transfers between devices with their start and end apart: 38 -> 38, of which waited for: 28 -> 30; matrix products, arithmetic and copies ran while one was open for 1% -> 1% of each run, Pallas kernels for 9% -> 7%
where the time goes in v3:
time: 144 us; the launch traced here: 143 us
  starting transfers between devices  50.3 us (35%)
  waiting for transfers between devices  44.9 us (31%)
  Pallas kernels  41.3 us (29%)
  local copies, waits for them, and re-layouts  5.46 us (4%)
    ppermute x30, starting transfers between devices, swap(): return lax.ppermute(value, 'tm', pairs)  48.6 us
    pallas_call x11, Pallas kernels, placed(): return run(*operands[:n_smem], *near)  41.3 us
    ppermute x30, waiting for transfers between devices, swap(): return lax.ppermute(value, 'tm', pairs)  39.5 us
    ppermute x8, waiting for transfers between devices, swap_core(): return lax.ppermute(value, 'sens', [(0, 1), (1, 0)])  5.42 us
    unnamed x20, local copies, waits for them, and re-layouts  5.38 us
  transfers between devices with their start and end apart: 38, of which 30 were waited for; matrix products, arithmetic and copies ran while one was open for 1% of the time, Pallas kernels for 7%

profile of v3, /device:TPU:0, one launch (start us, length us, event | category | flops | bytes accessed | tf_op | source)
XLA Modules:
  0.0 143.0 jit_solution(7554480701880146034)
XLA Ops:
  1.2 0.8 copy.10
  2.1 1.0 copy-done
  3.1 0.9 copy-done.4
  4.0 1.1 shard_map.94
  5.7 0.9 collective-permute-done.1.flags_other
  6.6 0.8 copy-done.2
  7.4 0.9 copy-done.5
  8.3 0.9 copy-done.6
  9.2 6.7 %shard_map.95 = (bf16[16,5,128,256]{3,2,1,0:T(8,128)(2,1)S(1)}, bf16[15,128,256]{2,1,0:T(8,128)(2,1)S(1)}, f32[31,128,128]{2,1,0:T(8,128)S(1)}) custom-call(s32[4]{0:T(128)S(1)} %pad_add_fusion.where, f32[32,4]{1,0:T(8,128)S(1)} %convert_element_type.3.flags.flags_own, f32[32,4]{1,0:T(8,128)S(1)} %collective-permute-done.1.flags_other, ...), custom_call_target="tpu_custom_call" | custom-call | tf_op jit(solution)/shard_map/pallas_call | solution.py:69
  16.0 1.7 %shard_map.96 = (f32[256,128]{1,0:T(8,128)S(1)}, f32[32,128]{1,0:T(8,128)S(1)}, f32[136,128]{1,0:T(8,128)S(1)}) custom-call(f32[256,128]{1,0:T(8,128)S(1)} %get-tuple-element.25.mine, f32[256,128]{1,0:T(8,128)S(1)} %collective-permute-done.received, bf16[16,5,128,256]{3,2,1,0:T(8,128)(2,1)S(1)} %get-tuple-element.27.powers, ...), custom_call_target="tpu_custom_call" | custom-call | tf_op jit(solution)/shard_map/pallas_call | solution.py:69
  18.0 0.9 collective-permute-done.4.other.c1
  19.0 0.7 shard_map.97.own.x0
  19.7 1.7 %collective-permute-start.5 = (f32[136,128]{1,0:T(8,128)S(1)}, f32[136,128]{1,0:T(8,128)S(1)}, u32[]{:S(2)}, u32[]{:S(2)}) collective-permute-start(f32[136,128]{1,0:T(8,128)S(1)} %shard_map.97.own.x0), channel_id=1, source_target_pairs={{0,2},{2,0},{4,6},{6,4},{8,10},{10,8},{12,14},{14,12},{16,18},{18,... | collective-permute-start | bytes 208904 | tf_op jit(solution)/shard_map/ppermute | solution.py:445
  21.4 2.7 %collective-permute-start.6 = (f32[136,128]{1,0:T(8,128)S(1)}, f32[136,128]{1,0:T(8,128)S(1)}, u32[]{:S(2)}, u32[]{:S(2)}) collective-permute-start(f32[136,128]{1,0:T(8,128)S(1)} %shard_map.97.own.x0), channel_id=1, source_target_pairs={{0,4},{2,6},{4,0},{6,2},{8,12},{10,14},{12,8},{14,10},{16,20},{18,... | collective-permute-start | bytes 208904 | tf_op jit(solution)/shard_map/ppermute | solution.py:445
  24.5 3.5 %collective-permute-done.6.r2.x2 = f32[136,128]{1,0:T(8,128)S(1)} collective-permute-done((f32[136,128]{1,0:T(8,128)S(1)}, f32[136,128]{1,0:T(8,128)S(1)}, u32[]{:S(2)}, u32[]{:S(2)}) %collective-permute-start.6) | collective-permute-done | bytes 69664 | tf_op jit(solution)/shard_map/ppermute | solution.py:445
  28.0 1.6 %collective-permute-done.7.r3.x3 = f32[136,128]{1,0:T(8,128)S(1)} collective-permute-done((f32[136,128]{1,0:T(8,128)S(1)}, f32[136,128]{1,0:T(8,128)S(1)}, u32[]{:S(2)}, u32[]{:S(2)}) %collective-permute-start.7) | collective-permute-done | bytes 69664 | tf_op jit(solution)/shard_map/ppermute | solution.py:445
  29.6 1.0 shard_map.98.own.z0
  30.6 4.1 %collective-permute-start.10 = (f32[136,128]{1,0:T(8,128)S(1)}, f32[136,128]{1,0:T(8,128)S(1)}, u32[]{:S(2)}, u32[]{:S(2)}) collective-permute-start(f32[136,128]{1,0:T(8,128)S(1)} %shard_map.98.own.z0), channel_id=1, source_target_pairs={{0,24},{2,26},{4,28},{6,30},{8,16},{10,18},{12,20},{14,22},{16,8},... | collective-permute-start | bytes 208904 | tf_op jit(solution)/shard_map/ppermute | solution.py:445
  34.7 1.6 %collective-permute-start.9 = (f32[136,128]{1,0:T(8,128)S(1)}, f32[136,128]{1,0:T(8,128)S(1)}, u32[]{:S(2)}, u32[]{:S(2)}) collective-permute-start(f32[136,128]{1,0:T(8,128)S(1)} %shard_map.98.own.z0), channel_id=1, source_target_pairs={{0,16},{2,18},{4,20},{6,22},{8,24},{10,26},{12,28},{14,30},{16,0},... | collective-permute-start | bytes 208904 | tf_op jit(solution)/shard_map/ppermute | solution.py:445
  36.3 0.9 collective-permute-done.10.r3.z3
  37.2 1.8 %collective-permute-done.8.r1.z1 = f32[136,128]{1,0:T(8,128)S(1)} collective-permute-done((f32[136,128]{1,0:T(8,128)S(1)}, f32[136,128]{1,0:T(8,128)S(1)}, u32[]{:S(2)}, u32[]{:S(2)}) %collective-permute-start.8) | collective-permute-done | bytes 69664 | tf_op jit(solution)/shard_map/ppermute | solution.py:445
  39.0 1.5 %collective-permute-done.9.r2.z2 = f32[136,128]{1,0:T(8,128)S(1)} collective-permute-done((f32[136,128]{1,0:T(8,128)S(1)}, f32[136,128]{1,0:T(8,128)S(1)}, u32[]{:S(2)}, u32[]{:S(2)}) %collective-permute-start.9) | collective-permute-done | bytes 69664 | tf_op jit(solution)/shard_map/ppermute | solution.py:445
  40.5 1.0 shard_map.99.y0
  41.5 1.6 %collective-permute-start.11 = (f32[136,128]{1,0:T(8,128)S(1)}, f32[136,128]{1,0:T(8,128)S(1)}, u32[]{:S(2)}, u32[]{:S(2)}) collective-permute-start(f32[136,128]{1,0:T(8,128)S(1)} %shard_map.99.y0), channel_id=1, source_target_pairs={{0,32},{2,34},{4,36},{6,38},{8,40},{10,42},{12,44},{14,46},{16,48}... | collective-permute-start | bytes 208904 | tf_op jit(solution)/shard_map/ppermute | solution.py:445
  43.1 2.9 %collective-permute-start.12 = (f32[136,128]{1,0:T(8,128)S(1)}, f32[136,128]{1,0:T(8,128)S(1)}, u32[]{:S(2)}, u32[]{:S(2)}) collective-permute-start(f32[136,128]{1,0:T(8,128)S(1)} %shard_map.99.y0), channel_id=1, source_target_pairs={{0,64},{2,66},{4,68},{6,70},{8,72},{10,74},{12,76},{14,78},{16,80}... | collective-permute-start | bytes 208904 | tf_op jit(solution)/shard_map/ppermute | solution.py:445
  46.3 2.5 %shard_map.100 = (bf16[15,128,256]{2,1,0:T(8,128)(2,1)S(1)}, bf16[128,256]{1,0:T(8,128)(2,1)S(1)}) custom-call(f32[128,128]{1,0:T(8,128)S(1)} %copy-done.7, f32[128,128]{1,0:T(8,128)S(1)} %copy-done.3), custom_call_target="tpu_custom_call" | custom-call | tf_op jit(solution)/shard_map/pallas_call | solution.py:69
  49.1 2.5 %collective-permute-done.13.y3 = f32[136,128]{1,0:T(8,128)S(1)} collective-permute-done((f32[136,128]{1,0:T(8,128)S(1)}, f32[136,128]{1,0:T(8,128)S(1)}, u32[]{:S(2)}, u32[]{:S(2)}) %collective-permute-start.13) | collective-permute-done | bytes 69664 | tf_op jit(solution)/shard_map/ppermute | solution.py:445
  51.6 4.9 %shard_map.101 = (f32[256,128]{1,0:T(8,128)S(1)}, f32[8,128]{1,0:T(8,128)S(1)}, f32[8,128]{1,0:T(8,128)S(1)}) custom-call(s32[4]{0:T(128)S(1)} %pad_add_fusion.where, f32[136,128]{1,0:T(8,128)S(1)} %shard_map.99.y0, f32[136,128]{1,0:T(8,128)S(1)} %collective-permute-done.11.y1, f32[136,128]{1,0:T(8,128)S(1)} %collective-permute-done.12.y2, ...), custom_call_target="tpu_custom_call" | custom-call | tf_op jit(solution)/shard_map/pallas_call | solution.py:69
  56.5 1.1 collective-permute-done.14
  57.6 2.4 %collective-permute-start.16 = (f32[2,128]{1,0:T(2,128)S(1)}, f32[2,128]{1,0:T(2,128)S(1)}, u32[]{:S(2)}, u32[]{:S(2)}) collective-permute-start(f32[2,128]{1,0:T(2,128)S(1)} %pad_maximum_fusion.1), channel_id=1, source_target_pairs={{0,4},{2,6},{4,0},{6,2},{8,12},{10,14},{12,8},{14,10},{16,20},{18,... | collective-permute-start | bytes 3080 | tf_op jit(solution)/shard_map/ppermute | solution.py:445
  60.0 2.3 %collective-permute-start.17 = (f32[2,128]{1,0:T(2,128)S(1)}, f32[2,128]{1,0:T(2,128)S(1)}, u32[]{:S(2)}, u32[]{:S(2)}) collective-permute-start(f32[2,128]{1,0:T(2,128)S(1)} %pad_maximum_fusion.1), channel_id=1, source_target_pairs={{0,6},{2,4},{4,2},{6,0},{8,14},{10,12},{12,10},{14,8},{16,22},{18,... | collective-permute-start | bytes 3080 | tf_op jit(solution)/shard_map/ppermute | solution.py:445
  62.8 2.1 %collective-permute-done.17 = f32[2,128]{1,0:T(2,128)S(1)} collective-permute-done((f32[2,128]{1,0:T(2,128)S(1)}, f32[2,128]{1,0:T(2,128)S(1)}, u32[]{:S(2)}, u32[]{:S(2)}) %collective-permute-start.17) | collective-permute-done | bytes 1056 | tf_op jit(solution)/shard_map/ppermute | solution.py:445
  64.8 2.1 %collective-permute-start.18 = (f32[8,128]{1,0:T(8,128)S(1)}, f32[8,128]{1,0:T(8,128)S(1)}, u32[]{:S(2)}, u32[]{:S(2)}) collective-permute-start(f32[8,128]{1,0:T(8,128)S(1)} %concatenate.22), channel_id=1, source_target_pairs={{0,8},{2,10},{4,12},{6,14},{8,0},{10,2},{12,4},{14,6},{16,24},{18,... | collective-permute-start | bytes 12296 | tf_op jit(solution)/shard_map/ppermute | solution.py:445
  66.9 1.5 %collective-permute-start.19 = (f32[8,128]{1,0:T(8,128)S(1)}, f32[8,128]{1,0:T(8,128)S(1)}, u32[]{:S(2)}, u32[]{:S(2)}) collective-permute-start(f32[8,128]{1,0:T(8,128)S(1)} %concatenate.22), channel_id=1, source_target_pairs={{0,16},{2,18},{4,20},{6,22},{8,24},{10,26},{12,28},{14,30},{16,0},... | collective-permute-start | bytes 12296 | tf_op jit(solution)/shard_map/ppermute | solution.py:445
  68.4 1.3 collective-permute-start.20
  69.7 2.3 %collective-permute-done.19 = f32[8,128]{1,0:T(8,128)S(1)} collective-permute-done((f32[8,128]{1,0:T(8,128)S(1)}, f32[8,128]{1,0:T(8,128)S(1)}, u32[]{:S(2)}, u32[]{:S(2)}) %collective-permute-start.19) | collective-permute-done | bytes 4128 | tf_op jit(solution)/shard_map/ppermute | solution.py:445
  72.0 1.2 collective-permute-done.20
  73.3 1.8 %collective-permute-start.22 = (f32[32,128]{1,0:T(8,128)S(1)}, f32[32,128]{1,0:T(8,128)S(1)}, u32[]{:S(2)}, u32[]{:S(2)}) collective-permute-start(f32[32,128]{1,0:T(8,128)S(1)} %concatenate.23), channel_id=1, source_target_pairs={{0,64},{2,66},{4,68},{6,70},{8,72},{10,74},{12,76},{14,78},{16,80}... | collective-permute-start | bytes 49160 | tf_op jit(solution)/shard_map/ppermute | solution.py:445
  75.1 2.9 %collective-permute-start.23 = (f32[32,128]{1,0:T(8,128)S(1)}, f32[32,128]{1,0:T(8,128)S(1)}, u32[]{:S(2)}, u32[]{:S(2)}) collective-permute-start(f32[32,128]{1,0:T(8,128)S(1)} %concatenate.23), channel_id=1, source_target_pairs={{0,96},{2,98},{4,100},{6,102},{8,104},{10,106},{12,108},{14,110},{... | collective-permute-start | bytes 49160 | tf_op jit(solution)/shard_map/ppermute | solution.py:445
  78.0 0.6 collective-permute-done.22
  78.6 1.4 collective-permute-done.23
  80.1 3.3 %shard_map.102 = (f32[256,128]{1,0:T(8,128)S(1)}, f32[8,128]{1,0:T(8,128)S(1)}) custom-call(s32[4]{0:T(128)S(1)} %pad_add_fusion.where, f32[128,128]{1,0:T(8,128)S(1)} %concatenate.24.gathered, f32[256,128]{1,0:T(8,128)S(1)} %get-tuple-element.36.drives, f32[8,128]{1,0:T(8,128)S(1)} %get-tuple-element.37.final, ...), custom_call_target="tpu_custom_call" | custom-call | tf_op jit(solution)/shard_map/pallas_call | solution.py:69
  83.5 1.3 collective-permute-done.24.other
  84.8 2.4 %shard_map.103 = (f32[512,128]{1,0:T(8,128)}, f32[168,128]{1,0:T(8,128)S(1)}, f32[168,128]{1,0:T(8,128)S(1)}, f32[168,128]{1,0:T(8,128)S(1)}, f32[168,128]{1,0:T(8,128)S(1)}) custom-call(s32[4]{0:T(128)S(1)} %pad_add_fusion.where, f32[512,256]{1,0:T(8,128)S(1)} %copy-done.1, f32[32,4]{1,0:T(8,128)S(1)} %convert_element_type.3.flags.flags_own, ...), custom_call_target="tpu_custom_call" | custom-call | tf_op jit(solution)/shard_map/pallas_call | solution.py:69
  87.2 3.6 %collective-permute-start.26 = (f32[168,128]{1,0:T(8,128)S(1)}, f32[168,128]{1,0:T(8,128)S(1)}, u32[]{:S(2)}, u32[]{:S(2)}) collective-permute-start(f32[168,128]{1,0:T(8,128)S(1)} %get-tuple-element.42), channel_id=1, source_target_pairs={{0,4},{2,6},{4,0},{6,2},{8,12},{10,14},{12,8},{14,10},{16,20},{18,... | collective-permute-start | bytes 258056 | tf_op jit(solution)/shard_map/ppermute | solution.py:445
  90.8 1.1 collective-permute-start.27
  91.9 0.7 collective-permute-done.25
  92.6 2.7 %collective-permute-done.26 = f32[168,128]{1,0:T(8,128)S(1)} collective-permute-done((f32[168,128]{1,0:T(8,128)S(1)}, f32[168,128]{1,0:T(8,128)S(1)}, u32[]{:S(2)}, u32[]{:S(2)}) %collective-permute-start.26) | collective-permute-done | bytes 86048 | tf_op jit(solution)/shard_map/ppermute | solution.py:445
  95.3 1.7 %collective-permute-done.27 = f32[168,128]{1,0:T(8,128)S(1)} collective-permute-done((f32[168,128]{1,0:T(8,128)S(1)}, f32[168,128]{1,0:T(8,128)S(1)}, u32[]{:S(2)}, u32[]{:S(2)}) %collective-permute-start.27) | collective-permute-done | bytes 86048 | tf_op jit(solution)/shard_map/ppermute | solution.py:445
  97.2 2.9 %collective-permute-start.29 = (f32[168,128]{1,0:T(8,128)S(1)}, f32[168,128]{1,0:T(8,128)S(1)}, u32[]{:S(2)}, u32[]{:S(2)}) collective-permute-start(f32[168,128]{1,0:T(8,128)S(1)} %add_add_fusion.2), channel_id=1, source_target_pairs={{0,16},{2,18},{4,20},{6,22},{8,24},{10,26},{12,28},{14,30},{16,0},... | collective-permute-start | bytes 258056 | tf_op jit(solution)/shard_map/ppermute | solution.py:445
  100.0 1.8 %collective-permute-start.30 = (f32[168,128]{1,0:T(8,128)S(1)}, f32[168,128]{1,0:T(8,128)S(1)}, u32[]{:S(2)}, u32[]{:S(2)}) collective-permute-start(f32[168,128]{1,0:T(8,128)S(1)} %add_add_fusion.2), channel_id=1, source_target_pairs={{0,24},{2,26},{4,28},{6,30},{8,16},{10,18},{12,20},{14,22},{16,8},... | collective-permute-start | bytes 258056 | tf_op jit(solution)/shard_map/ppermute | solution.py:445
  102.2 1.9 %collective-permute-done.29 = f32[168,128]{1,0:T(8,128)S(1)} collective-permute-done((f32[168,128]{1,0:T(8,128)S(1)}, f32[168,128]{1,0:T(8,128)S(1)}, u32[]{:S(2)}, u32[]{:S(2)}) %collective-permute-start.29) | collective-permute-done | bytes 86048 | tf_op jit(solution)/shard_map/ppermute | solution.py:445
  104.0 1.7 %collective-permute-done.30 = f32[168,128]{1,0:T(8,128)S(1)} collective-permute-done((f32[168,128]{1,0:T(8,128)S(1)}, f32[168,128]{1,0:T(8,128)S(1)}, u32[]{:S(2)}, u32[]{:S(2)}) %collective-permute-start.30) | collective-permute-done | bytes 86048 | tf_op jit(solution)/shard_map/ppermute | solution.py:445
  105.7 0.6 collective-permute-start.31
  106.4 3.8 %collective-permute-start.32 = (f32[168,128]{1,0:T(8,128)S(1)}, f32[168,128]{1,0:T(8,128)S(1)}, u32[]{:S(2)}, u32[]{:S(2)}) collective-permute-start(f32[168,128]{1,0:T(8,128)S(1)} %add_add_fusion.1), channel_id=1, source_target_pairs={{0,64},{2,66},{4,68},{6,70},{8,72},{10,74},{12,76},{14,78},{16,80}... | collective-permute-start | bytes 258056 | tf_op jit(solution)/shard_map/ppermute | solution.py:445
  111.0 2.7 %collective-permute-done.32 = f32[168,128]{1,0:T(8,128)S(1)} collective-permute-done((f32[168,128]{1,0:T(8,128)S(1)}, f32[168,128]{1,0:T(8,128)S(1)}, u32[]{:S(2)}, u32[]{:S(2)}) %collective-permute-start.32) | collective-permute-done | bytes 86048 | tf_op jit(solution)/shard_map/ppermute | solution.py:445
  113.7 2.2 %collective-permute-done.33 = f32[168,128]{1,0:T(8,128)S(1)} collective-permute-done((f32[168,128]{1,0:T(8,128)S(1)}, f32[168,128]{1,0:T(8,128)S(1)}, u32[]{:S(2)}, u32[]{:S(2)}) %collective-permute-start.33) | collective-permute-done | bytes 86048 | tf_op jit(solution)/shard_map/ppermute | solution.py:445
  116.0 1.2 collective-permute-done.34
  117.3 2.4 %collective-permute-start.36 = (f32[200,128]{1,0:T(8,128)S(1)}, f32[200,128]{1,0:T(8,128)S(1)}, u32[]{:S(2)}, u32[]{:S(2)}) collective-permute-start(f32[200,128]{1,0:T(8,128)S(1)} %pad_maximum_fusion.own), channel_id=1, source_target_pairs={{0,4},{2,6},{4,0},{6,2},{8,12},{10,14},{12,8},{14,10},{16,20},{18,... | collective-permute-start | bytes 307208 | tf_op jit(solution)/shard_map/ppermute | solution.py:445
  119.7 2.3 %collective-permute-start.37 = (f32[200,128]{1,0:T(8,128)S(1)}, f32[200,128]{1,0:T(8,128)S(1)}, u32[]{:S(2)}, u32[]{:S(2)}) collective-permute-start(f32[200,128]{1,0:T(8,128)S(1)} %pad_maximum_fusion.own), channel_id=1, source_target_pairs={{0,6},{2,4},{4,2},{6,0},{8,14},{10,12},{12,10},{14,8},{16,22},{18,... | collective-permute-start | bytes 307208 | tf_op jit(solution)/shard_map/ppermute | solution.py:445
  122.0 1.0 collective-permute-done.35.r1
  123.0 1.9 %collective-permute-done.36.r2 = f32[200,128]{1,0:T(8,128)S(1)} collective-permute-done((f32[200,128]{1,0:T(8,128)S(1)}, f32[200,128]{1,0:T(8,128)S(1)}, u32[]{:S(2)}, u32[]{:S(2)}) %collective-permute-start.36) | collective-permute-done | bytes 102432 | tf_op jit(solution)/shard_map/ppermute | solution.py:445
  125.0 1.9 %collective-permute-done.37.r3 = f32[200,128]{1,0:T(8,128)S(1)} collective-permute-done((f32[200,128]{1,0:T(8,128)S(1)}, f32[200,128]{1,0:T(8,128)S(1)}, u32[]{:S(2)}, u32[]{:S(2)}) %collective-permute-start.37) | collective-permute-done | bytes 102432 | tf_op jit(solution)/shard_map/ppermute | solution.py:445
  126.9 16.1 %shard_map.104 = (f32[128,128]{1,0:T(8,128)}, f32[256,128]{1,0:T(8,128)}) custom-call(s32[4]{0:T(128)S(1)} %pad_add_fusion.where, f32[200,128]{1,0:T(8,128)S(1)} %pad_maximum_fusion.own, f32[200,128]{1,0:T(8,128)S(1)} %collective-permute-done.35.r1, f32[200,128]{1,0:T(8,128)S(1)} %collective-permute-done.36.r2, f32[200,128]{1,0:T(8,128)S(1)} %collective-permute-done.37.r3), custom_call_target="tpu_custom_call" | custom-call | tf_op jit(solution)/shard_map/pallas_call | solution.py:69
  (56 shorter events, 4.8 us)
Async XLA Ops:
  0.6 5.9 %collective-permute-start.2 = (f32[128,256]{1,0:T(8,128)}, f32[128,256]{1,0:T(8,128)S(1)}, u32[]{:S(2)}, u32[]{:S(2)}) collective-permute-start(f32[128,256]{1,0:T(8,128)} %gain_own.1), channel_id=1, source_target_pairs={{0,1},{1,0},{2,3},{3,2},{4,5},{5,4},{6,7},{7,6},{8,9},{9,8},{10,11... | collective-permute-start | bytes 393224 | tf_op jit(solution)/shard_map/ppermute | solution.py:449
  0.7 5.8 %collective-permute-start.3 = (f32[256,128]{1,0:T(8,128)}, f32[256,128]{1,0:T(8,128)S(1)}, u32[]{:S(2)}, u32[]{:S(2)}) collective-permute-start(f32[256,128]{1,0:T(8,128)} %sense_own.1), channel_id=1, source_target_pairs={{0,1},{1,0},{2,3},{3,2},{4,5},{5,4},{6,7},{7,6},{8,9},{9,8},{10,11... | collective-permute-start | bytes 393224 | tf_op jit(solution)/shard_map/ppermute | solution.py:449
  2.1 1.0 copy-start
  3.1 0.9 copy-start.4
  4.0 42.3 %copy-start.3 = (f32[128,128]{1,0:T(8,128)S(1)}, f32[128,128]{1,0:T(8,128)}, u32[]{:S(2)}) copy-start(f32[128,128]{1,0:T(8,128)} %trans.5) | copy-start | bytes 196612
  4.0 42.3 %copy-start.7 = (f32[128,128]{1,0:T(8,128)S(1)}, f32[128,128]{1,0:T(8,128)}, u32[]{:S(2)}) copy-start(f32[128,128]{1,0:T(8,128)} %smooth_gain.1) | copy-start | bytes 196612
  5.1 46.5 %copy-start.8 = (f32[128]{0:T(128)S(1)}, f32[128]{0:T(128)}, u32[]{:S(2)}) copy-start(f32[128]{0:T(128)} %param.13) | copy-start | bytes 1540
  5.1 10.9 %collective-permute-start = (f32[256,128]{1,0:T(8,128)S(1)}, f32[256,128]{1,0:T(8,128)S(1)}, u32[]{:S(2)}, u32[]{:S(2)}) collective-permute-start(f32[256,128]{1,0:T(8,128)S(1)} %get-tuple-element.26), channel_id=1, source_target_pairs={{0,1},{1,0},{2,3},{3,2},{4,5},{5,4},{6,7},{7,6},{8,9},{9,8},{10,11... | collective-permute-start | bytes 393224 | tf_op jit(solution)/shard_map/ppermute | solution.py:449
  5.3 1.3 collective-permute-start.1
  6.6 0.8 copy-start.2
  7.4 0.9 copy-start.5
  8.3 0.9 copy-start.6
  17.7 1.3 collective-permute-start.4
  19.7 4.8 %collective-permute-start.5 = (f32[136,128]{1,0:T(8,128)S(1)}, f32[136,128]{1,0:T(8,128)S(1)}, u32[]{:S(2)}, u32[]{:S(2)}) collective-permute-start(f32[136,128]{1,0:T(8,128)S(1)} %shard_map.97.own.x0), channel_id=1, source_target_pairs={{0,2},{2,0},{4,6},{6,4},{8,10},{10,8},{12,14},{14,12},{16,18},{18,... | collective-permute-start | bytes 208904 | tf_op jit(solution)/shard_map/ppermute | solution.py:445
  21.4 6.6 %collective-permute-start.6 = (f32[136,128]{1,0:T(8,128)S(1)}, f32[136,128]{1,0:T(8,128)S(1)}, u32[]{:S(2)}, u32[]{:S(2)}) collective-permute-start(f32[136,128]{1,0:T(8,128)S(1)} %shard_map.97.own.x0), channel_id=1, source_target_pairs={{0,4},{2,6},{4,0},{6,2},{8,12},{10,14},{12,8},{14,10},{16,20},{18,... | collective-permute-start | bytes 208904 | tf_op jit(solution)/shard_map/ppermute | solution.py:445
  24.1 5.5 %collective-permute-start.7 = (f32[136,128]{1,0:T(8,128)S(1)}, f32[136,128]{1,0:T(8,128)S(1)}, u32[]{:S(2)}, u32[]{:S(2)}) collective-permute-start(f32[136,128]{1,0:T(8,128)S(1)} %shard_map.97.own.x0), channel_id=1, source_target_pairs={{0,6},{2,4},{4,2},{6,0},{8,14},{10,12},{12,10},{14,8},{16,22},{18,... | collective-permute-start | bytes 208904 | tf_op jit(solution)/shard_map/ppermute | solution.py:445
  30.6 54.3 %copy-start.1 = (f32[512,256]{1,0:T(8,128)S(1)}, f32[512,256]{1,0:T(8,128)}, u32[]{:S(2)}) copy-start(f32[512,256]{1,0:T(8,128)} %tel.3) | copy-start | bytes 1572868
  30.6 6.6 %collective-permute-start.10 = (f32[136,128]{1,0:T(8,128)S(1)}, f32[136,128]{1,0:T(8,128)S(1)}, u32[]{:S(2)}, u32[]{:S(2)}) collective-permute-start(f32[136,128]{1,0:T(8,128)S(1)} %shard_map.98.own.z0), channel_id=1, source_target_pairs={{0,24},{2,26},{4,28},{6,30},{8,16},{10,18},{12,20},{14,22},{16,8},... | collective-permute-start | bytes 208904 | tf_op jit(solution)/shard_map/ppermute | solution.py:445
  34.7 4.3 %collective-permute-start.8 = (f32[136,128]{1,0:T(8,128)S(1)}, f32[136,128]{1,0:T(8,128)S(1)}, u32[]{:S(2)}, u32[]{:S(2)}) collective-permute-start(f32[136,128]{1,0:T(8,128)S(1)} %shard_map.98.own.z0), channel_id=1, source_target_pairs={{0,8},{2,10},{4,12},{6,14},{8,0},{10,2},{12,4},{14,6},{16,24},{18,... | collective-permute-start | bytes 208904 | tf_op jit(solution)/shard_map/ppermute | solution.py:445
  34.7 5.8 %collective-permute-start.9 = (f32[136,128]{1,0:T(8,128)S(1)}, f32[136,128]{1,0:T(8,128)S(1)}, u32[]{:S(2)}, u32[]{:S(2)}) collective-permute-start(f32[136,128]{1,0:T(8,128)S(1)} %shard_map.98.own.z0), channel_id=1, source_target_pairs={{0,16},{2,18},{4,20},{6,22},{8,24},{10,26},{12,28},{14,30},{16,0},... | collective-permute-start | bytes 208904 | tf_op jit(solution)/shard_map/ppermute | solution.py:445
  41.5 7.3 %collective-permute-start.11 = (f32[136,128]{1,0:T(8,128)S(1)}, f32[136,128]{1,0:T(8,128)S(1)}, u32[]{:S(2)}, u32[]{:S(2)}) collective-permute-start(f32[136,128]{1,0:T(8,128)S(1)} %shard_map.99.y0), channel_id=1, source_target_pairs={{0,32},{2,34},{4,36},{6,38},{8,40},{10,42},{12,44},{14,46},{16,48}... | collective-permute-start | bytes 208904 | tf_op jit(solution)/shard_map/ppermute | solution.py:445
  43.1 5.9 %collective-permute-start.12 = (f32[136,128]{1,0:T(8,128)S(1)}, f32[136,128]{1,0:T(8,128)S(1)}, u32[]{:S(2)}, u32[]{:S(2)}) collective-permute-start(f32[136,128]{1,0:T(8,128)S(1)} %shard_map.99.y0), channel_id=1, source_target_pairs={{0,64},{2,66},{4,68},{6,70},{8,72},{10,74},{12,76},{14,78},{16,80}... | collective-permute-start | bytes 208904 | tf_op jit(solution)/shard_map/ppermute | solution.py:445
  46.0 5.5 %collective-permute-start.13 = (f32[136,128]{1,0:T(8,128)S(1)}, f32[136,128]{1,0:T(8,128)S(1)}, u32[]{:S(2)}, u32[]{:S(2)}) collective-permute-start(f32[136,128]{1,0:T(8,128)S(1)} %shard_map.99.y0), channel_id=1, source_target_pairs={{0,96},{2,98},{4,100},{6,102},{8,104},{10,106},{12,108},{14,110},{... | collective-permute-start | bytes 208904 | tf_op jit(solution)/shard_map/ppermute | solution.py:445
  56.4 1.1 collective-permute-start.14
  57.6 4.7 %collective-permute-start.15 = (f32[2,128]{1,0:T(2,128)S(1)}, f32[2,128]{1,0:T(2,128)S(1)}, u32[]{:S(2)}, u32[]{:S(2)}) collective-permute-start(f32[2,128]{1,0:T(2,128)S(1)} %pad_maximum_fusion.1), channel_id=1, source_target_pairs={{0,2},{2,0},{4,6},{6,4},{8,10},{10,8},{12,14},{14,12},{16,18},{18,... | collective-permute-start | bytes 3080 | tf_op jit(solution)/shard_map/ppermute | solution.py:445
  57.6 5.2 %collective-permute-start.16 = (f32[2,128]{1,0:T(2,128)S(1)}, f32[2,128]{1,0:T(2,128)S(1)}, u32[]{:S(2)}, u32[]{:S(2)}) collective-permute-start(f32[2,128]{1,0:T(2,128)S(1)} %pad_maximum_fusion.1), channel_id=1, source_target_pairs={{0,4},{2,6},{4,0},{6,2},{8,12},{10,14},{12,8},{14,10},{16,20},{18,... | collective-permute-start | bytes 3080 | tf_op jit(solution)/shard_map/ppermute | solution.py:445
  60.0 4.8 %collective-permute-start.17 = (f32[2,128]{1,0:T(2,128)S(1)}, f32[2,128]{1,0:T(2,128)S(1)}, u32[]{:S(2)}, u32[]{:S(2)}) collective-permute-start(f32[2,128]{1,0:T(2,128)S(1)} %pad_maximum_fusion.1), channel_id=1, source_target_pairs={{0,6},{2,4},{4,2},{6,0},{8,14},{10,12},{12,10},{14,8},{16,22},{18,... | collective-permute-start | bytes 3080 | tf_op jit(solution)/shard_map/ppermute | solution.py:445
  64.8 4.9 %collective-permute-start.18 = (f32[8,128]{1,0:T(8,128)S(1)}, f32[8,128]{1,0:T(8,128)S(1)}, u32[]{:S(2)}, u32[]{:S(2)}) collective-permute-start(f32[8,128]{1,0:T(8,128)S(1)} %concatenate.22), channel_id=1, source_target_pairs={{0,8},{2,10},{4,12},{6,14},{8,0},{10,2},{12,4},{14,6},{16,24},{18,... | collective-permute-start | bytes 12296 | tf_op jit(solution)/shard_map/ppermute | solution.py:445
  66.9 5.1 %collective-permute-start.19 = (f32[8,128]{1,0:T(8,128)S(1)}, f32[8,128]{1,0:T(8,128)S(1)}, u32[]{:S(2)}, u32[]{:S(2)}) collective-permute-start(f32[8,128]{1,0:T(8,128)S(1)} %concatenate.22), channel_id=1, source_target_pairs={{0,16},{2,18},{4,20},{6,22},{8,24},{10,26},{12,28},{14,30},{16,0},... | collective-permute-start | bytes 12296 | tf_op jit(solution)/shard_map/ppermute | solution.py:445
  68.4 4.8 %collective-permute-start.20 = (f32[8,128]{1,0:T(8,128)S(1)}, f32[8,128]{1,0:T(8,128)S(1)}, u32[]{:S(2)}, u32[]{:S(2)}) collective-permute-start(f32[8,128]{1,0:T(8,128)S(1)} %concatenate.22), channel_id=1, source_target_pairs={{0,24},{2,26},{4,28},{6,30},{8,16},{10,18},{12,20},{14,22},{16,8},... | collective-permute-start | bytes 12296 | tf_op jit(solution)/shard_map/ppermute | solution.py:445
  73.2 4.8 %collective-permute-start.21 = (f32[32,128]{1,0:T(8,128)S(1)}, f32[32,128]{1,0:T(8,128)S(1)}, u32[]{:S(2)}, u32[]{:S(2)}) collective-permute-start(f32[32,128]{1,0:T(8,128)S(1)} %concatenate.23), channel_id=1, source_target_pairs={{0,32},{2,34},{4,36},{6,38},{8,40},{10,42},{12,44},{14,46},{16,48}... | collective-permute-start | bytes 49160 | tf_op jit(solution)/shard_map/ppermute | solution.py:445
  73.3 5.3 %collective-permute-start.22 = (f32[32,128]{1,0:T(8,128)S(1)}, f32[32,128]{1,0:T(8,128)S(1)}, u32[]{:S(2)}, u32[]{:S(2)}) collective-permute-start(f32[32,128]{1,0:T(8,128)S(1)} %concatenate.23), channel_id=1, source_target_pairs={{0,64},{2,66},{4,68},{6,70},{8,72},{10,74},{12,76},{14,78},{16,80}... | collective-permute-start | bytes 49160 | tf_op jit(solution)/shard_map/ppermute | solution.py:445
  75.1 4.9 %collective-permute-start.23 = (f32[32,128]{1,0:T(8,128)S(1)}, f32[32,128]{1,0:T(8,128)S(1)}, u32[]{:S(2)}, u32[]{:S(2)}) collective-permute-start(f32[32,128]{1,0:T(8,128)S(1)} %concatenate.23), channel_id=1, source_target_pairs={{0,96},{2,98},{4,100},{6,102},{8,104},{10,106},{12,108},{14,110},{... | collective-permute-start | bytes 49160 | tf_op jit(solution)/shard_map/ppermute | solution.py:445
  83.4 1.4 %collective-permute-start.24 = (f32[264,128]{1,0:T(8,128)S(1)}, f32[264,128]{1,0:T(8,128)S(1)}, u32[]{:S(2)}, u32[]{:S(2)}) collective-permute-start(f32[264,128]{1,0:T(8,128)S(1)} %constant_dynamic-update-slice_fusion.own), channel_id=1, source_target_pairs={{0,1},{1,0},{2,3},{3,2},{4,5},{5,4},{6,7},{7,6},{8,9},{9,8},{10,11... | collective-permute-start | bytes 405512 | tf_op jit(solution)/shard_map/ppermute | solution.py:449
  87.2 5.4 %collective-permute-start.25 = (f32[168,128]{1,0:T(8,128)S(1)}, f32[168,128]{1,0:T(8,128)S(1)}, u32[]{:S(2)}, u32[]{:S(2)}) collective-permute-start(f32[168,128]{1,0:T(8,128)S(1)} %get-tuple-element.41), channel_id=1, source_target_pairs={{0,2},{2,0},{4,6},{6,4},{8,10},{10,8},{12,14},{14,12},{16,18},{18,... | collective-permute-start | bytes 258056 | tf_op jit(solution)/shard_map/ppermute | solution.py:445
  87.2 8.1 %collective-permute-start.26 = (f32[168,128]{1,0:T(8,128)S(1)}, f32[168,128]{1,0:T(8,128)S(1)}, u32[]{:S(2)}, u32[]{:S(2)}) collective-permute-start(f32[168,128]{1,0:T(8,128)S(1)} %get-tuple-element.42), channel_id=1, source_target_pairs={{0,4},{2,6},{4,0},{6,2},{8,12},{10,14},{12,8},{14,10},{16,20},{18,... | collective-permute-start | bytes 258056 | tf_op jit(solution)/shard_map/ppermute | solution.py:445
  90.8 6.2 %collective-permute-start.27 = (f32[168,128]{1,0:T(8,128)S(1)}, f32[168,128]{1,0:T(8,128)S(1)}, u32[]{:S(2)}, u32[]{:S(2)}) collective-permute-start(f32[168,128]{1,0:T(8,128)S(1)} %get-tuple-element.43), channel_id=1, source_target_pairs={{0,6},{2,4},{4,2},{6,0},{8,14},{10,12},{12,10},{14,8},{16,22},{18,... | collective-permute-start | bytes 258056 | tf_op jit(solution)/shard_map/ppermute | solution.py:445
  97.1 5.1 %collective-permute-start.28 = (f32[168,128]{1,0:T(8,128)S(1)}, f32[168,128]{1,0:T(8,128)S(1)}, u32[]{:S(2)}, u32[]{:S(2)}) collective-permute-start(f32[168,128]{1,0:T(8,128)S(1)} %add_add_fusion.2), channel_id=1, source_target_pairs={{0,8},{2,10},{4,12},{6,14},{8,0},{10,2},{12,4},{14,6},{16,24},{18,... | collective-permute-start | bytes 258056 | tf_op jit(solution)/shard_map/ppermute | solution.py:445
  97.2 6.9 %collective-permute-start.29 = (f32[168,128]{1,0:T(8,128)S(1)}, f32[168,128]{1,0:T(8,128)S(1)}, u32[]{:S(2)}, u32[]{:S(2)}) collective-permute-start(f32[168,128]{1,0:T(8,128)S(1)} %add_add_fusion.2), channel_id=1, source_target_pairs={{0,16},{2,18},{4,20},{6,22},{8,24},{10,26},{12,28},{14,30},{16,0},... | collective-permute-start | bytes 258056 | tf_op jit(solution)/shard_map/ppermute | solution.py:445
  100.0 5.7 %collective-permute-start.30 = (f32[168,128]{1,0:T(8,128)S(1)}, f32[168,128]{1,0:T(8,128)S(1)}, u32[]{:S(2)}, u32[]{:S(2)}) collective-permute-start(f32[168,128]{1,0:T(8,128)S(1)} %add_add_fusion.2), channel_id=1, source_target_pairs={{0,24},{2,26},{4,28},{6,30},{8,16},{10,18},{12,20},{14,22},{16,8},... | collective-permute-start | bytes 258056 | tf_op jit(solution)/shard_map/ppermute | solution.py:445
  105.7 5.3 %collective-permute-start.31 = (f32[168,128]{1,0:T(8,128)S(1)}, f32[168,128]{1,0:T(8,128)S(1)}, u32[]{:S(2)}, u32[]{:S(2)}) collective-permute-start(f32[168,128]{1,0:T(8,128)S(1)} %add_add_fusion.1), channel_id=1, source_target_pairs={{0,32},{2,34},{4,36},{6,38},{8,40},{10,42},{12,44},{14,46},{16,48}... | collective-permute-start | bytes 258056 | tf_op jit(solution)/shard_map/ppermute | solution.py:445
  106.4 7.3 %collective-permute-start.32 = (f32[168,128]{1,0:T(8,128)S(1)}, f32[168,128]{1,0:T(8,128)S(1)}, u32[]{:S(2)}, u32[]{:S(2)}) collective-permute-start(f32[168,128]{1,0:T(8,128)S(1)} %add_add_fusion.1), channel_id=1, source_target_pairs={{0,64},{2,66},{4,68},{6,70},{8,72},{10,74},{12,76},{14,78},{16,80}... | collective-permute-start | bytes 258056 | tf_op jit(solution)/shard_map/ppermute | solution.py:445
  110.2 5.7 %collective-permute-start.33 = (f32[168,128]{1,0:T(8,128)S(1)}, f32[168,128]{1,0:T(8,128)S(1)}, u32[]{:S(2)}, u32[]{:S(2)}) collective-permute-start(f32[168,128]{1,0:T(8,128)S(1)} %add_add_fusion.1), channel_id=1, source_target_pairs={{0,96},{2,98},{4,100},{6,102},{8,104},{10,106},{12,108},{14,110},{... | collective-permute-start | bytes 258056 | tf_op jit(solution)/shard_map/ppermute | solution.py:445
  115.9 1.3 collective-permute-start.34
  117.2 5.8 %collective-permute-start.35 = (f32[200,128]{1,0:T(8,128)S(1)}, f32[200,128]{1,0:T(8,128)S(1)}, u32[]{:S(2)}, u32[]{:S(2)}) collective-permute-start(f32[200,128]{1,0:T(8,128)S(1)} %pad_maximum_fusion.own), channel_id=1, source_target_pairs={{0,2},{2,0},{4,6},{6,4},{8,10},{10,8},{12,14},{14,12},{16,18},{18,... | collective-permute-start | bytes 307208 | tf_op jit(solution)/shard_map/ppermute | solution.py:445
  117.3 7.7 %collective-permute-start.36 = (f32[200,128]{1,0:T(8,128)S(1)}, f32[200,128]{1,0:T(8,128)S(1)}, u32[]{:S(2)}, u32[]{:S(2)}) collective-permute-start(f32[200,128]{1,0:T(8,128)S(1)} %pad_maximum_fusion.own), channel_id=1, source_target_pairs={{0,4},{2,6},{4,0},{6,2},{8,12},{10,14},{12,8},{14,10},{16,20},{18,... | collective-permute-start | bytes 307208 | tf_op jit(solution)/shard_map/ppermute | solution.py:445
  119.7 7.2 %collective-permute-start.37 = (f32[200,128]{1,0:T(8,128)S(1)}, f32[200,128]{1,0:T(8,128)S(1)}, u32[]{:S(2)}, u32[]{:S(2)}) collective-permute-start(f32[200,128]{1,0:T(8,128)S(1)} %pad_maximum_fusion.own), channel_id=1, source_target_pairs={{0,6},{2,4},{4,2},{6,0},{8,14},{10,12},{12,10},{14,8},{16,22},{18,... | collective-permute-start | bytes 307208 | tf_op jit(solution)/shard_map/ppermute | solution.py:445

commit v4 on v3

--- a/solution.py
+++ b/solution.py
@@ -15,8 +15,12 @@
 LEN = 16
 ROWS = SEGS * LEN
 PACK = W + 8
-SLAB = W // 4
-CHUNK = W + SLAB + 8
+NEAR = 8
+FAR = 8
+PLANE = 16
+PLANES = 4
+STATS = 6 * W
+SLICE = STATS // PLANE
 VMEM_LIMIT = 24 * 1024 * 1024
 
 
@@ -51,7 +55,7 @@
     return jnp.where(rows == cols, 1.0, 0.0).astype(F32)
 
 
-def call(kernel, out_shapes, n_smem, n_in, scratch=()):
+def call(kernel, out_shapes, n_smem, n_in, scratch=(), far=()):
     smem = [pl.BlockSpec(memory_space=pltpu.SMEM)] * n_smem
     vmem = [pl.BlockSpec(memory_space=pltpu.VMEM)] * n_in
     outs = [out if leaves else pltpu.VMEM(out.shape, out.dtype) for out, leaves in out_shapes]
@@ -65,7 +69,10 @@
     )
 
     def placed(*operands):
-        near = [pltpu.with_memory_space_constraint(v, pltpu.VMEM) for v in operands[n_smem:]]
+        near = [
+            pltpu.with_memory_space_constraint(v, pltpu.HBM if i in far else pltpu.VMEM)
+            for i, v in enumerate(operands[n_smem:])
+        ]
         return run(*operands[:n_smem], *near)
 
     return placed
@@ -93,7 +100,7 @@
     gain_t = gain[...].T
     packed = wide(gain_t)
     fl = flags[...]
-    for out, core in ((theirs, 1 - where[3]), (mine, where[3])):
+    for out, core in ((theirs, 1 - where[1]), (mine, where[1])):
         start = pl.multiple_of(core * ROWS, ROWS)
         seg_start = pl.multiple_of(core * SEGS, SEGS)
         mask = mask_of(flags[pl.ds(seg_start, SEGS), :], ROWS, SEGS)
@@ -104,9 +111,19 @@
         out[...] = total[:, :W] + total[:, W:]
 
 
+def gain_maps(dev, trans_dev, gain_powers, drive_map):
+    dev_wide = wide(dev)
+    drive_map[...] = wide(-chained(trans_dev, dev, dev_wide))
+    for level in range(15):
+        gain_powers[level] = dev_wide
+        if level < 14:
+            dev = 2.0 * dev + times(dev_wide, dev_wide)
+            dev_wide = wide(dev)
+
+
 def maps_kernel(
-    where, flags_own, flags_other, trans, gain_own, gain_other, sense_own, sense_other,
-    powers, tree, whole, removed, single,
+    where, flags_own, flags_other, trans, gain_own, gain_other, sense_own, sense_other, smooth_gain,
+    powers, tree, whole, gain_powers, drive_map, removed, single,
 ):
     a = trans[...]
     a_wide = wide(a)
@@ -129,7 +146,7 @@
         devs = []
         for j in range(batch):
             k = i * batch + j
-            row = where[3] * SEGS + k
+            row = where[1] * SEGS + k
             dev = single[...]
             for g in range(4):
                 dev = dev - flags_own[row, g] * removed[g]
@@ -146,6 +163,7 @@
         return carry
 
     lax.fori_loop(0, SEGS // batch, group, 0)
+    gain_maps(smooth_gain[...].T - identity(), base, gain_powers, drive_map)
     count, base_at, source_at = SEGS, SEGS, 0
     while count > 1:
         for p in range(count // 2):
@@ -190,7 +208,7 @@
             ends[at + p : at + p + 1] = row
         at += len(level)
     packed[0:W] = whole[2 * SEGS - 2]
-    packed[W:PACK] = jnp.broadcast_to(level[0], (8, W))
+    packed[W:PACK] = jnp.broadcast_to(level[0], (PACK - W, W))
 
 
 def join2(first, second):
@@ -201,41 +219,68 @@
     return dev, row
 
 
+def repeated(out, row, value, copies, rows):
+    for j in range(copies):
+        out[j * rows + row : j * rows + row + value.shape[0]] = value
+
+
 def pair_kernel(where, own, other, out):
-    core = where[3]
+    core = where[1]
     mine, theirs = own[...], other[...]
     first = jnp.where(core == 0, mine, theirs)
     second = jnp.where(core == 0, theirs, mine)
     dev, row = join2(first, second)
-    out[0:W] = dev
-    out[W:PACK] = row
-
-
-def four_kernel(axis, where, own, r1, r2, r3, out, ordered):
-    at = where[axis]
-    for k, ref in enumerate((own, r1, r2, r3)):
-        ordered[at ^ k] = ref[...]
-    dev0, row0 = join2(ordered[0], ordered[1])
-    dev1, row1 = join2(ordered[2], ordered[3])
-    wide1 = wide(dev1)
-    out[0:W] = chained(dev0, dev1, wide1)
-    out[W:PACK] = moved(row0, wide1) + row1
+    repeated(out, 0, dev, NEAR, PACK)
+    repeated(out, W, row, NEAR, PACK)
+
+
+def split_maps(raw):
+    return [(raw[j * PACK : j * PACK + W], raw[j * PACK + W : (j + 1) * PACK]) for j in range(8)]
+
+
+def joined(first, second):
+    second_wide = wide(second[0])
+    return chained(first[0], second[0], second_wide), moved(first[1], second_wide) + second[1]
+
+
+def eight_kernel(raw, out, early):
+    level = split_maps(raw)
+    pairs = [joined(level[2 * p], level[2 * p + 1]) for p in range(4)]
+    fours = [joined(pairs[0], pairs[1]), joined(pairs[2], pairs[3])]
+    dev, row = joined(*fours)
+    repeated(out, 0, dev, FAR, PACK)
+    repeated(out, W, row, FAR, PACK)
+    for slot, (dev, row) in enumerate((fours[0], pairs[0], pairs[2])):
+        early[slot, 0:W] = dev
+        early[slot, W:PACK] = row
+
+
+def advance(state, at, raw, early):
+    def step(state, used, packed):
+        ahead = moved(state, wide(packed[0:W])) + packed[W : W + 8]
+        return jnp.where(used, ahead, state)
+
+    state = step(state, at >= 4, early[0])
+    state = step(state, (at & 2) != 0, early[1 + (at >> 2)])
+    start = pl.multiple_of((at & 6) * PACK, 8)
+    return step(state, (at & 1) != 0, raw[pl.ds(start, PACK)])
 
 
 def filter_kernel(
-    where, y0, y1, y2, y3, z0, z1, z2, z3, x0, x1, x2, x3, c0, c1,
-    initial, inputs, ends, powers, tree, gain_powers, drive_map, trans,
-    drives, final, shift, ordered,
+    where, far, near, early, c1, initial, inputs, ends, powers, tree, gain_powers, drive_map,
+    trans, drives, final, shift, far_early,
 ):
+    device, core = where[0], where[1]
+    level = split_maps(far)
+    pairs = [joined(level[2 * p], level[2 * p + 1]) for p in range(3)]
+    for slot, (dev, row) in enumerate((joined(pairs[0], pairs[1]), pairs[0], pairs[2])):
+        far_early[slot, 0:W] = dev
+        far_early[slot, W:PACK] = row
     state = jnp.broadcast_to(initial[...], (8, W))
-    for axis, refs in ((0, (y0, y1, y2, y3)), (1, (z0, z1, z2, z3)), (2, (x0, x1, x2, x3)), (3, (c0, c1))):
-        at = where[axis]
-        for k, ref in enumerate(refs):
-            ordered[4 * axis + (at ^ k)] = ref[...]
-        for j in range(len(refs) - 1):
-            slot = 4 * axis + j
-            ahead = moved(state, wide(ordered[slot, 0:W])) + ordered[slot, W:PACK]
-            state = jnp.where(j < at, ahead, state)
+    state = advance(state, device // NEAR, far, far_early)
+    state = advance(state, device % NEAR, near, early)
+    ahead = moved(state, wide(c1[0:W])) + c1[W : W + 8]
+    state = jnp.where(core == 1, ahead, state)
     starts = {0: state}
     for span, maps_at, ends_at in ((8, 12, 28), (4, 8, 24), (2, 0, 16), (1, -1, 0)):
         for begin in range(0, SEGS, 2 * span):
@@ -254,7 +299,7 @@
     last = jnp.broadcast_to(rows[ROWS - 1 : ROWS], (8, W))
     final_row = last + times(wide(last), wide(trans[...].T - identity()))
     final[...] = final_row
-    top = (where[0] == 3) & (where[1] == 3) & (where[2] == 3) & (where[3] == 1)
+    top = (device == NEAR * FAR - 1) & (core == 1)
     part = drive
     for level in (7, 6, 5, 4, 3):
         half = 1 << level
@@ -264,40 +309,24 @@
         behind = pltpu.roll(part, 8 - half, 0)
         part = part + moved(behind, gain_powers[level])
     from_top = moved(final_row, gain_powers[8])
-    shift[...] = jnp.broadcast_to(part[0:1], (8, W)) + jnp.where(top, from_top, 0.0)
-
-
-def gain_kernel(smooth_gain, trans, gain_powers, drive_map):
-    dev = smooth_gain[...].T - identity()
-    adev = trans[...].T - identity()
-    dev_wide = wide(dev)
-    drive_map[...] = wide(-chained(adev, dev, dev_wide))
-    for level in range(15):
-        gain_powers[level] = dev_wide
-        if level < 14:
-            dev = 2.0 * dev + times(dev_wide, dev_wide)
-            dev_wide = wide(dev)
-
-
-def smooth_kernel(where, gathered, drives, final, gain_powers, smoothed, incoming):
+    own = part[0:1] + jnp.where(top, from_top[0:1], 0.0)
+    shift[...] = jnp.broadcast_to(own, (W, W))
+
+
+def smooth_kernel(where, gathered, drives, final, gain_powers, smoothed, incoming, suffix):
     rows = gathered[...]
-    bits = (
-        where[3], where[2] & 1, where[2] >> 1, where[1] & 1, where[1] >> 1, where[0] & 1, where[0] >> 1
-    )
-    later = []
+    place = 2 * where[0] + where[1]
     for level in range(7):
-        dist = 1 << level
-        ahead = moved(rows, gain_powers[8 + level])
-        later.append(rows[dist : dist + 1])
-        other = pltpu.roll(rows, W - dist, 0)
-        other_ahead = pltpu.roll(ahead, W - dist, 0)
-        rows = jnp.where(bits[level] == 0, rows + other_ahead, other + ahead)
+        suffix[level] = rows
+        if level < 6:
+            ahead = moved(rows, gain_powers[8 + level])
+            rows = rows + pltpu.roll(ahead, W - (1 << level), 0)
     state = jnp.zeros((8, W), F32)
-    top = bits[0]
     for level in (6, 5, 4, 3, 2, 1, 0):
-        nxt = moved(state, gain_powers[8 + level]) + later[level]
-        state = jnp.where(bits[level] == 0, nxt, state)
-        top = top & bits[level]
+        sibling = ((place >> level) | 1) << level
+        ahead = moved(state, gain_powers[8 + level]) + suffix[level, pl.ds(sibling, 1)]
+        state = jnp.where(((place >> level) & 1) == 0, ahead, state)
+    top = jnp.where(place == W - 1, 1, 0)
     state = jnp.where(top == 1, final[...], state)
     incoming[...] = state
     entry = moved(state, gain_powers[0])
@@ -311,8 +340,8 @@
     smoothed[...] = part
 
 
-def stats_kernel(where, tel, flags, own, other, smoothed, out0, out1, out2, out3, full, parts):
-    core = where[3]
+def stats_kernel(where, tel, flags, own, other, smoothed, parts, full):
+    core = where[1]
     full[pl.ds(pl.multiple_of(core * ROWS, ROWS), ROWS)] = own[0:ROWS]
     full[pl.ds(pl.multiple_of((1 - core) * ROWS, ROWS), ROWS)] = other[0:ROWS]
     rows = full[...]
@@ -325,7 +354,7 @@
     )
     packed = wide(rows)
     packed_t = jnp.concatenate([rows.T.astype(BF16), (rows - rows.astype(BF16).astype(F32)).T.astype(BF16)], axis=0)
-    last_chip = (where[0] == 3) & (where[1] == 3) & (where[2] == 3)
+    last_chip = where[0] == NEAR * FAR - 1
     lane_at = lax.broadcasted_iota(jnp.int32, (2 * W, count), 1)
     kept = jnp.where(last_chip & (lane_at == count - 1), jnp.zeros_like(packed_t), packed_t)
 
@@ -335,10 +364,6 @@
     upper = lax.broadcasted_iota(jnp.int32, (W, W), 0) - lax.broadcasted_iota(jnp.int32, (W, W), 1)
     lag_gram = fold(jnp.dot(kept, packed, preferred_element_type=F32))
     lag_cross_t = fold(jnp.dot(kept, wide(following), preferred_element_type=F32))
-    lag = jnp.where(jnp.logical_and(upper <= 0, core == 0), lag_gram, lag_cross_t)
-    for j in range(4):
-        parts[j, W : W + SLAB] = lag[j * SLAB : (j + 1) * SLAB]
-        parts[j, W + SLAB :] = jnp.zeros((8, W), F32)
     fl = flags[...]
     repeat = (
         lax.broadcasted_iota(jnp.int32, (2 * SEGS, count), 0)
@@ -351,20 +376,35 @@
     for g in range(4):
         masked_t = packed_t * lane_flags[g : g + 1].astype(BF16)
         grams.append(fold(jnp.dot(masked_t, packed, preferred_element_type=F32)))
+    def diagonal(gram):
+        return jnp.sum(jnp.where(upper == 0, gram, 0.0), axis=0, keepdims=True)
+
     for tile in range(2):
-        parts[tile, 0:W] = jnp.where(upper <= 0, grams[2 * tile], grams[2 * tile + 1])
-        parts[0, W + SLAB + tile : W + SLAB + tile + 1] = jnp.sum(
-            jnp.where(upper == 0, grams[2 * tile + 1], 0.0), axis=0, keepdims=True
-        )
+        parts[tile * W : (tile + 1) * W] = jnp.where(upper <= 0, grams[2 * tile], grams[2 * tile + 1])
+    parts[4 * W : 5 * W] = jnp.where(upper <= 0, lag_gram, lag_cross_t)
+    parts[5 * W : 6 * W] = jnp.where(upper <= 0, lag_cross_t, 0.0)
+    lane = lax.broadcasted_iota(jnp.int32, (1, W), 1)
+    for tile in range(2):
+        line = diagonal(grams[2 * tile + 1])
+        for half in range(2):
+            row = 6 * W - 4 + 2 * tile + half
+            moved_line = line if half == 0 else pltpu.roll(line, W // 2, 1)
+            parts[row : row + 1] = jnp.where(lane < W // 2, moved_line, parts[row : row + 1])
     high, low = halves(tel[...] * mask_of(fl, count, 2 * SEGS))
     cross = jnp.dot(packed_t, high, preferred_element_type=F32) + jnp.dot(
         packed_t, low, preferred_element_type=F32
     )
     cross = cross[:W] + cross[W:]
-    parts[2, 0:W] = cross[:, :W]
-    parts[3, 0:W] = cross[:, W:]
-    for k, out in enumerate((out0, out1, out2, out3)):
-        out[...] = parts[where[2] ^ k]
+    parts[2 * W : 3 * W] = cross[:, :W]
+    parts[3 * W : 4 * W] = cross[:, W:]
+
+def sum_kernel(count, copies, parts, out):
+    rows = SLICE
+    total = parts[0:rows]
+    for j in range(1, count):
+        total = total + parts[j * rows : (j + 1) * rows]
+    for j in range(copies):
+        out[j * rows : (j + 1) * rows] = total
 
 
 def inverses(matrices):
@@ -397,21 +437,13 @@
     return jnp.dot(left, right, precision=lax.Precision.HIGHEST, preferred_element_type=F32)
 
 
-def solve_kernel(ridge, where, own, r1, r2, r3, new_transition, new_sensing, parts):
-    at = where[2]
-    core = where[3]
-    for k, ref in enumerate((own, r1, r2, r3)):
-        parts[at ^ k] = ref[...]
+def solve_kernel(ridge, stats, new_transition, new_sensing):
     rows = lax.broadcasted_iota(jnp.int32, (W, W), 0)
     lanes = lax.broadcasted_iota(jnp.int32, (W, W), 1)
     eye = jnp.where(rows == lanes, ridge, 0.0).astype(F32)
-    slabs = [parts[j, W : W + SLAB] for j in range(4)]
-    far = [parts[j, W + SLAB + 8 :] for j in range(4)]
-    lag_here = jnp.concatenate(slabs, axis=0)
-    lag_far = jnp.concatenate(far, axis=0)
-    lag_a = jnp.where(core == 0, lag_here, lag_far)
-    lag_b = jnp.where(core == 0, lag_far, lag_here)
-
+    lag_a = stats[4 * W : 5 * W]
+    lag_b = stats[5 * W : 6 * W]
+    half = lax.broadcasted_iota(jnp.int32, (1, W), 1) < W // 2
     def upper(tile):
         return jnp.where(rows <= lanes, tile, 0.0) + jnp.where(rows < lanes, tile, 0.0).T
 
@@ -421,105 +453,91 @@
 
     grams = [upper(lag_a)]
     for tile in range(2):
-        grams.append(upper(parts[tile, 0:W]))
-        grams.append(lower(parts[tile, 0:W], parts[0, W + SLAB + tile : W + SLAB + tile + 1]))
+        packed = stats[tile * W : (tile + 1) * W]
+        row = 6 * W - 4 + 2 * tile
+        line = jnp.where(half, stats[row : row + 1], pltpu.roll(stats[row + 1 : row + 2], W // 2, 1))
+        grams.append(upper(packed))
+        grams.append(lower(packed, line))
     done = inverses([gram + eye for gram in grams])
     lag_cross_t = jnp.where(rows > lanes, lag_a, lag_b)
     new_transition[...] = exact(lag_cross_t.T, done[0])
     for tile in range(2):
-        cross = parts[2 + tile, 0:W].T
-        for half in range(2):
-            g = 2 * tile + half
-            new_sensing[g * 64 : (g + 1) * 64] = exact(cross[half * 64 : (half + 1) * 64], done[1 + g])
-
-
-STRIDE = {"x": 1, "z": 4, "y": 16}
-
-
-def swap(value, axis, k):
-    stride = STRIDE[axis]
-    pairs = []
-    for i in range(64):
-        at = (i // stride) % 4
-        pairs.append((i, i + ((at ^ k) - at) * stride))
-    return lax.ppermute(value, "tm", pairs)
+        cross = stats[(2 + tile) * W : (3 + tile) * W].T
+        for side in range(2):
+            g = 2 * tile + side
+            new_sensing[g * 64 : (g + 1) * 64] = exact(cross[side * 64 : (side + 1) * 64], done[1 + g])
 
 
 def swap_core(value):
     return lax.ppermute(value, "sens", [(0, 1), (1, 0)])
 
 
-def three(value, axis):
-    return [swap(value, axis, k) for k in (1, 2, 3)]
+def exchange(value, stride, count):
+    groups = [
+        [first + stride * j for j in range(count)]
+        for first in range(NEAR * FAR)
+        if (first // stride) % count == 0
+    ]
+    return lax.all_to_all(value, "tm", 0, 0, axis_index_groups=groups, tiled=True)
 
 
 def on_device(telemetry, present, transition, sensing, filter_gain, smooth_gain, initial_state):
-    device = lax.axis_index("tm")
-    core = lax.axis_index("sens")
-    at_y, at_z, at_x = device // 16, (device // 4) % 4, device % 4
-    where = jnp.stack([at_y, at_z, at_x, core]).astype(jnp.int32)
+    where = jnp.stack([lax.axis_index("tm"), lax.axis_index("sens")]).astype(jnp.int32)
     flags = present.astype(F32)
 
     other_gain = swap_core(filter_gain)
     other_sensing = swap_core(sensing)
     other_flags = swap_core(flags)
-    mine, theirs = call(push_kernel, [shape(ROWS, W)] * 2, 1, 3)(where, telemetry, flags, filter_gain)
+    mine, theirs = call(push_kernel, [shape(ROWS, W)] * 2, 1, 3, far=(0, 2))(
+        where, telemetry, flags, filter_gain
+    )
     received = swap_core(theirs)
-    powers, tree, whole = call(
+    powers, tree, whole, gain_powers, drive_map = call(
         maps_kernel,
-        [shape(SEGS, 5, W, 2 * W, dtype=BF16), shape(SEGS - 1, W, 2 * W, dtype=BF16), shape(2 * SEGS - 1, W, W)],
-        3, 5,
+        [
+            shape(SEGS, 5, W, 2 * W, dtype=BF16), shape(SEGS - 1, W, 2 * W, dtype=BF16),
+            shape(2 * SEGS - 1, W, W), shape(15, W, 2 * W, dtype=BF16), shape(W, 2 * W, dtype=BF16),
+        ],
+        3, 6,
         scratch=[pltpu.VMEM((8, W, W), F32), pltpu.VMEM((W, W), F32)],
-    )(where, flags, other_flags, transition, filter_gain, other_gain, sensing, other_sensing)
+        far=(0, 1, 3, 5),
+    )(where, flags, other_flags, transition, filter_gain, other_gain, sensing, other_sensing, smooth_gain)
     inputs, ends, packed = call(
         shift_kernel, [shape(ROWS, W), shape(32, W), shape(PACK, W)], 0, 5
     )(mine, received, powers, tree, whole)
 
-    gain_powers, drive_map = call(
-        gain_kernel, [shape(15, W, 2 * W, dtype=BF16), shape(W, 2 * W, dtype=BF16)], 0, 2
-    )(smooth_gain, transition)
-
-    by_core = [packed, swap_core(packed)]
-    (chip,) = call(pair_kernel, [shape(PACK, W)], 1, 2)(where, *by_core)
-    ordered = [pltpu.VMEM((4, PACK, W), F32)]
-    by_x = [chip] + three(chip, "x")
-    (row,) = call(functools.partial(four_kernel, 2), [shape(PACK, W)], 1, 4, ordered)(where, *by_x)
-    by_z = [row] + three(row, "z")
-    (plane,) = call(functools.partial(four_kernel, 1), [shape(PACK, W)], 1, 4, ordered)(where, *by_z)
-    by_y = [plane] + three(plane, "y")
-
+    other_packed = swap_core(packed)
+    (chip,) = call(pair_kernel, [shape(NEAR * PACK, W)], 1, 2)(where, packed, other_packed)
+    near = exchange(chip, 1, NEAR)
+    group, early = call(eight_kernel, [shape(FAR * PACK, W), shape(3, PACK, W)], 0, 1)(near)
+    far = exchange(group, NEAR, FAR)
     drives, final, shift = call(
-        filter_kernel, [shape(ROWS, W), shape(8, W), shape(8, W)], 1, 14 + 8,
-        [pltpu.VMEM((16, PACK, W), F32)],
+        filter_kernel, [shape(ROWS, W), shape(8, W), shape(W, W)], 1, 12,
+        [pltpu.VMEM((3, PACK, W), F32)],
     )(
-        where, *by_y, *by_z, *by_x, *by_core, initial_state.reshape(1, W), inputs, ends, powers, tree,
+        where, far, near, early, other_packed, initial_state.reshape(1, W), inputs, ends, powers, tree,
         gain_powers, drive_map, transition,
     )
-    gathered = shift[:1]
-    gathered = jnp.concatenate([gathered, swap_core(gathered)], axis=0)
-    for axis in ("x", "z", "y"):
-        gathered = jnp.concatenate([gathered] + three(gathered, axis), axis=0)
-    smoothed, incoming = call(smooth_kernel, [shape(ROWS, W), shape(8, W)], 1, 4)(
-        where, gathered, drives, final, gain_powers
-    )
+    gathered = lax.all_to_all(shift, ("tm", "sens"), 0, 0, tiled=True)
+    smoothed, incoming = call(
+        smooth_kernel, [shape(ROWS, W), shape(8, W)], 1, 4, [pltpu.VMEM((7, W, W), F32)]
+    )(where, gathered, drives, final, gain_powers)
     both = jnp.concatenate([smoothed, incoming], axis=0)
     other_both = swap_core(both)
-    smoothed_out, *chunks = call(
-        stats_kernel, [shape(2 * ROWS, W, leaves=True)] + [shape(CHUNK, W)] * 4, 1, 4,
-        [pltpu.VMEM((2 * ROWS, W), F32), pltpu.VMEM((4, CHUNK, W), F32)],
+    smoothed_out, stats = call(
+        stats_kernel, [shape(2 * ROWS, W, leaves=True), shape(STATS, W)], 1, 4,
+        [pltpu.VMEM((2 * ROWS, W), F32)],
     )(where, telemetry, flags, both, other_both)
 
-    got = [swap(chunks[k], "x", k) for k in (1, 2, 3)]
-    part = (chunks[0] + got[0]) + (got[1] + got[2])
-    for axis in ("z", "y"):
-        got = three(part, axis)
-        part = (part + got[0]) + (got[1] + got[2])
-    part = jnp.concatenate([part, swap_core(part[W : W + SLAB])], axis=0)
+    stats = exchange(stats, 1, PLANE)
+    (stats,) = call(functools.partial(sum_kernel, PLANE, PLANES), [shape(PLANES * SLICE, W)], 0, 1)(stats)
+    stats = exchange(stats, PLANE, PLANES)
+    (stats,) = call(functools.partial(sum_kernel, PLANES, PLANE), [shape(STATS, W)], 0, 1)(stats)
+    stats = exchange(stats, 1, PLANE)
     ridge = RIDGE * telemetry.shape[0] * lax.axis_size("tm")
     new_transition, new_sensing = call(
-        functools.partial(solve_kernel, ridge), [shape(W, W, leaves=True), shape(2 * W, W, leaves=True)], 1, 4,
-        [pltpu.VMEM((4, CHUNK + SLAB, W), F32)],
-    )(where, part, *three(part, "x"))
+        functools.partial(solve_kernel, ridge), [shape(W, W, leaves=True), shape(2 * W, W, leaves=True)], 0, 1
+    )(stats)
     return new_transition, new_sensing, smoothed_out
 
 

time: 144 us -> 130 us (0.903)
  blocking collectives: 0 us -> 83.2 us
  starting transfers between devices: 50.3 us -> 1.78 us
  waiting for transfers between devices: 44.9 us -> 3.14 us
  local copies, waits for them, and re-layouts: 5.46 us -> 0.79 us
    all_to_all x0 -> x6, blocking collectives: none -> 83.2 us  [the longest x5 69.9 us: exchange(): lax.all_to_all(value, 'tm', 0, 0, axis_index_groups=groups, tiled=True)]
    ppermute x30 -> x0, starting transfers between devices: 48.6 us -> none  [swap(): return lax.ppermute(value, 'tm', pairs)]
    ppermute x30 -> x0, waiting for transfers between devices: 39.5 us -> none  [swap(): return lax.ppermute(value, 'tm', pairs)]
    unnamed x20 -> x8, local copies, waits for them, and re-layouts: 5.38 us -> 0.79 us
    ppermute x8 -> x6, waiting for transfers between devices: 5.42 us -> 3.14 us  [swap_core(): return lax.ppermute(value, 'sens', [(0, 1), (1, 0)])]
  transfers between devices with their start and end apart: 38 -> 6, of which waited for: 30 -> 3; matrix products, arithmetic and copies ran while one was open for 1% -> 1% of each run, Pallas kernels for 7% -> 8%
where the time goes in v4:
time: 130 us
  blocking collectives  83.2 us (64%)
  Pallas kernels  39.9 us (31%)
  waiting for transfers between devices  3.14 us (2%)
  starting transfers between devices  1.78 us (1%)
    all_to_all x5, blocking collectives, exchange(): lax.all_to_all(value, 'tm', 0, 0, axis_index_groups=groups, tiled=True)  69.9 us
    pallas_call x11, Pallas kernels, placed(): return run(*operands[:n_smem], *near)  39.9 us
    all_to_all x1, blocking collectives, on_device(): gathered = lax.all_to_all(shift, ('tm', 'sens'), 0, 0, tiled=True)  13.3 us
    ppermute x6, waiting for transfers between devices, swap_core(): return lax.ppermute(value, 'sens', [(0, 1), (1, 0)])  3.14 us
  transfers between devices with their start and end apart: 6, of which 3 were waited for; matrix products, arithmetic and copies ran while one was open for 1% of the time, Pallas kernels for 8%

profile of v4, /device:TPU:0, one launch (start us, length us, event | category | flops | bytes accessed | tf_op | source)
XLA Modules:
  0.0 129.6 jit_solution(549149064607558216)
XLA Ops:
  0.6 0.1 collective-permute-start.2
  0.7 0.5 collective-permute-start.3
  1.2 0.1 pad_add_fusion.where
  1.3 0.8 copy.11
  2.1 1.6 %shard_map.94 = (f32[256,128]{1,0:T(8,128)S(1)}, f32[256,128]{1,0:T(8,128)S(1)}) custom-call(s32[2]{0:T(128)S(1)} %pad_add_fusion.where, f32[512,256]{1,0:T(8,128)} %tel.3, f32[32,4]{1,0:T(8,128)S(1)} %convert_element_type.3.flags.flags_own, f32[128,256]{1,0:T(8,128)} %gain_own.1), custom_call_target="tpu_custom_call" | custom-call | tf_op jit(solution)/shard_map/pallas_call | solution.py:76
  3.7 0.2 collective-permute-start
  3.8 0.4 collective-permute-start.1
  4.3 0.9 collective-permute-done.1.flags_other
  5.1 0.0 collective-permute-done.2.gain_other
  5.1 0.0 collective-permute-done.3.sense_other
  5.1 9.1 %shard_map.95 = (bf16[16,5,128,256]{3,2,1,0:T(8,128)(2,1)S(1)}, bf16[15,128,256]{2,1,0:T(8,128)(2,1)S(1)}, f32[31,128,128]{2,1,0:T(8,128)S(1)}, bf16[15,128,256]{2,1,0:T(8,128)(2,1)S(1)}, bf16[128,256]{1,0:T(8,128)(2,1)S(1)}) custom-call(s32[2]{0:T(128)S(1)} %pad_add_fusion.where, f32[32,4]{1,0:T(8,128)S(1)} %convert_element_type.3.flags.flags_own, ...), custom_call_target="tpu_custom_call" | custom-call | tf_op jit(solution)/shard_map/pallas_call | solution.py:76
  14.2 0.0 collective-permute-done.received
  14.2 0.0 copy-start.1
  14.2 0.0 copy-start.2
  14.2 1.7 %shard_map.96 = (f32[256,128]{1,0:T(8,128)S(1)}, f32[32,128]{1,0:T(8,128)S(1)}, f32[136,128]{1,0:T(8,128)S(1)}) custom-call(f32[256,128]{1,0:T(8,128)S(1)} %get-tuple-element.24.mine, f32[256,128]{1,0:T(8,128)S(1)} %collective-permute-done.received, bf16[16,5,128,256]{3,2,1,0:T(8,128)(2,1)S(1)} %get-tuple-element.26.powers, ...), custom_call_target="tpu_custom_call" | custom-call | tf_op jit(solution)/shard_map/pallas_call | solution.py:76
  15.9 0.3 collective-permute-start.4
  16.3 0.9 collective-permute-done.4.other.c1
  17.2 0.7 shard_map.97
  18.0 16.7 %all_to_all.66 = f32[8,136,128]{2,1,0:T(8,128)S(1)} all-to-all(f32[8,136,128]{2,1,0:T(8,128)S(1)} %bitcast.20), channel_id=1, replica_groups={{0,2,4,6,8,10,12,14},{16,18,20,22,24,26,28,30},{32,34,36,38,40,42,44,46..., dimensions={0} | all-to-all | bytes 1114112 | tf_op jit(solution)/shard_map/all_to_all | solution.py:481
  34.6 0.7 shard_map.98
  35.3 19.0 %all_to_all.67 = f32[8,136,128]{2,1,0:T(8,128)S(1)} all-to-all(f32[8,136,128]{2,1,0:T(8,128)S(1)} %bitcast.24), channel_id=1, replica_groups={{0,16,32,48,64,80,96,112},{2,18,34,50,66,82,98,114},{4,20,36,52,68,84,1..., dimensions={0} | all-to-all | bytes 1114112 | tf_op jit(solution)/shard_map/all_to_all | solution.py:481
  54.3 0.0 copy-start
  54.3 0.0 copy-done.1
  54.3 0.0 copy-done.2
  54.3 4.9 %shard_map.99 = (f32[256,128]{1,0:T(8,128)S(1)}, f32[8,128]{1,0:T(8,128)S(1)}, f32[128,128]{1,0:T(8,128)S(1)}) custom-call(s32[2]{0:T(128)S(1)} %pad_add_fusion.where, f32[1088,128]{1,0:T(8,128)S(1)} %bitcast.19, f32[1088,128]{1,0:T(8,128)S(1)} %bitcast.18, f32[3,136,128]{2,1,0:T(8,128)S(1)} %get-tuple-element.31.early, ...), custom_call_target="tpu_custom_call" | custom-call | tf_op jit(solution)/shard_map/pallas_call | solution.py:76
  59.2 13.3 %all_to_all.68 = f32[128,1,128]{2,1,0:T(1,128)S(1)} all-to-all(f32[128,1,128]{2,1,0:T(1,128)S(1)} %bitcast.29), channel_id=1, replica_groups=mesh['tm'=64,'sens'=2] {'tm','sens'}, dimensions={0} | all-to-all | bytes 131072 | tf_op jit(solution)/shard_map/all_to_all | solution.py:521
  72.4 3.3 %shard_map.100 = (f32[256,128]{1,0:T(8,128)S(1)}, f32[8,128]{1,0:T(8,128)S(1)}) custom-call(s32[2]{0:T(128)S(1)} %pad_add_fusion.where, f32[128,128]{1,0:T(8,128)S(1)} %bitcast.28, f32[256,128]{1,0:T(8,128)S(1)} %get-tuple-element.37.drives, f32[8,128]{1,0:T(8,128)S(1)} %get-tuple-element.38.final, bf16[15,128,256]{2,1,0:T(8,128)(2,1)S(1)} %get-tuple-element.34.gain_powers), custom_call_target="tpu_custom_call" | custom-call | tf_op jit(solution)/shard_map/pallas_call | solution.py:76
  75.8 0.3 collective-permute-start.5
  76.0 1.3 %collective-permute-done.5.other = f32[264,128]{1,0:T(8,128)S(1)} collective-permute-done((f32[264,128]{1,0:T(8,128)S(1)}, f32[264,128]{1,0:T(8,128)S(1)}, u32[]{:S(2)}, u32[]{:S(2)}) %collective-permute-start.5) | collective-permute-done | bytes 135200 | tf_op jit(solution)/shard_map/ppermute | solution.py:472
  77.4 0.0 copy-done
  77.4 2.3 %shard_map.101 = (f32[512,128]{1,0:T(8,128)}, f32[768,128]{1,0:T(8,128)S(1)}) custom-call(s32[2]{0:T(128)S(1)} %pad_add_fusion.where, f32[512,256]{1,0:T(8,128)S(1)} %copy-done, f32[32,4]{1,0:T(8,128)S(1)} %convert_element_type.3.flags.flags_own, f32[264,128]{1,0:T(8,128)S(1)} %constant_dynamic-update-slice_fusion.own, ...), custom_call_target="tpu_custom_call" | custom-call | tf_op jit(solution)/shard_map/pallas_call | solution.py:76
  79.7 13.8 %all_to_all.69 = f32[16,48,128]{2,1,0:T(8,128)S(1)} all-to-all(f32[16,48,128]{2,1,0:T(8,128)S(1)} %bitcast.25), channel_id=1, replica_groups={{0,2,4,6,8,10,12,14,16,18,20,22,24,26,28,30},{32,34,36,38,40,42,44,46,4..., dimensions={0} | all-to-all | bytes 786432 | tf_op jit(solution)/shard_map/all_to_all | solution.py:481
  93.6 8.2 %all_to_all.70 = f32[4,48,128]{2,1,0:T(8,128)S(1)} all-to-all(f32[4,48,128]{2,1,0:T(8,128)S(1)} %bitcast.26), channel_id=1, replica_groups={{0,32,64,96},{2,34,66,98},{4,36,68,100},{6,38,70,102},{8,40,72,104},{10..., dimensions={0} | all-to-all | bytes 196608 | tf_op jit(solution)/shard_map/all_to_all | solution.py:481
  101.8 12.3 %all_to_all.71 = f32[16,48,128]{2,1,0:T(8,128)S(1)} all-to-all(f32[16,48,128]{2,1,0:T(8,128)S(1)} %bitcast.23), channel_id=1, replica_groups={{0,2,4,6,8,10,12,14,16,18,20,22,24,26,28,30},{32,34,36,38,40,42,44,46,4..., dimensions={0} | all-to-all | bytes 786432 | tf_op jit(solution)/shard_map/all_to_all | solution.py:481
  114.1 15.5 %shard_map.104 = (f32[128,128]{1,0:T(8,128)}, f32[256,128]{1,0:T(8,128)}) custom-call(f32[768,128]{1,0:T(8,128)S(1)} %bitcast.21), custom_call_target="tpu_custom_call" | custom-call | tf_op jit(solution)/shard_map/pallas_call | solution.py:76
  (5 shorter events, 0.1 us)
Async XLA Ops:
  0.6 4.5 %collective-permute-start.2 = (f32[128,256]{1,0:T(8,128)}, f32[128,256]{1,0:T(8,128)S(1)}, u32[]{:S(2)}, u32[]{:S(2)}) collective-permute-start(f32[128,256]{1,0:T(8,128)} %gain_own.1), channel_id=1, source_target_pairs={{0,1},{1,0},{2,3},{3,2},{4,5},{5,4},{6,7},{7,6},{8,9},{9,8},{10,11... | collective-permute-start | bytes 393224 | tf_op jit(solution)/shard_map/ppermute | solution.py:472
  0.7 4.4 %collective-permute-start.3 = (f32[256,128]{1,0:T(8,128)}, f32[256,128]{1,0:T(8,128)S(1)}, u32[]{:S(2)}, u32[]{:S(2)}) collective-permute-start(f32[256,128]{1,0:T(8,128)} %sense_own.1), channel_id=1, source_target_pairs={{0,1},{1,0},{2,3},{3,2},{4,5},{5,4},{6,7},{7,6},{8,9},{9,8},{10,11... | collective-permute-start | bytes 393224 | tf_op jit(solution)/shard_map/ppermute | solution.py:472
  3.7 10.5 %collective-permute-start = (f32[256,128]{1,0:T(8,128)S(1)}, f32[256,128]{1,0:T(8,128)S(1)}, u32[]{:S(2)}, u32[]{:S(2)}) collective-permute-start(f32[256,128]{1,0:T(8,128)S(1)} %get-tuple-element.25), channel_id=1, source_target_pairs={{0,1},{1,0},{2,3},{3,2},{4,5},{5,4},{6,7},{7,6},{8,9},{9,8},{10,11... | collective-permute-start | bytes 393224 | tf_op jit(solution)/shard_map/ppermute | solution.py:472
  3.8 1.3 collective-permute-start.1
  14.2 40.1 %copy-start.1 = (f32[128,128]{1,0:T(8,128)S(1)}, f32[128,128]{1,0:T(8,128)}, u32[]{:S(2)}) copy-start(f32[128,128]{1,0:T(8,128)} %trans.3) | copy-start | bytes 196612
  14.2 40.1 %copy-start.2 = (f32[128]{0:T(128)S(1)}, f32[128]{0:T(128)}, u32[]{:S(2)}) copy-start(f32[128]{0:T(128)} %param.13) | copy-start | bytes 1540
  15.9 1.3 collective-permute-start.4
  54.3 23.1 %copy-start = (f32[512,256]{1,0:T(8,128)S(1)}, f32[512,256]{1,0:T(8,128)}, u32[]{:S(2)}) copy-start(f32[512,256]{1,0:T(8,128)} %tel.3) | copy-start | bytes 1572868
  75.8 1.6 %collective-permute-start.5 = (f32[264,128]{1,0:T(8,128)S(1)}, f32[264,128]{1,0:T(8,128)S(1)}, u32[]{:S(2)}, u32[]{:S(2)}) collective-permute-start(f32[264,128]{1,0:T(8,128)S(1)} %constant_dynamic-update-slice_fusion.own), channel_id=1, source_target_pairs={{0,1},{1,0},{2,3},{3,2},{4,5},{5,4},{6,7},{7,6},{8,9},{9,8},{10,11... | collective-permute-start | bytes 405512 | tf_op jit(solution)/shard_map/ppermute | solution.py:472

commit v5 on v4

--- a/solution.py
+++ b/solution.py
@@ -407,34 +407,79 @@
         out[j * rows : (j + 1) * rows] = total
 
 
+def exact(left, right):
+    return jnp.dot(left, right, precision=lax.Precision.HIGHEST, preferred_element_type=F32)
+
+
+def sweep(entry, count):
+    entry = [list(row) for row in entry]
+    for q in range(count):
+        scale = 1.0 / entry[q][q]
+        row = [entry[q][c] * scale for c in range(count)]
+        for r in range(count):
+            for c in range(r, count):
+                if q not in (r, c):
+                    entry[r][c] = entry[r][c] - entry[r][q] * row[c]
+        for r in range(count):
+            entry[r][q] = entry[q][r] = row[r]
+        entry[q][q] = -scale
+        for r in range(count):
+            for c in range(r):
+                entry[r][c] = entry[c][r]
+    return entry
+
+
 def inverses(matrices):
-    unit = 8
+    unit, pivots = 32, 8
     lane = lax.broadcasted_iota(jnp.int32, (W, W), 1)
+    lane_tile = lane[:8]
     lane_head = lane[:unit]
     row_head = lax.broadcasted_iota(jnp.int32, (unit, W), 0)
-
-    def block(b, held):
+    sublane = lax.broadcasted_iota(jnp.int32, (8, W), 0)
+
+    def panel(b, held):
         heads = [m[:unit] for m in held]
-        rests = [m[unit:] for m in held]
-        for j in range(unit):
-            for p in range(len(held)):
-                head, rest = heads[p], rests[p]
-                row = head[j : j + 1]
-                scale = 1.0 / row[:, j : j + 1]
-                row = jnp.where(lane_head[:1] == j, scale, row * scale)
-                head_next = jnp.where(lane_head == j, 0.0, head) - head[:, j : j + 1] * row
-                heads[p] = jnp.where(row_head == j, row, head_next)
-                rests[p] = jnp.where(lane[unit:] == j, 0.0, rest) - rest[:, j : j + 1] * row
-        return tuple(
-            pltpu.roll(jnp.concatenate([rest, head], axis=0), W - unit, 1)
-            for head, rest in zip(heads, rests)
-        )
-
-    return lax.fori_loop(0, W // unit, block, tuple(matrices))
-
-
-def exact(left, right):
-    return jnp.dot(left, right, precision=lax.Precision.HIGHEST, preferred_element_type=F32)
+        for j in range(0, unit, pivots):
+            stacked = []
+            for r in range(pivots):
+                rows = jnp.broadcast_to(heads[0][j + r : j + r + 1], (8, W))
+                for p in range(1, len(heads)):
+                    mine = jnp.broadcast_to(heads[p][j + r : j + r + 1], (8, W))
+                    rows = jnp.where(sublane == p, mine, rows)
+                stacked.append(rows)
+            entry = [[None] * pivots for _ in range(pivots)]
+            for r in range(pivots):
+                for c in range(r, pivots):
+                    value = jnp.broadcast_to(stacked[r][:, j + c : j + c + 1], (8, W))
+                    entry[r][c] = entry[c][r] = value
+            entry = sweep(entry, pivots)
+            fresh = []
+            for r in range(pivots):
+                total = entry[r][0] * stacked[0]
+                for c in range(1, pivots):
+                    total = total + entry[r][c] * stacked[c]
+                for c in range(pivots):
+                    total = jnp.where(lane_tile == j + c, entry[r][c], total)
+                fresh.append(-total)
+            for p, head in enumerate(heads):
+                rows = [
+                    jnp.concatenate([jnp.broadcast_to(row[p : p + 1], (8, W))] * (unit // 8), axis=0)
+                    for row in fresh
+                ]
+                after = jnp.where(lane_head // pivots == j // pivots, 0.0, head)
+                for r in range(pivots):
+                    after = after - jnp.broadcast_to(head[:, j + r : j + r + 1], (unit, W)) * rows[r]
+                for r in range(pivots):
+                    after = jnp.where(row_head == j + r, rows[r], after)
+                heads[p] = after
+        turned = []
+        for head, m in zip(heads, held):
+            rest = m[unit:]
+            rest = jnp.where(lane[unit:] < unit, 0.0, rest) - exact(rest[:, :unit], head)
+            turned.append(pltpu.roll(jnp.concatenate([rest, head], axis=0), W - unit, 1))
+        return tuple(turned)
+
+    return lax.fori_loop(0, W // unit, panel, tuple(matrices))
 
 
 def solve_kernel(ridge, stats, new_transition, new_sensing):

time: 130 us -> 123 us (0.946)
  Pallas kernels: 39.9 us -> 33.1 us
    pallas_call x11, Pallas kernels: 39.9 us -> 33.1 us  [placed(): return run(*operands[:n_smem], *near)]
  transfers between devices with their start and end apart: 6 -> 6, of which waited for: 3 -> 3; matrix products, arithmetic and copies ran while one was open for 1% -> 1% of each run, Pallas kernels for 8% -> 9%
where the time goes in v5:
time: 123 us
  blocking collectives  83.2 us (68%)
  Pallas kernels  33.1 us (27%)
  waiting for transfers between devices  3.14 us (3%)
  starting transfers between devices  1.78 us (1%)
    all_to_all x5, blocking collectives, exchange(): lax.all_to_all(value, 'tm', 0, 0, axis_index_groups=groups, tiled=True)  69.9 us
    pallas_call x11, Pallas kernels, placed(): return run(*operands[:n_smem], *near)  33.1 us
    all_to_all x1, blocking collectives, on_device(): gathered = lax.all_to_all(shift, ('tm', 'sens'), 0, 0, tiled=True)  13.3 us
    ppermute x6, waiting for transfers between devices, swap_core(): return lax.ppermute(value, 'sens', [(0, 1), (1, 0)])  3.14 us
  transfers between devices with their start and end apart: 6, of which 3 were waited for; matrix products, arithmetic and copies ran while one was open for 1% of the time, Pallas kernels for 9%

profile of v5, /device:TPU:0, one launch (start us, length us, event | category | flops | bytes accessed | tf_op | source)
XLA Modules:
  0.0 122.8 jit_solution(11470279047768064341)
XLA Ops:
  0.6 0.1 collective-permute-start.2
  0.7 0.5 collective-permute-start.3
  1.2 0.1 pad_add_fusion.where
  1.3 0.8 copy.11
  2.1 1.6 %shard_map.94 = (f32[256,128]{1,0:T(8,128)S(1)}, f32[256,128]{1,0:T(8,128)S(1)}) custom-call(s32[2]{0:T(128)S(1)} %pad_add_fusion.where, f32[512,256]{1,0:T(8,128)} %tel.3, f32[32,4]{1,0:T(8,128)S(1)} %convert_element_type.3.flags.flags_own, f32[128,256]{1,0:T(8,128)} %gain_own.1), custom_call_target="tpu_custom_call" | custom-call | tf_op jit(solution)/shard_map/pallas_call | solution.py:76
  3.7 0.2 collective-permute-start
  3.8 0.4 collective-permute-start.1
  4.3 0.9 collective-permute-done.1.flags_other
  5.1 0.0 collective-permute-done.2.gain_other
  5.1 0.0 collective-permute-done.3.sense_other
  5.1 9.1 %shard_map.95 = (bf16[16,5,128,256]{3,2,1,0:T(8,128)(2,1)S(1)}, bf16[15,128,256]{2,1,0:T(8,128)(2,1)S(1)}, f32[31,128,128]{2,1,0:T(8,128)S(1)}, bf16[15,128,256]{2,1,0:T(8,128)(2,1)S(1)}, bf16[128,256]{1,0:T(8,128)(2,1)S(1)}) custom-call(s32[2]{0:T(128)S(1)} %pad_add_fusion.where, f32[32,4]{1,0:T(8,128)S(1)} %convert_element_type.3.flags.flags_own, ...), custom_call_target="tpu_custom_call" | custom-call | tf_op jit(solution)/shard_map/pallas_call | solution.py:76
  14.2 0.0 collective-permute-done.received
  14.2 0.0 copy-start.1
  14.2 0.0 copy-start.2
  14.2 1.7 %shard_map.96 = (f32[256,128]{1,0:T(8,128)S(1)}, f32[32,128]{1,0:T(8,128)S(1)}, f32[136,128]{1,0:T(8,128)S(1)}) custom-call(f32[256,128]{1,0:T(8,128)S(1)} %get-tuple-element.24.mine, f32[256,128]{1,0:T(8,128)S(1)} %collective-permute-done.received, bf16[16,5,128,256]{3,2,1,0:T(8,128)(2,1)S(1)} %get-tuple-element.26.powers, ...), custom_call_target="tpu_custom_call" | custom-call | tf_op jit(solution)/shard_map/pallas_call | solution.py:76
  15.9 0.3 collective-permute-start.4
  16.3 0.9 collective-permute-done.4.other.c1
  17.2 0.7 shard_map.97
  18.0 16.7 %all_to_all.66 = f32[8,136,128]{2,1,0:T(8,128)S(1)} all-to-all(f32[8,136,128]{2,1,0:T(8,128)S(1)} %bitcast.20), channel_id=1, replica_groups={{0,2,4,6,8,10,12,14},{16,18,20,22,24,26,28,30},{32,34,36,38,40,42,44,46..., dimensions={0} | all-to-all | bytes 1114112 | tf_op jit(solution)/shard_map/all_to_all | solution.py:526
  34.6 0.7 shard_map.98
  35.3 19.0 %all_to_all.67 = f32[8,136,128]{2,1,0:T(8,128)S(1)} all-to-all(f32[8,136,128]{2,1,0:T(8,128)S(1)} %bitcast.24), channel_id=1, replica_groups={{0,16,32,48,64,80,96,112},{2,18,34,50,66,82,98,114},{4,20,36,52,68,84,1..., dimensions={0} | all-to-all | bytes 1114112 | tf_op jit(solution)/shard_map/all_to_all | solution.py:526
  54.3 0.0 copy-start
  54.3 0.0 copy-done.1
  54.3 0.0 copy-done.2
  54.3 4.9 %shard_map.99 = (f32[256,128]{1,0:T(8,128)S(1)}, f32[8,128]{1,0:T(8,128)S(1)}, f32[128,128]{1,0:T(8,128)S(1)}) custom-call(s32[2]{0:T(128)S(1)} %pad_add_fusion.where, f32[1088,128]{1,0:T(8,128)S(1)} %bitcast.19, f32[1088,128]{1,0:T(8,128)S(1)} %bitcast.18, f32[3,136,128]{2,1,0:T(8,128)S(1)} %get-tuple-element.31.early, ...), custom_call_target="tpu_custom_call" | custom-call | tf_op jit(solution)/shard_map/pallas_call | solution.py:76
  59.2 13.3 %all_to_all.68 = f32[128,1,128]{2,1,0:T(1,128)S(1)} all-to-all(f32[128,1,128]{2,1,0:T(1,128)S(1)} %bitcast.29), channel_id=1, replica_groups=mesh['tm'=64,'sens'=2] {'tm','sens'}, dimensions={0} | all-to-all | bytes 131072 | tf_op jit(solution)/shard_map/all_to_all | solution.py:566
  72.4 3.3 %shard_map.100 = (f32[256,128]{1,0:T(8,128)S(1)}, f32[8,128]{1,0:T(8,128)S(1)}) custom-call(s32[2]{0:T(128)S(1)} %pad_add_fusion.where, f32[128,128]{1,0:T(8,128)S(1)} %bitcast.28, f32[256,128]{1,0:T(8,128)S(1)} %get-tuple-element.37.drives, f32[8,128]{1,0:T(8,128)S(1)} %get-tuple-element.38.final, bf16[15,128,256]{2,1,0:T(8,128)(2,1)S(1)} %get-tuple-element.34.gain_powers), custom_call_target="tpu_custom_call" | custom-call | tf_op jit(solution)/shard_map/pallas_call | solution.py:76
  75.8 0.3 collective-permute-start.5
  76.0 1.3 %collective-permute-done.5.other = f32[264,128]{1,0:T(8,128)S(1)} collective-permute-done((f32[264,128]{1,0:T(8,128)S(1)}, f32[264,128]{1,0:T(8,128)S(1)}, u32[]{:S(2)}, u32[]{:S(2)}) %collective-permute-start.5) | collective-permute-done | bytes 135200 | tf_op jit(solution)/shard_map/ppermute | solution.py:517
  77.4 0.0 copy-done
  77.4 2.3 %shard_map.101 = (f32[512,128]{1,0:T(8,128)}, f32[768,128]{1,0:T(8,128)S(1)}) custom-call(s32[2]{0:T(128)S(1)} %pad_add_fusion.where, f32[512,256]{1,0:T(8,128)S(1)} %copy-done, f32[32,4]{1,0:T(8,128)S(1)} %convert_element_type.3.flags.flags_own, f32[264,128]{1,0:T(8,128)S(1)} %constant_dynamic-update-slice_fusion.own, ...), custom_call_target="tpu_custom_call" | custom-call | tf_op jit(solution)/shard_map/pallas_call | solution.py:76
  79.7 13.8 %all_to_all.69 = f32[16,48,128]{2,1,0:T(8,128)S(1)} all-to-all(f32[16,48,128]{2,1,0:T(8,128)S(1)} %bitcast.25), channel_id=1, replica_groups={{0,2,4,6,8,10,12,14,16,18,20,22,24,26,28,30},{32,34,36,38,40,42,44,46,4..., dimensions={0} | all-to-all | bytes 786432 | tf_op jit(solution)/shard_map/all_to_all | solution.py:526
  93.6 8.2 %all_to_all.70 = f32[4,48,128]{2,1,0:T(8,128)S(1)} all-to-all(f32[4,48,128]{2,1,0:T(8,128)S(1)} %bitcast.26), channel_id=1, replica_groups={{0,32,64,96},{2,34,66,98},{4,36,68,100},{6,38,70,102},{8,40,72,104},{10..., dimensions={0} | all-to-all | bytes 196608 | tf_op jit(solution)/shard_map/all_to_all | solution.py:526
  101.8 12.3 %all_to_all.71 = f32[16,48,128]{2,1,0:T(8,128)S(1)} all-to-all(f32[16,48,128]{2,1,0:T(8,128)S(1)} %bitcast.23), channel_id=1, replica_groups={{0,2,4,6,8,10,12,14,16,18,20,22,24,26,28,30},{32,34,36,38,40,42,44,46,4..., dimensions={0} | all-to-all | bytes 786432 | tf_op jit(solution)/shard_map/all_to_all | solution.py:526
  114.1 8.7 %shard_map.104 = (f32[128,128]{1,0:T(8,128)}, f32[256,128]{1,0:T(8,128)}) custom-call(f32[768,128]{1,0:T(8,128)S(1)} %bitcast.21), custom_call_target="tpu_custom_call" | custom-call | tf_op jit(solution)/shard_map/pallas_call | solution.py:76
  (5 shorter events, 0.1 us)
Async XLA Ops:
  0.6 4.5 %collective-permute-start.2 = (f32[128,256]{1,0:T(8,128)}, f32[128,256]{1,0:T(8,128)S(1)}, u32[]{:S(2)}, u32[]{:S(2)}) collective-permute-start(f32[128,256]{1,0:T(8,128)} %gain_own.1), channel_id=1, source_target_pairs={{0,1},{1,0},{2,3},{3,2},{4,5},{5,4},{6,7},{7,6},{8,9},{9,8},{10,11... | collective-permute-start | bytes 393224 | tf_op jit(solution)/shard_map/ppermute | solution.py:517
  0.7 4.4 %collective-permute-start.3 = (f32[256,128]{1,0:T(8,128)}, f32[256,128]{1,0:T(8,128)S(1)}, u32[]{:S(2)}, u32[]{:S(2)}) collective-permute-start(f32[256,128]{1,0:T(8,128)} %sense_own.1), channel_id=1, source_target_pairs={{0,1},{1,0},{2,3},{3,2},{4,5},{5,4},{6,7},{7,6},{8,9},{9,8},{10,11... | collective-permute-start | bytes 393224 | tf_op jit(solution)/shard_map/ppermute | solution.py:517
  3.7 10.5 %collective-permute-start = (f32[256,128]{1,0:T(8,128)S(1)}, f32[256,128]{1,0:T(8,128)S(1)}, u32[]{:S(2)}, u32[]{:S(2)}) collective-permute-start(f32[256,128]{1,0:T(8,128)S(1)} %get-tuple-element.25), channel_id=1, source_target_pairs={{0,1},{1,0},{2,3},{3,2},{4,5},{5,4},{6,7},{7,6},{8,9},{9,8},{10,11... | collective-permute-start | bytes 393224 | tf_op jit(solution)/shard_map/ppermute | solution.py:517
  3.8 1.3 %collective-permute-start.1 = (f32[32,4]{1,0:T(8,128)S(1)}, f32[32,4]{1,0:T(8,128)S(1)}, u32[]{:S(2)}, u32[]{:S(2)}) collective-permute-start(f32[32,4]{1,0:T(8,128)S(1)} %convert_element_type.3.flags.flags_own), channel_id=1, source_target_pairs={{0,1},{1,0},{2,3},{3,2},{4,5},{5,4},{6,7},{7,6},{8,9},{9,8},{10,11... | collective-permute-start | bytes 1544 | tf_op jit(solution)/shard_map/ppermute | solution.py:517
  14.2 40.1 %copy-start.1 = (f32[128,128]{1,0:T(8,128)S(1)}, f32[128,128]{1,0:T(8,128)}, u32[]{:S(2)}) copy-start(f32[128,128]{1,0:T(8,128)} %trans.3) | copy-start | bytes 196612
  14.2 40.1 %copy-start.2 = (f32[128]{0:T(128)S(1)}, f32[128]{0:T(128)}, u32[]{:S(2)}) copy-start(f32[128]{0:T(128)} %param.13) | copy-start | bytes 1540
  15.9 1.3 %collective-permute-start.4 = (f32[136,128]{1,0:T(8,128)S(1)}, f32[136,128]{1,0:T(8,128)S(1)}, u32[]{:S(2)}, u32[]{:S(2)}) collective-permute-start(f32[136,128]{1,0:T(8,128)S(1)} %get-tuple-element.29.own), channel_id=1, source_target_pairs={{0,1},{1,0},{2,3},{3,2},{4,5},{5,4},{6,7},{7,6},{8,9},{9,8},{10,11... | collective-permute-start | bytes 208904 | tf_op jit(solution)/shard_map/ppermute | solution.py:517
  54.3 23.1 %copy-start = (f32[512,256]{1,0:T(8,128)S(1)}, f32[512,256]{1,0:T(8,128)}, u32[]{:S(2)}) copy-start(f32[512,256]{1,0:T(8,128)} %tel.3) | copy-start | bytes 1572868
  75.8 1.6 %collective-permute-start.5 = (f32[264,128]{1,0:T(8,128)S(1)}, f32[264,128]{1,0:T(8,128)S(1)}, u32[]{:S(2)}, u32[]{:S(2)}) collective-permute-start(f32[264,128]{1,0:T(8,128)S(1)} %constant_dynamic-update-slice_fusion.own), channel_id=1, source_target_pairs={{0,1},{1,0},{2,3},{3,2},{4,5},{5,4},{6,7},{7,6},{8,9},{9,8},{10,11... | collective-permute-start | bytes 405512 | tf_op jit(solution)/shard_map/ppermute | solution.py:517

commit v6 on v5

--- a/solution.py
+++ b/solution.py
@@ -19,6 +19,7 @@
 FAR = 8
 PLANE = 16
 PLANES = 4
+BATCH = 8
 STATS = 6 * W
 SLICE = STATS // PLANE
 VMEM_LIMIT = 24 * 1024 * 1024
@@ -82,15 +83,18 @@
     return jax.ShapeDtypeStruct(dims, dtype), leaves
 
 
-def mask_of(flags, rows, segs):
-    cols = flags.shape[1] * 64
+def mask_of(flags, rows, first):
+    blocks, segs = flags.shape
     spread = (
-        lax.broadcasted_iota(jnp.int32, (flags.shape[1], cols), 0)
-        == lax.broadcasted_iota(jnp.int32, (flags.shape[1], cols), 1) // 64
-    )
-    by_sensor = jnp.dot(flags.astype(BF16), spread.astype(BF16), preferred_element_type=F32)
+        lax.broadcasted_iota(jnp.int32, (blocks, 64 * blocks), 0)
+        == lax.broadcasted_iota(jnp.int32, (blocks, 64 * blocks), 1) // 64
+    )
+    by_sensor = lax.dot_general(
+        flags.astype(F32).astype(BF16), spread.astype(BF16), (((0,), (0,)), ((), ())),
+        preferred_element_type=F32,
+    )
     repeat = (
-        lax.broadcasted_iota(jnp.int32, (rows, segs), 0) // LEN
+        lax.broadcasted_iota(jnp.int32, (rows, segs), 0) // LEN + first
         == lax.broadcasted_iota(jnp.int32, (rows, segs), 1)
     )
     return jnp.dot(repeat.astype(BF16), by_sensor.astype(BF16), preferred_element_type=F32)
@@ -99,26 +103,14 @@
 def push_kernel(where, tel, flags, gain, mine, theirs):
     gain_t = gain[...].T
     packed = wide(gain_t)
-    fl = flags[...]
     for out, core in ((theirs, 1 - where[1]), (mine, where[1])):
         start = pl.multiple_of(core * ROWS, ROWS)
-        seg_start = pl.multiple_of(core * SEGS, SEGS)
-        mask = mask_of(flags[pl.ds(seg_start, SEGS), :], ROWS, SEGS)
+        mask = mask_of(flags[...], ROWS, core * SEGS)
         high, low = halves(tel[pl.ds(start, ROWS), :] * mask)
         total = jnp.dot(high, packed, preferred_element_type=F32) + jnp.dot(
             low, packed, preferred_element_type=F32
         )
         out[...] = total[:, :W] + total[:, W:]
-
-
-def gain_maps(dev, trans_dev, gain_powers, drive_map):
-    dev_wide = wide(dev)
-    drive_map[...] = wide(-chained(trans_dev, dev, dev_wide))
-    for level in range(15):
-        gain_powers[level] = dev_wide
-        if level < 14:
-            dev = 2.0 * dev + times(dev_wide, dev_wide)
-            dev_wide = wide(dev)
 
 
 def maps_kernel(
@@ -140,30 +132,35 @@
             removed[side * 4 + g] = part[:, :W] + part[:, W:]
     base = a.T - identity()
     single[...] = base
-    batch = 4
-
-    def group(i, carry):
+    gain_dev = smooth_gain[...].T - identity()
+    drive_map[...] = wide(-chained(base, gain_dev, wide(gain_dev)))
+    batch = BATCH
+
+    def group(i, gain_dev):
         devs = []
         for j in range(batch):
             k = i * batch + j
             row = where[1] * SEGS + k
             dev = single[...]
             for g in range(4):
-                dev = dev - flags_own[row, g] * removed[g]
-                dev = dev - flags_other[row, g] * removed[4 + g]
+                dev = dev - flags_own[g, row].astype(F32) * removed[g]
+                dev = dev - flags_other[g, row].astype(F32) * removed[4 + g]
             devs.append(dev)
         for level in range(4):
             for j in range(batch):
                 packed = wide(devs[j])
                 powers[i * batch + j, level] = packed
                 devs[j] = 2.0 * devs[j] + times(packed, packed)
+            for j in range(batch // 4):
+                packed = wide(gain_dev)
+                gain_powers[(4 * i + level) * (batch // 4) + j] = packed
+                gain_dev = 2.0 * gain_dev + times(packed, packed)
         for j in range(batch):
             powers[i * batch + j, 4] = wide(devs[j])
             whole[i * batch + j] = devs[j]
-        return carry
-
-    lax.fori_loop(0, SEGS // batch, group, 0)
-    gain_maps(smooth_gain[...].T - identity(), base, gain_powers, drive_map)
+        return gain_dev
+
+    lax.fori_loop(0, SEGS // batch, group, gain_dev)
     count, base_at, source_at = SEGS, SEGS, 0
     while count > 1:
         for p in range(count // 2):
@@ -264,6 +261,19 @@
     state = step(state, (at & 2) != 0, early[1 + (at >> 2)])
     start = pl.multiple_of((at & 6) * PACK, 8)
     return step(state, (at & 1) != 0, raw[pl.ds(start, PACK)])
+
+
+def power_sum(part, powers, first):
+    level = part.shape[0].bit_length() - 2
+    while level >= 3:
+        half = 1 << level
+        part = part[:half] + moved(part[half:], powers[first + level])
+        level -= 1
+    while level >= 0:
+        behind = pltpu.roll(part, 8 - (1 << level), 0)
+        part = part + moved(behind, powers[first + level])
+        level -= 1
+    return part
 
 
 def filter_kernel(
@@ -300,32 +310,18 @@
     final_row = last + times(wide(last), wide(trans[...].T - identity()))
     final[...] = final_row
     top = (device == NEAR * FAR - 1) & (core == 1)
-    part = drive
-    for level in (7, 6, 5, 4, 3):
-        half = 1 << level
-        part = part[:half] + moved(part[half:], gain_powers[level])
-    for level in (2, 1, 0):
-        half = 1 << level
-        behind = pltpu.roll(part, 8 - half, 0)
-        part = part + moved(behind, gain_powers[level])
+    part = power_sum(drive, gain_powers, 0)
     from_top = moved(final_row, gain_powers[8])
     own = part[0:1] + jnp.where(top, from_top[0:1], 0.0)
     shift[...] = jnp.broadcast_to(own, (W, W))
 
 
-def smooth_kernel(where, gathered, drives, final, gain_powers, smoothed, incoming, suffix):
-    rows = gathered[...]
+def smooth_kernel(where, gathered, drives, final, gain_powers, smoothed, incoming):
     place = 2 * where[0] + where[1]
-    for level in range(7):
-        suffix[level] = rows
-        if level < 6:
-            ahead = moved(rows, gain_powers[8 + level])
-            rows = rows + pltpu.roll(ahead, W - (1 << level), 0)
-    state = jnp.zeros((8, W), F32)
-    for level in (6, 5, 4, 3, 2, 1, 0):
-        sibling = ((place >> level) | 1) << level
-        ahead = moved(state, gain_powers[8 + level]) + suffix[level, pl.ds(sibling, 1)]
-        state = jnp.where(((place >> level) & 1) == 0, ahead, state)
+    later = pltpu.roll(gathered[...], W - 1 - place, 0)
+    row = lax.broadcasted_iota(jnp.int32, (W, W), 0)
+    later = jnp.where(row < W - 1 - place, later, 0.0)
+    state = jnp.broadcast_to(power_sum(later, gain_powers, 8)[0:1], (8, W))
     top = jnp.where(place == W - 1, 1, 0)
     state = jnp.where(top == 1, final[...], state)
     incoming[...] = state
@@ -369,9 +365,7 @@
         lax.broadcasted_iota(jnp.int32, (2 * SEGS, count), 0)
         == lax.broadcasted_iota(jnp.int32, (2 * SEGS, count), 1) // LEN
     )
-    lane_flags = lax.dot_general(
-        fl.astype(BF16), repeat.astype(BF16), (((0,), (0,)), ((), ())), preferred_element_type=F32
-    )
+    lane_flags = jnp.dot(fl.astype(F32).astype(BF16), repeat.astype(BF16), preferred_element_type=F32)
     grams = []
     for g in range(4):
         masked_t = packed_t * lane_flags[g : g + 1].astype(BF16)
@@ -390,7 +384,7 @@
             row = 6 * W - 4 + 2 * tile + half
             moved_line = line if half == 0 else pltpu.roll(line, W // 2, 1)
             parts[row : row + 1] = jnp.where(lane < W // 2, moved_line, parts[row : row + 1])
-    high, low = halves(tel[...] * mask_of(fl, count, 2 * SEGS))
+    high, low = halves(tel[...] * mask_of(fl, count, 0))
     cross = jnp.dot(packed_t, high, preferred_element_type=F32) + jnp.dot(
         packed_t, low, preferred_element_type=F32
     )
@@ -528,25 +522,24 @@
 
 def on_device(telemetry, present, transition, sensing, filter_gain, smooth_gain, initial_state):
     where = jnp.stack([lax.axis_index("tm"), lax.axis_index("sens")]).astype(jnp.int32)
-    flags = present.astype(F32)
-
+    present = present.T
     other_gain = swap_core(filter_gain)
     other_sensing = swap_core(sensing)
-    other_flags = swap_core(flags)
-    mine, theirs = call(push_kernel, [shape(ROWS, W)] * 2, 1, 3, far=(0, 2))(
-        where, telemetry, flags, filter_gain
+    other_present = swap_core(present)
+    mine, theirs = call(push_kernel, [shape(ROWS, W)] * 2, 1, 3, far=(0, 1, 2))(
+        where, telemetry, present, filter_gain
     )
     received = swap_core(theirs)
     powers, tree, whole, gain_powers, drive_map = call(
         maps_kernel,
         [
             shape(SEGS, 5, W, 2 * W, dtype=BF16), shape(SEGS - 1, W, 2 * W, dtype=BF16),
-            shape(2 * SEGS - 1, W, W), shape(15, W, 2 * W, dtype=BF16), shape(W, 2 * W, dtype=BF16),
+            shape(2 * SEGS - 1, W, W), shape(16, W, 2 * W, dtype=BF16), shape(W, 2 * W, dtype=BF16),
         ],
         3, 6,
         scratch=[pltpu.VMEM((8, W, W), F32), pltpu.VMEM((W, W), F32)],
         far=(0, 1, 3, 5),
-    )(where, flags, other_flags, transition, filter_gain, other_gain, sensing, other_sensing, smooth_gain)
+    )(where, present, other_present, transition, filter_gain, other_gain, sensing, other_sensing, smooth_gain)
     inputs, ends, packed = call(
         shift_kernel, [shape(ROWS, W), shape(32, W), shape(PACK, W)], 0, 5
     )(mine, received, powers, tree, whole)
@@ -565,14 +558,14 @@
     )
     gathered = lax.all_to_all(shift, ("tm", "sens"), 0, 0, tiled=True)
     smoothed, incoming = call(
-        smooth_kernel, [shape(ROWS, W), shape(8, W)], 1, 4, [pltpu.VMEM((7, W, W), F32)]
+        smooth_kernel, [shape(ROWS, W), shape(8, W)], 1, 4
     )(where, gathered, drives, final, gain_powers)
     both = jnp.concatenate([smoothed, incoming], axis=0)
     other_both = swap_core(both)
     smoothed_out, stats = call(
         stats_kernel, [shape(2 * ROWS, W, leaves=True), shape(STATS, W)], 1, 4,
         [pltpu.VMEM((2 * ROWS, W), F32)],
-    )(where, telemetry, flags, both, other_both)
+    )(where, telemetry, present, both, other_both)
 
     stats = exchange(stats, 1, PLANE)
     (stats,) = call(functools.partial(sum_kernel, PLANE, PLANES), [shape(PLANES * SLICE, W)], 0, 1)(stats)

time: 123 us -> 120 us (0.976)
  Pallas kernels: 33.1 us -> 29.7 us
    pallas_call x11, Pallas kernels: 33.1 us -> 29.7 us  [placed(): return run(*operands[:n_smem], *near)]
  transfers between devices with their start and end apart: 6 -> 6, of which waited for: 3 -> 3; matrix products, arithmetic and copies ran while one was open for 1% -> 0% of each run, Pallas kernels for 9% -> 7%
where the time goes in v6:
time: 120 us
  blocking collectives  83.2 us (69%)
  Pallas kernels  29.7 us (25%)
  waiting for transfers between devices  3.34 us (3%)
  starting transfers between devices  1.77 us (1%)
    all_to_all x5, blocking collectives, exchange(): lax.all_to_all(value, 'tm', 0, 0, axis_index_groups=groups, tiled=True)  69.9 us
    pallas_call x11, Pallas kernels, placed(): return run(*operands[:n_smem], *near)  29.7 us
    all_to_all x1, blocking collectives, on_device(): gathered = lax.all_to_all(shift, ('tm', 'sens'), 0, 0, tiled=True)  13.3 us
    ppermute x6, waiting for transfers between devices, swap_core(): return lax.ppermute(value, 'sens', [(0, 1), (1, 0)])  3.34 us
  transfers between devices with their start and end apart: 6, of which 3 were waited for; matrix products, arithmetic and copies ran while one was open for 0% of the time, Pallas kernels for 7%

profile of v6, /device:TPU:0, one launch (start us, length us, event | category | flops | bytes accessed | tf_op | source)
XLA Modules:
  0.0 119.6 jit_solution(2801761808546323042)
XLA Ops:
  0.6 0.1 collective-permute-start.2
  0.7 0.5 collective-permute-start.3
  1.2 0.1 pad_add_fusion.where
  1.3 1.7 %shard_map.94 = (f32[256,128]{1,0:T(8,128)S(1)}, f32[256,128]{1,0:T(8,128)S(1)}) custom-call(s32[2]{0:T(128)S(1)} %pad_add_fusion.where, f32[512,256]{1,0:T(8,128)} %tel.3, s32[4,32]{1,0:T(4,128)} %bitcast.31, f32[128,256]{1,0:T(8,128)} %gain_own.1), custom_call_target="tpu_custom_call" | custom-call | tf_op jit(solution)/shard_map/pallas_call | solution.py:77
  3.0 0.2 collective-permute-start
  3.1 0.4 collective-permute-start.1
  3.6 1.0 collective-permute-done.1.flags_other
  4.6 0.0 collective-permute-done.2.gain_other
  4.6 0.0 collective-permute-done.3.sense_other
  4.6 0.0 copy-start.2
  4.6 0.7 copy-done.2
  5.3 6.3 %shard_map.95 = (bf16[16,5,128,256]{3,2,1,0:T(8,128)(2,1)S(1)}, bf16[15,128,256]{2,1,0:T(8,128)(2,1)S(1)}, f32[31,128,128]{2,1,0:T(8,128)S(1)}, bf16[16,128,256]{2,1,0:T(8,128)(2,1)S(1)}, bf16[128,256]{1,0:T(8,128)(2,1)S(1)}) custom-call(s32[2]{0:T(128)S(1)} %pad_add_fusion.where, s32[4,32]{1,0:T(4,128)S(1)} %bitcast.33, ...), custom_call_target="tpu_custom_call" | custom-call | tf_op jit(solution)/shard_map/pallas_call | solution.py:77
  11.6 0.0 collective-permute-done.received
  11.6 0.0 copy-start.1
  11.6 0.0 copy-start.4
  11.6 1.7 %shard_map.96 = (f32[256,128]{1,0:T(8,128)S(1)}, f32[32,128]{1,0:T(8,128)S(1)}, f32[136,128]{1,0:T(8,128)S(1)}) custom-call(f32[256,128]{1,0:T(8,128)S(1)} %get-tuple-element.24.mine, f32[256,128]{1,0:T(8,128)S(1)} %collective-permute-done.received, bf16[16,5,128,256]{3,2,1,0:T(8,128)(2,1)S(1)} %get-tuple-element.26.powers, ...), custom_call_target="tpu_custom_call" | custom-call | tf_op jit(solution)/shard_map/pallas_call | solution.py:77
  13.4 0.3 collective-permute-start.4
  13.7 0.9 collective-permute-done.4.other.c1
  14.6 0.7 shard_map.97
  15.4 16.7 %all_to_all.66 = f32[8,136,128]{2,1,0:T(8,128)S(1)} all-to-all(f32[8,136,128]{2,1,0:T(8,128)S(1)} %bitcast.21), channel_id=1, replica_groups={{0,2,4,6,8,10,12,14},{16,18,20,22,24,26,28,30},{32,34,36,38,40,42,44,46..., dimensions={0} | all-to-all | bytes 1114112 | tf_op jit(solution)/shard_map/all_to_all | solution.py:520
  32.0 0.7 shard_map.98
  32.7 19.0 %all_to_all.67 = f32[8,136,128]{2,1,0:T(8,128)S(1)} all-to-all(f32[8,136,128]{2,1,0:T(8,128)S(1)} %bitcast.25), channel_id=1, replica_groups={{0,16,32,48,64,80,96,112},{2,18,34,50,66,82,98,114},{4,20,36,52,68,84,1..., dimensions={0} | all-to-all | bytes 1114112 | tf_op jit(solution)/shard_map/all_to_all | solution.py:520
  51.7 0.0 copy-done.1
  51.7 0.0 copy-done.4
  51.7 0.0 copy-start
  51.7 0.0 copy-start.3
  51.7 4.9 %shard_map.99 = (f32[256,128]{1,0:T(8,128)S(1)}, f32[8,128]{1,0:T(8,128)S(1)}, f32[128,128]{1,0:T(8,128)S(1)}) custom-call(s32[2]{0:T(128)S(1)} %pad_add_fusion.where, f32[1088,128]{1,0:T(8,128)S(1)} %bitcast.20, f32[1088,128]{1,0:T(8,128)S(1)} %bitcast.19, f32[3,136,128]{2,1,0:T(8,128)S(1)} %get-tuple-element.31.early, ...), custom_call_target="tpu_custom_call" | custom-call | tf_op jit(solution)/shard_map/pallas_call | solution.py:77
  56.6 13.3 %all_to_all.68 = f32[128,1,128]{2,1,0:T(1,128)S(1)} all-to-all(f32[128,1,128]{2,1,0:T(1,128)S(1)} %bitcast.30), channel_id=1, replica_groups=mesh['tm'=64,'sens'=2] {'tm','sens'}, dimensions={0} | all-to-all | bytes 131072 | tf_op jit(solution)/shard_map/all_to_all | solution.py:559
  69.9 2.6 %shard_map.100 = (f32[256,128]{1,0:T(8,128)S(1)}, f32[8,128]{1,0:T(8,128)S(1)}) custom-call(s32[2]{0:T(128)S(1)} %pad_add_fusion.where, f32[128,128]{1,0:T(8,128)S(1)} %bitcast.29, f32[256,128]{1,0:T(8,128)S(1)} %get-tuple-element.37.drives, f32[8,128]{1,0:T(8,128)S(1)} %get-tuple-element.38.final, bf16[16,128,256]{2,1,0:T(8,128)(2,1)S(1)} %get-tuple-element.34.gain_powers), custom_call_target="tpu_custom_call" | custom-call | tf_op jit(solution)/shard_map/pallas_call | solution.py:77
  72.5 0.3 collective-permute-start.5
  72.8 1.3 %collective-permute-done.5.other = f32[264,128]{1,0:T(8,128)S(1)} collective-permute-done((f32[264,128]{1,0:T(8,128)S(1)}, f32[264,128]{1,0:T(8,128)S(1)}, u32[]{:S(2)}, u32[]{:S(2)}) %collective-permute-start.5) | collective-permute-done | bytes 135200 | tf_op jit(solution)/shard_map/ppermute | solution.py:511
  74.1 0.0 copy-done
  74.1 0.0 copy-done.3
  74.2 2.4 %shard_map.101 = (f32[512,128]{1,0:T(8,128)}, f32[768,128]{1,0:T(8,128)S(1)}) custom-call(s32[2]{0:T(128)S(1)} %pad_add_fusion.where, f32[512,256]{1,0:T(8,128)S(1)} %copy-done, s32[4,32]{1,0:T(4,128)S(1)} %bitcast.34, f32[264,128]{1,0:T(8,128)S(1)} %constant_dynamic-update-slice_fusion.own, f32[264,128]{1,0:T(8,128)S(1)} %collective-permute-done.5.other), custom_call_target="tpu_custom_call" | custom-call | tf_op jit(solution)/shard_map/pallas_call | solution.py:77
  76.5 13.8 %all_to_all.69 = f32[16,48,128]{2,1,0:T(8,128)S(1)} all-to-all(f32[16,48,128]{2,1,0:T(8,128)S(1)} %bitcast.26), channel_id=1, replica_groups={{0,2,4,6,8,10,12,14,16,18,20,22,24,26,28,30},{32,34,36,38,40,42,44,46,4..., dimensions={0} | all-to-all | bytes 786432 | tf_op jit(solution)/shard_map/all_to_all | solution.py:520
  90.4 8.2 %all_to_all.70 = f32[4,48,128]{2,1,0:T(8,128)S(1)} all-to-all(f32[4,48,128]{2,1,0:T(8,128)S(1)} %bitcast.27), channel_id=1, replica_groups={{0,32,64,96},{2,34,66,98},{4,36,68,100},{6,38,70,102},{8,40,72,104},{10..., dimensions={0} | all-to-all | bytes 196608 | tf_op jit(solution)/shard_map/all_to_all | solution.py:520
  98.6 12.3 %all_to_all.71 = f32[16,48,128]{2,1,0:T(8,128)S(1)} all-to-all(f32[16,48,128]{2,1,0:T(8,128)S(1)} %bitcast.24), channel_id=1, replica_groups={{0,2,4,6,8,10,12,14,16,18,20,22,24,26,28,30},{32,34,36,38,40,42,44,46,4..., dimensions={0} | all-to-all | bytes 786432 | tf_op jit(solution)/shard_map/all_to_all | solution.py:520
  110.9 8.7 %shard_map.104 = (f32[128,128]{1,0:T(8,128)}, f32[256,128]{1,0:T(8,128)}) custom-call(f32[768,128]{1,0:T(8,128)S(1)} %bitcast.22), custom_call_target="tpu_custom_call" | custom-call | tf_op jit(solution)/shard_map/pallas_call | solution.py:77
  (4 shorter events, 0.1 us)
Async XLA Ops:
  0.6 4.0 %collective-permute-start.2 = (f32[128,256]{1,0:T(8,128)}, f32[128,256]{1,0:T(8,128)S(1)}, u32[]{:S(2)}, u32[]{:S(2)}) collective-permute-start(f32[128,256]{1,0:T(8,128)} %gain_own.1), channel_id=1, source_target_pairs={{0,1},{1,0},{2,3},{3,2},{4,5},{5,4},{6,7},{7,6},{8,9},{9,8},{10,11... | collective-permute-start | bytes 393224 | tf_op jit(solution)/shard_map/ppermute | solution.py:511
  0.7 3.9 %collective-permute-start.3 = (f32[256,128]{1,0:T(8,128)}, f32[256,128]{1,0:T(8,128)S(1)}, u32[]{:S(2)}, u32[]{:S(2)}) collective-permute-start(f32[256,128]{1,0:T(8,128)} %sense_own.1), channel_id=1, source_target_pairs={{0,1},{1,0},{2,3},{3,2},{4,5},{5,4},{6,7},{7,6},{8,9},{9,8},{10,11... | collective-permute-start | bytes 393224 | tf_op jit(solution)/shard_map/ppermute | solution.py:511
  3.0 8.6 %collective-permute-start = (f32[256,128]{1,0:T(8,128)S(1)}, f32[256,128]{1,0:T(8,128)S(1)}, u32[]{:S(2)}, u32[]{:S(2)}) collective-permute-start(f32[256,128]{1,0:T(8,128)S(1)} %get-tuple-element.25), channel_id=1, source_target_pairs={{0,1},{1,0},{2,3},{3,2},{4,5},{5,4},{6,7},{7,6},{8,9},{9,8},{10,11... | collective-permute-start | bytes 393224 | tf_op jit(solution)/shard_map/ppermute | solution.py:511
  3.1 1.5 %collective-permute-start.1 = (s32[4,32]{1,0:T(4,128)}, s32[4,32]{1,0:T(4,128)S(1)}, u32[]{:S(2)}, u32[]{:S(2)}) collective-permute-start(s32[4,32]{1,0:T(4,128)} %bitcast.32), channel_id=1, source_target_pairs={{0,1},{1,0},{2,3},{3,2},{4,5},{5,4},{6,7},{7,6},{8,9},{9,8},{10,11... | collective-permute-start | bytes 1544 | tf_op jit(solution)/shard_map/ppermute | solution.py:511
  4.6 0.7 copy-start.2
  11.6 40.1 %copy-start.1 = (f32[128,128]{1,0:T(8,128)S(1)}, f32[128,128]{1,0:T(8,128)}, u32[]{:S(2)}) copy-start(f32[128,128]{1,0:T(8,128)} %trans.3) | copy-start | bytes 196612
  11.6 40.1 %copy-start.4 = (f32[128]{0:T(128)S(1)}, f32[128]{0:T(128)}, u32[]{:S(2)}) copy-start(f32[128]{0:T(128)} %param.13) | copy-start | bytes 1540
  13.4 1.3 %collective-permute-start.4 = (f32[136,128]{1,0:T(8,128)S(1)}, f32[136,128]{1,0:T(8,128)S(1)}, u32[]{:S(2)}, u32[]{:S(2)}) collective-permute-start(f32[136,128]{1,0:T(8,128)S(1)} %get-tuple-element.29.own), channel_id=1, source_target_pairs={{0,1},{1,0},{2,3},{3,2},{4,5},{5,4},{6,7},{7,6},{8,9},{9,8},{10,11... | collective-permute-start | bytes 208904 | tf_op jit(solution)/shard_map/ppermute | solution.py:511
  51.7 22.4 %copy-start = (f32[512,256]{1,0:T(8,128)S(1)}, f32[512,256]{1,0:T(8,128)}, u32[]{:S(2)}) copy-start(f32[512,256]{1,0:T(8,128)} %tel.3) | copy-start | bytes 1572868
  51.7 22.4 %copy-start.3 = (s32[32,4]{0,1:T(4,128)S(1)}, s32[32,4]{0,1:T(4,128)}, u32[]{:S(2)}) copy-start(s32[32,4]{0,1:T(4,128)} %param.8) | copy-start | bytes 1540
  72.5 1.6 %collective-permute-start.5 = (f32[264,128]{1,0:T(8,128)S(1)}, f32[264,128]{1,0:T(8,128)S(1)}, u32[]{:S(2)}, u32[]{:S(2)}) collective-permute-start(f32[264,128]{1,0:T(8,128)S(1)} %constant_dynamic-update-slice_fusion.own), channel_id=1, source_target_pairs={{0,1},{1,0},{2,3},{3,2},{4,5},{5,4},{6,7},{7,6},{8,9},{9,8},{10,11... | collective-permute-start | bytes 405512 | tf_op jit(solution)/shard_map/ppermute | solution.py:511

commit v7 on v6

--- a/solution.py
+++ b/solution.py
@@ -19,7 +19,6 @@
 FAR = 8
 PLANE = 16
 PLANES = 4
-BATCH = 8
 STATS = 6 * W
 SLICE = STATS // PLANE
 VMEM_LIMIT = 24 * 1024 * 1024
@@ -56,7 +55,7 @@
     return jnp.where(rows == cols, 1.0, 0.0).astype(F32)
 
 
-def call(kernel, out_shapes, n_smem, n_in, scratch=(), far=()):
+def call(kernel, out_shapes, n_smem, n_in, scratch=(), far=(), far_scalars=()):
     smem = [pl.BlockSpec(memory_space=pltpu.SMEM)] * n_smem
     vmem = [pl.BlockSpec(memory_space=pltpu.VMEM)] * n_in
     outs = [out if leaves else pltpu.VMEM(out.shape, out.dtype) for out, leaves in out_shapes]
@@ -74,7 +73,11 @@
             pltpu.with_memory_space_constraint(v, pltpu.HBM if i in far else pltpu.VMEM)
             for i, v in enumerate(operands[n_smem:])
         ]
-        return run(*operands[:n_smem], *near)
+        scalars = [
+            pltpu.with_memory_space_constraint(v, pltpu.HBM) if i in far_scalars else v
+            for i, v in enumerate(operands[:n_smem])
+        ]
+        return run(*scalars, *near)
 
     return placed
 
@@ -100,7 +103,7 @@
     return jnp.dot(repeat.astype(BF16), by_sensor.astype(BF16), preferred_element_type=F32)
 
 
-def push_kernel(where, tel, flags, gain, mine, theirs):
+def push_kernel(where, tel, flags, gain, unused, mine, theirs):
     gain_t = gain[...].T
     packed = wide(gain_t)
     for out, core in ((theirs, 1 - where[1]), (mine, where[1])):
@@ -115,7 +118,7 @@
 
 def maps_kernel(
     where, flags_own, flags_other, trans, gain_own, gain_other, sense_own, sense_other, smooth_gain,
-    powers, tree, whole, gain_powers, drive_map, removed, single,
+    powers, tree, whole, gain_powers, gain_triples, drive_map, removed, single,
 ):
     a = trans[...]
     a_wide = wide(a)
@@ -134,7 +137,7 @@
     single[...] = base
     gain_dev = smooth_gain[...].T - identity()
     drive_map[...] = wide(-chained(base, gain_dev, wide(gain_dev)))
-    batch = BATCH
+    batch = 8
 
     def group(i, gain_dev):
         devs = []
@@ -151,10 +154,13 @@
                 packed = wide(devs[j])
                 powers[i * batch + j, level] = packed
                 devs[j] = 2.0 * devs[j] + times(packed, packed)
-            for j in range(batch // 4):
-                packed = wide(gain_dev)
-                gain_powers[(4 * i + level) * (batch // 4) + j] = packed
-                gain_dev = 2.0 * gain_dev + times(packed, packed)
+            packed = wide(gain_dev)
+            twice = 2.0 * gain_dev + times(packed, packed)
+            twice_packed = wide(twice)
+            gain_powers[8 * i + 2 * level] = packed
+            gain_powers[8 * i + 2 * level + 1] = twice_packed
+            gain_triples[4 * i + level] = wide(chained(gain_dev, twice, twice_packed))
+            gain_dev = 2.0 * twice + times(twice_packed, twice_packed)
         for j in range(batch):
             powers[i * batch + j, 4] = wide(devs[j])
             whole[i * batch + j] = devs[j]
@@ -252,33 +258,57 @@
         early[slot, W:PACK] = row
 
 
-def advance(state, at, raw, early):
-    def step(state, used, packed):
-        ahead = moved(state, wide(packed[0:W])) + packed[W : W + 8]
-        return jnp.where(used, ahead, state)
-
-    state = step(state, at >= 4, early[0])
-    state = step(state, (at & 2) != 0, early[1 + (at >> 2)])
+def stages(at, raw, early):
     start = pl.multiple_of((at & 6) * PACK, 8)
-    return step(state, (at & 1) != 0, raw[pl.ds(start, PACK)])
-
-
-def power_sum(part, powers, first):
-    level = part.shape[0].bit_length() - 2
-    while level >= 3:
+    packed = (
+        (at >= 4, early[0]), ((at & 2) != 0, early[1 + (at >> 2)]), ((at & 1) != 0, raw[pl.ds(start, PACK)])
+    )
+    return [masked(used, value) for used, value in packed]
+
+
+def masked(used, packed):
+    packed = jnp.where(used, packed, 0.0)
+    return packed[0:W], packed[W : W + 8]
+
+
+def after_map(state, joined_map):
+    return moved(state, wide(joined_map[0])) + joined_map[1]
+
+
+def moved_sum(first, others, devs):
+    total = first
+    for rows in others:
+        total = total + rows
+    left = jnp.concatenate([wide(rows) for rows in others], axis=1)
+    right = jnp.concatenate([part for dev in devs for part in (dev, dev)], axis=0)
+    out = jnp.dot(left, right, preferred_element_type=F32)
+    return total + (out[:, :W] + out[:, W:])
+
+
+def power_sum(part, powers, triples, first):
+    level = part.shape[0].bit_length() - 1
+    if level % 2:
+        level -= 1
         half = 1 << level
-        part = part[:half] + moved(part[half:], powers[first + level])
-        level -= 1
-    while level >= 0:
-        behind = pltpu.roll(part, 8 - (1 << level), 0)
-        part = part + moved(behind, powers[first + level])
-        level -= 1
+        part = moved_sum(part[:half], [part[half:]], [powers[first + level]])
+    while level:
+        level -= 2
+        span = 1 << level
+        devs = [powers[first + level], powers[first + level + 1], triples[(first + level) // 2]]
+        if span >= 8:
+            pieces = [part[q * span : (q + 1) * span] for q in range(4)]
+        elif span == 4:
+            near, far = part[:8], part[8:]
+            pieces = [near, pltpu.roll(near, 4, 0), far, pltpu.roll(far, 4, 0)]
+        else:
+            pieces = [part] + [pltpu.roll(part, 8 - q * span, 0) for q in (1, 2, 3)]
+        part = moved_sum(pieces[0], pieces[1:], devs)
     return part
 
 
 def filter_kernel(
-    where, far, near, early, c1, initial, inputs, ends, powers, tree, gain_powers, drive_map,
-    trans, drives, final, shift, far_early,
+    where, far, near, early, c1, initial, inputs, ends, powers, tree, gain_powers, gain_triples, drive_map,
+    trans, drives, shift, far_early,
 ):
     device, core = where[0], where[1]
     level = split_maps(far)
@@ -287,10 +317,11 @@
         far_early[slot, 0:W] = dev
         far_early[slot, W:PACK] = row
     state = jnp.broadcast_to(initial[...], (8, W))
-    state = advance(state, device // NEAR, far, far_early)
-    state = advance(state, device % NEAR, near, early)
-    ahead = moved(state, wide(c1[0:W])) + c1[W : W + 8]
-    state = jnp.where(core == 1, ahead, state)
+    for stage in stages(device // NEAR, far, far_early):
+        state = after_map(state, stage)
+    inner = stages(device % NEAR, near, early)
+    inner.append(masked(core == 1, c1[...]))
+    state = after_map(state, joined(joined(inner[0], inner[1]), joined(inner[2], inner[3])))
     starts = {0: state}
     for span, maps_at, ends_at in ((8, 12, 28), (4, 8, 24), (2, 0, 16), (1, -1, 0)):
         for begin in range(0, SEGS, 2 * span):
@@ -305,51 +336,51 @@
     rows = inputs[...] + jnp.where(row_at == 0, spread, 0.0)
     rows = seg_scan(rows, powers)
     drive = times(wide(rows), drive_map[...])
-    drives[...] = drive
+    drives[0:ROWS] = drive
     last = jnp.broadcast_to(rows[ROWS - 1 : ROWS], (8, W))
     final_row = last + times(wide(last), wide(trans[...].T - identity()))
-    final[...] = final_row
+    drives[ROWS : ROWS + 8] = final_row
     top = (device == NEAR * FAR - 1) & (core == 1)
-    part = power_sum(drive, gain_powers, 0)
+    part = power_sum(drive, gain_powers, gain_triples, 0)
     from_top = moved(final_row, gain_powers[8])
     own = part[0:1] + jnp.where(top, from_top[0:1], 0.0)
     shift[...] = jnp.broadcast_to(own, (W, W))
 
 
-def smooth_kernel(where, gathered, drives, final, gain_powers, smoothed, incoming):
-    place = 2 * where[0] + where[1]
+def stats_kernel(
+    where, gathered, own, other, gain_powers, gain_triples, tel, flags, smoothed, parts, full,
+):
+    core = where[1]
+    count = 2 * ROWS
+    place = 2 * where[0] + 1
     later = pltpu.roll(gathered[...], W - 1 - place, 0)
     row = lax.broadcasted_iota(jnp.int32, (W, W), 0)
     later = jnp.where(row < W - 1 - place, later, 0.0)
-    state = jnp.broadcast_to(power_sum(later, gain_powers, 8)[0:1], (8, W))
-    top = jnp.where(place == W - 1, 1, 0)
-    state = jnp.where(top == 1, final[...], state)
-    incoming[...] = state
-    entry = moved(state, gain_powers[0])
-    row_at = lax.broadcasted_iota(jnp.int32, (ROWS, W), 0)
-    part = drives[...]
-    part = part + jnp.where(row_at == ROWS - 1, jnp.broadcast_to(entry[0:1], (ROWS, W)), 0.0)
-    for level in range(8):
-        reach = 1 << level
-        behind = jnp.where(row_at < ROWS - reach, pltpu.roll(part, ROWS - reach, 0), 0.0)
-        part = part + moved(behind, gain_powers[level])
-    smoothed[...] = part
-
-
-def stats_kernel(where, tel, flags, own, other, smoothed, parts, full):
-    core = where[1]
+    state = jnp.broadcast_to(power_sum(later, gain_powers, gain_triples, 8)[0:1], (8, W))
+    final = jnp.where(core == 1, own[ROWS : ROWS + 8], other[ROWS : ROWS + 8])
+    state = jnp.where(place == W - 1, final, state)
     full[pl.ds(pl.multiple_of(core * ROWS, ROWS), ROWS)] = own[0:ROWS]
     full[pl.ds(pl.multiple_of((1 - core) * ROWS, ROWS), ROWS)] = other[0:ROWS]
+    row_at = lax.broadcasted_iota(jnp.int32, (count, W), 0)
+    entry = moved(state, gain_powers[0])
     rows = full[...]
+    rows = rows + jnp.where(row_at == count - 1, jnp.broadcast_to(entry[0:1], (count, W)), 0.0)
+
+    def behind(rows, reach):
+        return jnp.where(row_at < count - reach, pltpu.roll(rows, count - reach, 0), 0.0)
+
+    for level in (0, 2, 4, 6):
+        three = [behind(rows, q << level) for q in (1, 2, 3)]
+        rows = moved_sum(rows, three, [gain_powers[level], gain_powers[level + 1], gain_triples[level // 2]])
+    half = moved(rows[ROWS:], gain_powers[8])
+    rows = jnp.concatenate([rows[:ROWS] + half, rows[ROWS:]], axis=0)
     smoothed[...] = rows
-    count = 2 * ROWS
-    after = jnp.where(core == 1, own[ROWS : ROWS + 8], other[ROWS : ROWS + 8])
-    row_at = lax.broadcasted_iota(jnp.int32, (count, W), 0)
     following = jnp.where(
-        row_at == count - 1, jnp.broadcast_to(after[0:1], (count, W)), pltpu.roll(rows, count - 1, 0)
+        row_at == count - 1, jnp.broadcast_to(state[0:1], (count, W)), pltpu.roll(rows, count - 1, 0)
     )
     packed = wide(rows)
-    packed_t = jnp.concatenate([rows.T.astype(BF16), (rows - rows.astype(BF16).astype(F32)).T.astype(BF16)], axis=0)
+    high = rows.astype(BF16)
+    packed_t = jnp.concatenate([rows.T.astype(BF16), (rows - high.astype(F32)).T.astype(BF16)], axis=0)
     last_chip = where[0] == NEAR * FAR - 1
     lane_at = lax.broadcasted_iota(jnp.int32, (2 * W, count), 1)
     kept = jnp.where(last_chip & (lane_at == count - 1), jnp.zeros_like(packed_t), packed_t)
@@ -526,19 +557,21 @@
     other_gain = swap_core(filter_gain)
     other_sensing = swap_core(sensing)
     other_present = swap_core(present)
-    mine, theirs = call(push_kernel, [shape(ROWS, W)] * 2, 1, 3, far=(0, 1, 2))(
-        where, telemetry, present, filter_gain
+    mine, theirs = call(push_kernel, [shape(ROWS, W)] * 2, 1, 4, far=(0, 1, 2))(
+        where, telemetry, present, filter_gain, other_present
     )
     received = swap_core(theirs)
-    powers, tree, whole, gain_powers, drive_map = call(
+    powers, tree, whole, gain_powers, gain_triples, drive_map = call(
         maps_kernel,
         [
             shape(SEGS, 5, W, 2 * W, dtype=BF16), shape(SEGS - 1, W, 2 * W, dtype=BF16),
-            shape(2 * SEGS - 1, W, W), shape(16, W, 2 * W, dtype=BF16), shape(W, 2 * W, dtype=BF16),
+            shape(2 * SEGS - 1, W, W), shape(16, W, 2 * W, dtype=BF16), shape(8, W, 2 * W, dtype=BF16),
+            shape(W, 2 * W, dtype=BF16),
         ],
         3, 6,
         scratch=[pltpu.VMEM((8, W, W), F32), pltpu.VMEM((W, W), F32)],
         far=(0, 1, 3, 5),
+        far_scalars=(1,),
     )(where, present, other_present, transition, filter_gain, other_gain, sensing, other_sensing, smooth_gain)
     inputs, ends, packed = call(
         shift_kernel, [shape(ROWS, W), shape(32, W), shape(PACK, W)], 0, 5
@@ -549,23 +582,18 @@
     near = exchange(chip, 1, NEAR)
     group, early = call(eight_kernel, [shape(FAR * PACK, W), shape(3, PACK, W)], 0, 1)(near)
     far = exchange(group, NEAR, FAR)
-    drives, final, shift = call(
-        filter_kernel, [shape(ROWS, W), shape(8, W), shape(W, W)], 1, 12,
-        [pltpu.VMEM((3, PACK, W), F32)],
+    drives, shift = call(
+        filter_kernel, [shape(ROWS + 8, W), shape(W, W)], 1, 13, [pltpu.VMEM((3, PACK, W), F32)]
     )(
         where, far, near, early, other_packed, initial_state.reshape(1, W), inputs, ends, powers, tree,
-        gain_powers, drive_map, transition,
-    )
+        gain_powers, gain_triples, drive_map, transition,
+    )
+    other_drives = swap_core(drives)
     gathered = lax.all_to_all(shift, ("tm", "sens"), 0, 0, tiled=True)
-    smoothed, incoming = call(
-        smooth_kernel, [shape(ROWS, W), shape(8, W)], 1, 4
-    )(where, gathered, drives, final, gain_powers)
-    both = jnp.concatenate([smoothed, incoming], axis=0)
-    other_both = swap_core(both)
-    smoothed_out, stats = call(
-        stats_kernel, [shape(2 * ROWS, W, leaves=True), shape(STATS, W)], 1, 4,
+    smoothed, stats = call(
+        stats_kernel, [shape(2 * ROWS, W, leaves=True), shape(STATS, W)], 1, 7,
         [pltpu.VMEM((2 * ROWS, W), F32)],
-    )(where, telemetry, present, both, other_both)
+    )(where, gathered, drives, other_drives, gain_powers, gain_triples, telemetry, present)
 
     stats = exchange(stats, 1, PLANE)
     (stats,) = call(functools.partial(sum_kernel, PLANE, PLANES), [shape(PLANES * SLICE, W)], 0, 1)(stats)
@@ -576,7 +604,7 @@
     new_transition, new_sensing = call(
         functools.partial(solve_kernel, ridge), [shape(W, W, leaves=True), shape(2 * W, W, leaves=True)], 0, 1
     )(stats)
-    return new_transition, new_sensing, smoothed_out
+    return new_transition, new_sensing, smoothed
 
 
 def solution(mesh):

time: 120 us -> 116 us (0.967)
  waiting for transfers between devices: 3.34 us -> 1.62 us
    ppermute x6, waiting for transfers between devices: 3.34 us -> 1.62 us  [swap_core(): return lax.ppermute(value, 'sens', [(0, 1), (1, 0)])]
    pallas_call x11 -> x10, Pallas kernels: 29.7 us -> 29.1 us  [placed(): return run(*scalars, *near)]
  transfers between devices with their start and end apart: 6 -> 6, of which waited for: 3 -> 2; matrix products, arithmetic and copies ran while one was open for 0% -> 0% of each run, Pallas kernels for 7% -> 7%
where the time goes in v7:
time: 116 us
  blocking collectives  82.8 us (71%)
  Pallas kernels  29.1 us (25%)
  waiting for transfers between devices  1.62 us (1%)
  starting transfers between devices  1.32 us (1%)
    all_to_all x5, blocking collectives, exchange(): lax.all_to_all(value, 'tm', 0, 0, axis_index_groups=groups, tiled=True)  69.5 us
    pallas_call x10, Pallas kernels, placed(): return run(*scalars, *near)  29.1 us
    all_to_all x1, blocking collectives, on_device(): gathered = lax.all_to_all(shift, ('tm', 'sens'), 0, 0, tiled=True)  13.3 us
  transfers between devices with their start and end apart: 6, of which 2 were waited for; matrix products, arithmetic and copies ran while one was open for 0% of the time, Pallas kernels for 7%

profile of v7, /device:TPU:0, one launch (start us, length us, event | category | flops | bytes accessed | tf_op | source)
XLA Modules:
  0.0 115.7 jit_solution(9140866253870677102)
XLA Ops:
  0.6 0.1 collective-permute-start
  0.7 0.5 collective-permute-start.2
  1.2 0.1 collective-permute-start.3
  1.3 0.1 pad_add_fusion.where
  1.4 0.7 collective-permute-done.unused.flags_other
  2.1 1.7 %shard_map.94 = (f32[256,128]{1,0:T(8,128)S(1)}, f32[256,128]{1,0:T(8,128)S(1)}) custom-call(s32[2]{0:T(128)S(1)} %pad_add_fusion.where, f32[512,256]{1,0:T(8,128)} %tel.3, s32[4,32]{1,0:T(4,128)} %bitcast.32, f32[128,256]{1,0:T(8,128)} %gain_own.1, s32[4,32]{1,0:T(4,128)S(1)} %collective-permute-done.unused.flags_other), custom_call_target="tpu_custom_call" | custom-call | tf_op jit(solution)/shard_map/pallas_call | solution.py:80
  3.8 0.3 collective-permute-start.1
  4.0 0.0 collective-permute-done.2.gain_other
  4.0 0.0 collective-permute-done.3.sense_other
  4.0 6.3 %shard_map.95 = (bf16[16,5,128,256]{3,2,1,0:T(8,128)(2,1)S(1)}, bf16[15,128,256]{2,1,0:T(8,128)(2,1)S(1)}, f32[31,128,128]{2,1,0:T(8,128)S(1)}, bf16[16,128,256]...) custom-call(s32[2]{0:T(128)S(1)} %pad_add_fusion.where, s32[4,32]{1,0:T(4,128)} %bitcast.33, ...), custom_call_target="tpu_custom_call" | custom-call | tf_op jit(solution)/shard_map/pallas_call | solution.py:80
  10.4 0.0 collective-permute-done.1.received
  10.4 0.0 copy-start.1
  10.4 0.0 copy-start.3
  10.4 1.7 %shard_map.96 = (f32[256,128]{1,0:T(8,128)S(1)}, f32[32,128]{1,0:T(8,128)S(1)}, f32[136,128]{1,0:T(8,128)S(1)}) custom-call(f32[256,128]{1,0:T(8,128)S(1)} %get-tuple-element.22.mine, f32[256,128]{1,0:T(8,128)S(1)} %collective-permute-done.1.received, bf16[16,5,128,256]{3,2,1,0:T(8,128)(2,1)S(1)} %get-tuple-element.24.powers, ...), custom_call_target="tpu_custom_call" | custom-call | tf_op jit(solution)/shard_map/pallas_call | solution.py:80
  12.1 0.3 collective-permute-start.4
  12.5 0.9 collective-permute-done.4.other.c1
  13.4 0.7 shard_map.97
  14.1 16.7 %all_to_all.66 = f32[8,136,128]{2,1,0:T(8,128)S(1)} all-to-all(f32[8,136,128]{2,1,0:T(8,128)S(1)} %bitcast.21), channel_id=1, replica_groups={{0,2,4,6,8,10,12,14},{16,18,20,22,24,26,28,30},{32,34,36,38,40,42,44,46..., dimensions={0} | all-to-all | bytes 1114112 | tf_op jit(solution)/shard_map/all_to_all | solution.py:551
  30.8 0.7 shard_map.98
  31.5 0.0 copy-start
  31.5 0.0 copy-start.2
  31.5 19.1 %all_to_all.67 = f32[8,136,128]{2,1,0:T(8,128)S(1)} all-to-all(f32[8,136,128]{2,1,0:T(8,128)S(1)} %bitcast.25), channel_id=1, replica_groups={{0,16,32,48,64,80,96,112},{2,18,34,50,66,82,98,114},{4,20,36,52,68,84,1..., dimensions={0} | all-to-all | bytes 1114112 | tf_op jit(solution)/shard_map/all_to_all | solution.py:551
  50.6 0.0 copy-done.1
  50.6 0.0 copy-done.3
  50.6 4.4 %shard_map.99 = (f32[264,128]{1,0:T(8,128)S(1)}, f32[128,128]{1,0:T(8,128)S(1)}) custom-call(s32[2]{0:T(128)S(1)} %pad_add_fusion.where, f32[1088,128]{1,0:T(8,128)S(1)} %bitcast.20, f32[1088,128]{1,0:T(8,128)S(1)} %bitcast.19, f32[3,136,128]{2,1,0:T(8,128)S(1)} %get-tuple-element.29.early, f32[136,128]{1,0:T(8,128)S(1)} %collective-permute-done.4.other.c1, ...), custom_call_target="tpu_custom_call" | custom-call | tf_op jit(solution)/shard_map/pallas_call | solution.py:80
  55.0 0.0 collective-permute-start.5
  55.1 13.3 %all_to_all.68 = f32[128,1,128]{2,1,0:T(1,128)S(1)} all-to-all(f32[128,1,128]{2,1,0:T(1,128)S(1)} %bitcast.30), channel_id=1, replica_groups=mesh['tm'=64,'sens'=2] {'tm','sens'}, dimensions={0} | all-to-all | bytes 131072 | tf_op jit(solution)/shard_map/all_to_all | solution.py:592
  68.3 0.0 collective-permute-done.5.other
  68.3 0.0 copy-done
  68.3 0.0 copy-done.2
  68.4 4.8 %shard_map.100 = (f32[512,128]{1,0:T(8,128)}, f32[768,128]{1,0:T(8,128)S(1)}) custom-call(s32[2]{0:T(128)S(1)} %pad_add_fusion.where, f32[128,128]{1,0:T(8,128)S(1)} %bitcast.29, f32[264,128]{1,0:T(8,128)S(1)} %get-tuple-element.36.own, f32[264,128]{1,0:T(8,128)S(1)} %collective-permute-done.5.other, ...), custom_call_target="tpu_custom_call" | custom-call | tf_op jit(solution)/shard_map/pallas_call | solution.py:80
  73.1 13.3 %all_to_all.69 = f32[16,48,128]{2,1,0:T(8,128)S(1)} all-to-all(f32[16,48,128]{2,1,0:T(8,128)S(1)} %bitcast.26), channel_id=1, replica_groups={{0,2,4,6,8,10,12,14,16,18,20,22,24,26,28,30},{32,34,36,38,40,42,44,46,4..., dimensions={0} | all-to-all | bytes 786432 | tf_op jit(solution)/shard_map/all_to_all | solution.py:551
  86.4 8.2 %all_to_all.70 = f32[4,48,128]{2,1,0:T(8,128)S(1)} all-to-all(f32[4,48,128]{2,1,0:T(8,128)S(1)} %bitcast.27), channel_id=1, replica_groups={{0,32,64,96},{2,34,66,98},{4,36,68,100},{6,38,70,102},{8,40,72,104},{10..., dimensions={0} | all-to-all | bytes 196608 | tf_op jit(solution)/shard_map/all_to_all | solution.py:551
  94.6 12.3 %all_to_all.71 = f32[16,48,128]{2,1,0:T(8,128)S(1)} all-to-all(f32[16,48,128]{2,1,0:T(8,128)S(1)} %bitcast.24), channel_id=1, replica_groups={{0,2,4,6,8,10,12,14,16,18,20,22,24,26,28,30},{32,34,36,38,40,42,44,46,4..., dimensions={0} | all-to-all | bytes 786432 | tf_op jit(solution)/shard_map/all_to_all | solution.py:551
  106.9 8.7 %shard_map.103 = (f32[128,128]{1,0:T(8,128)}, f32[256,128]{1,0:T(8,128)}) custom-call(f32[768,128]{1,0:T(8,128)S(1)} %bitcast.22), custom_call_target="tpu_custom_call" | custom-call | tf_op jit(solution)/shard_map/pallas_call | solution.py:80
  (2 shorter events, 0.1 us)
Async XLA Ops:
  0.6 1.4 %collective-permute-start = (s32[4,32]{1,0:T(4,128)}, s32[4,32]{1,0:T(4,128)S(1)}, u32[]{:S(2)}, u32[]{:S(2)}) collective-permute-start(s32[4,32]{1,0:T(4,128)} %bitcast.31), channel_id=1, source_target_pairs={{0,1},{1,0},{2,3},{3,2},{4,5},{5,4},{6,7},{7,6},{8,9},{9,8},{10,11... | collective-permute-start | bytes 1544 | tf_op jit(solution)/shard_map/ppermute | solution.py:542
  0.7 3.3 %collective-permute-start.2 = (f32[128,256]{1,0:T(8,128)}, f32[128,256]{1,0:T(8,128)S(1)}, u32[]{:S(2)}, u32[]{:S(2)}) collective-permute-start(f32[128,256]{1,0:T(8,128)} %gain_own.1), channel_id=1, source_target_pairs={{0,1},{1,0},{2,3},{3,2},{4,5},{5,4},{6,7},{7,6},{8,9},{9,8},{10,11... | collective-permute-start | bytes 393224 | tf_op jit(solution)/shard_map/ppermute | solution.py:542
  1.2 2.8 %collective-permute-start.3 = (f32[256,128]{1,0:T(8,128)}, f32[256,128]{1,0:T(8,128)S(1)}, u32[]{:S(2)}, u32[]{:S(2)}) collective-permute-start(f32[256,128]{1,0:T(8,128)} %sense_own.1), channel_id=1, source_target_pairs={{0,1},{1,0},{2,3},{3,2},{4,5},{5,4},{6,7},{7,6},{8,9},{9,8},{10,11... | collective-permute-start | bytes 393224 | tf_op jit(solution)/shard_map/ppermute | solution.py:542
  3.8 6.6 %collective-permute-start.1 = (f32[256,128]{1,0:T(8,128)S(1)}, f32[256,128]{1,0:T(8,128)S(1)}, u32[]{:S(2)}, u32[]{:S(2)}) collective-permute-start(f32[256,128]{1,0:T(8,128)S(1)} %get-tuple-element.23), channel_id=1, source_target_pairs={{0,1},{1,0},{2,3},{3,2},{4,5},{5,4},{6,7},{7,6},{8,9},{9,8},{10,11... | collective-permute-start | bytes 393224 | tf_op jit(solution)/shard_map/ppermute | solution.py:542
  10.4 40.2 %copy-start.1 = (f32[128,128]{1,0:T(8,128)S(1)}, f32[128,128]{1,0:T(8,128)}, u32[]{:S(2)}) copy-start(f32[128,128]{1,0:T(8,128)} %trans.3) | copy-start | bytes 196612
  10.4 40.2 %copy-start.3 = (f32[128]{0:T(128)S(1)}, f32[128]{0:T(128)}, u32[]{:S(2)}) copy-start(f32[128]{0:T(128)} %param.13) | copy-start | bytes 1540
  12.1 1.3 %collective-permute-start.4 = (f32[136,128]{1,0:T(8,128)S(1)}, f32[136,128]{1,0:T(8,128)S(1)}, u32[]{:S(2)}, u32[]{:S(2)}) collective-permute-start(f32[136,128]{1,0:T(8,128)S(1)} %get-tuple-element.27.own), channel_id=1, source_target_pairs={{0,1},{1,0},{2,3},{3,2},{4,5},{5,4},{6,7},{7,6},{8,9},{9,8},{10,11... | collective-permute-start | bytes 208904 | tf_op jit(solution)/shard_map/ppermute | solution.py:542
  31.5 36.9 %copy-start = (f32[512,256]{1,0:T(8,128)S(1)}, f32[512,256]{1,0:T(8,128)}, u32[]{:S(2)}) copy-start(f32[512,256]{1,0:T(8,128)} %tel.3) | copy-start | bytes 1572868
  31.5 36.9 %copy-start.2 = (s32[32,4]{0,1:T(4,128)S(1)}, s32[32,4]{0,1:T(4,128)}, u32[]{:S(2)}) copy-start(s32[32,4]{0,1:T(4,128)} %param.8) | copy-start | bytes 1540
  55.0 13.3 %collective-permute-start.5 = (f32[264,128]{1,0:T(8,128)S(1)}, f32[264,128]{1,0:T(8,128)S(1)}, u32[]{:S(2)}, u32[]{:S(2)}) collective-permute-start(f32[264,128]{1,0:T(8,128)S(1)} %get-tuple-element.36.own), channel_id=1, source_target_pairs={{0,1},{1,0},{2,3},{3,2},{4,5},{5,4},{6,7},{7,6},{8,9},{9,8},{10,11... | collective-permute-start | bytes 405512 | tf_op jit(solution)/shard_map/ppermute | solution.py:542

commit v8 on v7

--- a/solution.py
+++ b/solution.py
@@ -118,7 +118,7 @@
 
 def maps_kernel(
     where, flags_own, flags_other, trans, gain_own, gain_other, sense_own, sense_other, smooth_gain,
-    powers, tree, whole, gain_powers, gain_triples, drive_map, removed, single,
+    powers, whole, gain_powers, gain_triples, drive_map, removed, single,
 ):
     a = trans[...]
     a_wide = wide(a)
@@ -127,11 +127,11 @@
         seen = times(wide(sense[...]), a_wide)
         seen_high, seen_low = halves(seen.T)
         gain_wide = wide(gain[...].T)
+        zero = jnp.zeros_like(seen_high)
+        blocks = [jnp.where(lane == g, part, zero) for g in range(4) for part in (seen_high, seen_low)]
+        product = jnp.dot(jnp.concatenate(blocks, axis=0), gain_wide, preferred_element_type=F32)
         for g in range(4):
-            zero = jnp.zeros_like(seen_high)
-            part = jnp.dot(
-                jnp.where(lane == g, seen_high, zero), gain_wide, preferred_element_type=F32
-            ) + jnp.dot(jnp.where(lane == g, seen_low, zero), gain_wide, preferred_element_type=F32)
+            part = product[2 * g * W : (2 * g + 1) * W] + product[(2 * g + 1) * W : (2 * g + 2) * W]
             removed[side * 4 + g] = part[:, :W] + part[:, W:]
     base = a.T - identity()
     single[...] = base
@@ -167,35 +167,36 @@
         return gain_dev
 
     lax.fori_loop(0, SEGS // batch, group, gain_dev)
-    count, base_at, source_at = SEGS, SEGS, 0
-    while count > 1:
-        for p in range(count // 2):
-            second = whole[source_at + 2 * p + 1]
-            joined = chained(whole[source_at + 2 * p], second, wide(second))
-            whole[base_at + p] = joined
-            tree[base_at - SEGS + p] = wide(joined)
-        source_at = base_at
-        count //= 2
-        base_at += count
-
-
-def seg_scan(rows, powers):
+
+
+def seg_step(rows, powers, level, starts=None):
     row_at = lax.broadcasted_iota(jnp.int32, (ROWS, W), 0) % LEN
-    for level in range(4):
-        reach = 1 << level
-        before = jnp.where(row_at >= reach, pltpu.roll(rows, reach, 0), 0.0)
-        packed = wide(before)
-        parts = [
-            times(packed[k * LEN : (k + 1) * LEN], powers[k, level]) for k in range(SEGS)
-        ]
-        rows = rows + before + jnp.concatenate(parts, axis=0)
-    return rows
-
-
-def shift_kernel(mine, received, powers, tree, whole, inputs, ends, packed):
+    reach = 1 << level
+    before = jnp.where(row_at >= reach, pltpu.roll(rows, reach, 0), 0.0)
+    if starts is not None:
+        before = jnp.where(row_at == reach - 1, starts, before)
+    packed = wide(before)
+    parts = [times(packed[k * LEN : (k + 1) * LEN], powers[k, level]) for k in range(SEGS)]
+    return rows + before + jnp.concatenate(parts, axis=0)
+
+
+def shift_kernel(mine, received, powers, whole, inputs, ends, packed, tree):
     rows = mine[...] + received[...]
     inputs[...] = rows
-    reached = seg_scan(rows, powers)
+    devs = [whole[k] for k in range(SEGS)]
+    at = 0
+    composite = []
+    reached = rows
+    for step in range(4):
+        devs = [
+            chained(devs[2 * p], devs[2 * p + 1], wide(devs[2 * p + 1])) for p in range(len(devs) // 2)
+        ]
+        reached = seg_step(reached, powers, step)
+        for p, dev in enumerate(devs):
+            dev_wide = wide(dev)
+            composite.append(dev_wide)
+            tree[at + p] = dev_wide
+        at += len(devs)
     level = [reached[k * LEN + LEN - 1 : (k + 1) * LEN] for k in range(SEGS)]
     ends[0:SEGS] = jnp.concatenate(level, axis=0)
     maps = [powers[k, 4] for k in range(SEGS)]
@@ -205,12 +206,12 @@
             moved(jnp.broadcast_to(level[2 * p], (8, W)), maps[2 * p + 1])[0:1] + level[2 * p + 1]
             for p in range(len(level) // 2)
         ]
-        maps = [tree[tree_at + p] for p in range(len(level))]
+        maps = composite[tree_at : tree_at + len(level)]
         tree_at += len(level)
         for p, row in enumerate(level):
             ends[at + p : at + p + 1] = row
         at += len(level)
-    packed[0:W] = whole[2 * SEGS - 2]
+    packed[0:W] = devs[0]
     packed[W:PACK] = jnp.broadcast_to(level[0], (PACK - W, W))
 
 
@@ -328,13 +329,17 @@
             p = begin // span
             dev = powers[p, 4] if span == 1 else tree[maps_at + p]
             starts[begin + span] = moved(starts[begin], dev) + ends[ends_at + p : ends_at + p + 1]
-    entry = [moved(starts[k], powers[k, 0]) for k in range(SEGS)]
-    spread = jnp.concatenate(
-        [part for k in range(SEGS) for part in (entry[k], jnp.zeros((8, W), F32))], axis=0
-    )
+    starts[SEGS] = moved(starts[SEGS - 1], powers[SEGS - 1, 4]) + ends[SEGS - 1 : SEGS]
+
+    def spread(first):
+        return jnp.concatenate([starts[first + k] for k in range(SEGS) for half in range(2)], axis=0)
+
+    entry = spread(0)
+    rows = inputs[...]
+    for step in range(4):
+        rows = seg_step(rows, powers, step, entry)
     row_at = lax.broadcasted_iota(jnp.int32, (ROWS, W), 0) % LEN
-    rows = inputs[...] + jnp.where(row_at == 0, spread, 0.0)
-    rows = seg_scan(rows, powers)
+    rows = jnp.where(row_at == LEN - 1, spread(1), rows)
     drive = times(wide(rows), drive_map[...])
     drives[0:ROWS] = drive
     last = jnp.broadcast_to(rows[ROWS - 1 : ROWS], (8, W))
@@ -389,7 +394,6 @@
         return (out[:W, :W] + out[:W, W:]) + (out[W:, :W] + out[W:, W:])
 
     upper = lax.broadcasted_iota(jnp.int32, (W, W), 0) - lax.broadcasted_iota(jnp.int32, (W, W), 1)
-    lag_gram = fold(jnp.dot(kept, packed, preferred_element_type=F32))
     lag_cross_t = fold(jnp.dot(kept, wide(following), preferred_element_type=F32))
     fl = flags[...]
     repeat = (
@@ -397,10 +401,9 @@
         == lax.broadcasted_iota(jnp.int32, (2 * SEGS, count), 1) // LEN
     )
     lane_flags = jnp.dot(fl.astype(F32).astype(BF16), repeat.astype(BF16), preferred_element_type=F32)
-    grams = []
-    for g in range(4):
-        masked_t = packed_t * lane_flags[g : g + 1].astype(BF16)
-        grams.append(fold(jnp.dot(masked_t, packed, preferred_element_type=F32)))
+    flagged = [packed_t * lane_flags[g : g + 1].astype(BF16) for g in range(4)]
+    product = jnp.dot(jnp.concatenate([kept] + flagged, axis=0), packed, preferred_element_type=F32)
+    lag_gram, *grams = [fold(product[2 * W * g : 2 * W * (g + 1)]) for g in range(5)]
     def diagonal(gram):
         return jnp.sum(jnp.where(upper == 0, gram, 0.0), axis=0, keepdims=True)
 
@@ -561,21 +564,21 @@
         where, telemetry, present, filter_gain, other_present
     )
     received = swap_core(theirs)
-    powers, tree, whole, gain_powers, gain_triples, drive_map = call(
+    powers, whole, gain_powers, gain_triples, drive_map = call(
         maps_kernel,
         [
-            shape(SEGS, 5, W, 2 * W, dtype=BF16), shape(SEGS - 1, W, 2 * W, dtype=BF16),
-            shape(2 * SEGS - 1, W, W), shape(16, W, 2 * W, dtype=BF16), shape(8, W, 2 * W, dtype=BF16),
-            shape(W, 2 * W, dtype=BF16),
+            shape(SEGS, 5, W, 2 * W, dtype=BF16), shape(SEGS, W, W), shape(16, W, 2 * W, dtype=BF16),
+            shape(8, W, 2 * W, dtype=BF16), shape(W, 2 * W, dtype=BF16),
         ],
         3, 6,
         scratch=[pltpu.VMEM((8, W, W), F32), pltpu.VMEM((W, W), F32)],
         far=(0, 1, 3, 5),
         far_scalars=(1,),
     )(where, present, other_present, transition, filter_gain, other_gain, sensing, other_sensing, smooth_gain)
-    inputs, ends, packed = call(
-        shift_kernel, [shape(ROWS, W), shape(32, W), shape(PACK, W)], 0, 5
-    )(mine, received, powers, tree, whole)
+    inputs, ends, packed, tree = call(
+        shift_kernel,
+        [shape(ROWS, W), shape(32, W), shape(PACK, W), shape(SEGS - 1, W, 2 * W, dtype=BF16)], 0, 4
+    )(mine, received, powers, whole)
 
     other_packed = swap_core(packed)
     (chip,) = call(pair_kernel, [shape(NEAR * PACK, W)], 1, 2)(where, packed, other_packed)

time: 116 us -> 114 us (0.983)
  Pallas kernels: 29.1 us -> 27.4 us
    pallas_call x10, Pallas kernels: 29.1 us -> 27.4 us  [placed(): return run(*scalars, *near)]
  transfers between devices with their start and end apart: 6 -> 6, of which waited for: 2 -> 2; matrix products, arithmetic and copies ran while one was open for 0% -> 0% of each run, Pallas kernels for 7% -> 6%
where the time goes in v8:
time: 114 us
  blocking collectives  82.8 us (73%)
  Pallas kernels  27.4 us (24%)
  waiting for transfers between devices  1.62 us (1%)
  starting transfers between devices  1.33 us (1%)
    all_to_all x5, blocking collectives, exchange(): lax.all_to_all(value, 'tm', 0, 0, axis_index_groups=groups, tiled=True)  69.5 us
    pallas_call x10, Pallas kernels, placed(): return run(*scalars, *near)  27.4 us
    all_to_all x1, blocking collectives, on_device(): gathered = lax.all_to_all(shift, ('tm', 'sens'), 0, 0, tiled=True)  13.3 us
  transfers between devices with their start and end apart: 6, of which 2 were waited for; matrix products, arithmetic and copies ran while one was open for 0% of the time, Pallas kernels for 6%

profile of v8, /device:TPU:0, one launch (start us, length us, event | category | flops | bytes accessed | tf_op | source)
XLA Modules:
  0.0 114.0 jit_solution(11016670546275574489)
XLA Ops:
  0.6 0.1 collective-permute-start
  0.7 0.5 collective-permute-start.3
  1.2 0.1 collective-permute-start.2
  1.3 0.1 pad_add_fusion.where
  1.4 0.7 collective-permute-done.unused.flags_other
  2.1 1.7 %shard_map.94 = (f32[256,128]{1,0:T(8,128)S(1)}, f32[256,128]{1,0:T(8,128)S(1)}) custom-call(s32[2]{0:T(128)S(1)} %pad_add_fusion.where, f32[512,256]{1,0:T(8,128)} %tel.3, s32[4,32]{1,0:T(4,128)} %bitcast.32, f32[128,256]{1,0:T(8,128)} %gain_own.1, s32[4,32]{1,0:T(4,128)S(1)} %collective-permute-done.unused.flags_other), custom_call_target="tpu_custom_call" | custom-call | tf_op jit(solution)/shard_map/pallas_call | solution.py:80
  3.8 0.0 copy-start.1
  3.8 0.0 copy-start.3
  3.8 0.3 collective-permute-start.1
  4.0 0.0 collective-permute-done.3.sense_other
  4.0 0.0 collective-permute-done.2.gain_other
  4.0 5.3 %shard_map.95 = (bf16[16,5,128,256]{3,2,1,0:T(8,128)(2,1)S(1)}, f32[16,128,128]{2,1,0:T(8,128)S(1)}, bf16[16,128,256]{2,1,0:T(8,128)(2,1)S(1)}, bf16[8,128,256]{2,1,0:T(8,128)(2,1)S(1)}, bf16[128,256]{1,0:T(8,128)(2,1)S(1)}) custom-call(s32[2]{0:T(128)S(1)} %pad_add_fusion.where, s32[4,32]{1,0:T(4,128)} %bitcast.33, ...), custom_call_target="tpu_custom_call" | custom-call | tf_op jit(solution)/shard_map/pallas_call | solution.py:80
  9.3 0.0 collective-permute-done.1.received
  9.4 2.0 %shard_map.96 = (f32[256,128]{1,0:T(8,128)S(1)}, f32[32,128]{1,0:T(8,128)S(1)}, f32[136,128]{1,0:T(8,128)S(1)}, bf16[15,128,256]{2,1,0:T(8,128)(2,1)S(1)}) custom-call(f32[256,128]{1,0:T(8,128)S(1)} %get-tuple-element.22.mine, f32[256,128]{1,0:T(8,128)S(1)} %collective-permute-done.1.received, bf16[16,5,128,256]{3,2,1,0:T(8,128)(2,1)S(1)} %get-tuple-element.24.powers, ...), custom_call_target="tpu_custom_call" | custom-call | tf_op jit(solution)/shard_map/pallas_call | solution.py:80
  11.4 0.4 collective-permute-start.4
  11.7 0.9 collective-permute-done.4.other.c1
  12.7 0.7 shard_map.97
  13.4 16.7 %all_to_all.66 = f32[8,136,128]{2,1,0:T(8,128)S(1)} all-to-all(f32[8,136,128]{2,1,0:T(8,128)S(1)} %bitcast.21), channel_id=1, replica_groups={{0,2,4,6,8,10,12,14},{16,18,20,22,24,26,28,30},{32,34,36,38,40,42,44,46..., dimensions={0} | all-to-all | bytes 1114112 | tf_op jit(solution)/shard_map/all_to_all | solution.py:554
  30.1 0.7 shard_map.98
  30.7 0.0 copy-start
  30.7 0.0 copy-start.2
  30.8 19.1 %all_to_all.67 = f32[8,136,128]{2,1,0:T(8,128)S(1)} all-to-all(f32[8,136,128]{2,1,0:T(8,128)S(1)} %bitcast.25), channel_id=1, replica_groups={{0,16,32,48,64,80,96,112},{2,18,34,50,66,82,98,114},{4,20,36,52,68,84,1..., dimensions={0} | all-to-all | bytes 1114112 | tf_op jit(solution)/shard_map/all_to_all | solution.py:554
  49.9 0.0 copy-done.1
  49.9 0.0 copy-done.3
  49.9 4.2 %shard_map.99 = (f32[264,128]{1,0:T(8,128)S(1)}, f32[128,128]{1,0:T(8,128)S(1)}) custom-call(s32[2]{0:T(128)S(1)} %pad_add_fusion.where, f32[1088,128]{1,0:T(8,128)S(1)} %bitcast.20, f32[1088,128]{1,0:T(8,128)S(1)} %bitcast.19, f32[3,136,128]{2,1,0:T(8,128)S(1)} %get-tuple-element.28.early, f32[136,128]{1,0:T(8,128)S(1)} %collective-permute-done.4.other.c1, ...), custom_call_target="tpu_custom_call" | custom-call | tf_op jit(solution)/shard_map/pallas_call | solution.py:80
  54.1 0.0 collective-permute-start.5
  54.2 13.3 %all_to_all.68 = f32[128,1,128]{2,1,0:T(1,128)S(1)} all-to-all(f32[128,1,128]{2,1,0:T(1,128)S(1)} %bitcast.30), channel_id=1, replica_groups=mesh['tm'=64,'sens'=2] {'tm','sens'}, dimensions={0} | all-to-all | bytes 131072 | tf_op jit(solution)/shard_map/all_to_all | solution.py:595
  67.4 0.0 collective-permute-done.5.other
  67.5 0.0 copy-done
  67.5 0.0 copy-done.2
  67.5 4.0 %shard_map.100 = (f32[512,128]{1,0:T(8,128)}, f32[768,128]{1,0:T(8,128)S(1)}) custom-call(s32[2]{0:T(128)S(1)} %pad_add_fusion.where, f32[128,128]{1,0:T(8,128)S(1)} %bitcast.29, f32[264,128]{1,0:T(8,128)S(1)} %get-tuple-element.36.own, f32[264,128]{1,0:T(8,128)S(1)} %collective-permute-done.5.other, ...), custom_call_target="tpu_custom_call" | custom-call | tf_op jit(solution)/shard_map/pallas_call | solution.py:80
  71.5 13.3 %all_to_all.69 = f32[16,48,128]{2,1,0:T(8,128)S(1)} all-to-all(f32[16,48,128]{2,1,0:T(8,128)S(1)} %bitcast.26), channel_id=1, replica_groups={{0,2,4,6,8,10,12,14,16,18,20,22,24,26,28,30},{32,34,36,38,40,42,44,46,4..., dimensions={0} | all-to-all | bytes 786432 | tf_op jit(solution)/shard_map/all_to_all | solution.py:554
  84.8 8.2 %all_to_all.70 = f32[4,48,128]{2,1,0:T(8,128)S(1)} all-to-all(f32[4,48,128]{2,1,0:T(8,128)S(1)} %bitcast.27), channel_id=1, replica_groups={{0,32,64,96},{2,34,66,98},{4,36,68,100},{6,38,70,102},{8,40,72,104},{10..., dimensions={0} | all-to-all | bytes 196608 | tf_op jit(solution)/shard_map/all_to_all | solution.py:554
  93.0 12.3 %all_to_all.71 = f32[16,48,128]{2,1,0:T(8,128)S(1)} all-to-all(f32[16,48,128]{2,1,0:T(8,128)S(1)} %bitcast.24), channel_id=1, replica_groups={{0,2,4,6,8,10,12,14,16,18,20,22,24,26,28,30},{32,34,36,38,40,42,44,46,4..., dimensions={0} | all-to-all | bytes 786432 | tf_op jit(solution)/shard_map/all_to_all | solution.py:554
  105.3 8.7 %shard_map.103 = (f32[128,128]{1,0:T(8,128)}, f32[256,128]{1,0:T(8,128)}) custom-call(f32[768,128]{1,0:T(8,128)S(1)} %bitcast.22), custom_call_target="tpu_custom_call" | custom-call | tf_op jit(solution)/shard_map/pallas_call | solution.py:80
  (2 shorter events, 0.1 us)
Async XLA Ops:
  0.6 1.4 %collective-permute-start = (s32[4,32]{1,0:T(4,128)}, s32[4,32]{1,0:T(4,128)S(1)}, u32[]{:S(2)}, u32[]{:S(2)}) collective-permute-start(s32[4,32]{1,0:T(4,128)} %bitcast.31), channel_id=1, source_target_pairs={{0,1},{1,0},{2,3},{3,2},{4,5},{5,4},{6,7},{7,6},{8,9},{9,8},{10,11... | collective-permute-start | bytes 1544 | tf_op jit(solution)/shard_map/ppermute | solution.py:545
  0.7 3.3 %collective-permute-start.3 = (f32[256,128]{1,0:T(8,128)}, f32[256,128]{1,0:T(8,128)S(1)}, u32[]{:S(2)}, u32[]{:S(2)}) collective-permute-start(f32[256,128]{1,0:T(8,128)} %sense_own.1), channel_id=1, source_target_pairs={{0,1},{1,0},{2,3},{3,2},{4,5},{5,4},{6,7},{7,6},{8,9},{9,8},{10,11... | collective-permute-start | bytes 393224 | tf_op jit(solution)/shard_map/ppermute | solution.py:545
  1.2 2.8 %collective-permute-start.2 = (f32[128,256]{1,0:T(8,128)}, f32[128,256]{1,0:T(8,128)S(1)}, u32[]{:S(2)}, u32[]{:S(2)}) collective-permute-start(f32[128,256]{1,0:T(8,128)} %gain_own.1), channel_id=1, source_target_pairs={{0,1},{1,0},{2,3},{3,2},{4,5},{5,4},{6,7},{7,6},{8,9},{9,8},{10,11... | collective-permute-start | bytes 393224 | tf_op jit(solution)/shard_map/ppermute | solution.py:545
  3.8 46.1 %copy-start.1 = (f32[128,128]{1,0:T(8,128)S(1)}, f32[128,128]{1,0:T(8,128)}, u32[]{:S(2)}) copy-start(f32[128,128]{1,0:T(8,128)} %trans.3) | copy-start | bytes 196612
  3.8 46.1 %copy-start.3 = (f32[128]{0:T(128)S(1)}, f32[128]{0:T(128)}, u32[]{:S(2)}) copy-start(f32[128]{0:T(128)} %param.13) | copy-start | bytes 1540
  3.8 5.6 %collective-permute-start.1 = (f32[256,128]{1,0:T(8,128)S(1)}, f32[256,128]{1,0:T(8,128)S(1)}, u32[]{:S(2)}, u32[]{:S(2)}) collective-permute-start(f32[256,128]{1,0:T(8,128)S(1)} %get-tuple-element.23), channel_id=1, source_target_pairs={{0,1},{1,0},{2,3},{3,2},{4,5},{5,4},{6,7},{7,6},{8,9},{9,8},{10,11... | collective-permute-start | bytes 393224 | tf_op jit(solution)/shard_map/ppermute | solution.py:545
  11.4 1.3 %collective-permute-start.4 = (f32[136,128]{1,0:T(8,128)S(1)}, f32[136,128]{1,0:T(8,128)S(1)}, u32[]{:S(2)}, u32[]{:S(2)}) collective-permute-start(f32[136,128]{1,0:T(8,128)S(1)} %get-tuple-element.26.own), channel_id=1, source_target_pairs={{0,1},{1,0},{2,3},{3,2},{4,5},{5,4},{6,7},{7,6},{8,9},{9,8},{10,11... | collective-permute-start | bytes 208904 | tf_op jit(solution)/shard_map/ppermute | solution.py:545
  30.7 36.7 %copy-start = (f32[512,256]{1,0:T(8,128)S(1)}, f32[512,256]{1,0:T(8,128)}, u32[]{:S(2)}) copy-start(f32[512,256]{1,0:T(8,128)} %tel.3) | copy-start | bytes 1572868
  30.7 36.7 %copy-start.2 = (s32[32,4]{0,1:T(4,128)S(1)}, s32[32,4]{0,1:T(4,128)}, u32[]{:S(2)}) copy-start(s32[32,4]{0,1:T(4,128)} %param.8) | copy-start | bytes 1540
  54.1 13.3 %collective-permute-start.5 = (f32[264,128]{1,0:T(8,128)S(1)}, f32[264,128]{1,0:T(8,128)S(1)}, u32[]{:S(2)}, u32[]{:S(2)}) collective-permute-start(f32[264,128]{1,0:T(8,128)S(1)} %get-tuple-element.36.own), channel_id=1, source_target_pairs={{0,1},{1,0},{2,3},{3,2},{4,5},{5,4},{6,7},{7,6},{8,9},{9,8},{10,11... | collective-permute-start | bytes 405512 | tf_op jit(solution)/shard_map/ppermute | solution.py:545

commit v9 on v8

--- a/solution.py
+++ b/solution.py
@@ -461,18 +461,17 @@
     unit, pivots = 32, 8
     lane = lax.broadcasted_iota(jnp.int32, (W, W), 1)
     lane_tile = lane[:8]
-    lane_head = lane[:unit]
-    row_head = lax.broadcasted_iota(jnp.int32, (unit, W), 0)
     sublane = lax.broadcasted_iota(jnp.int32, (8, W), 0)
 
     def panel(b, held):
-        heads = [m[:unit] for m in held]
-        for j in range(0, unit, pivots):
+        heads = [[m[t : t + 8] for t in range(0, unit, 8)] for m in held]
+        for here in range(unit // pivots):
+            j = here * pivots
             stacked = []
             for r in range(pivots):
-                rows = jnp.broadcast_to(heads[0][j + r : j + r + 1], (8, W))
+                rows = jnp.broadcast_to(heads[0][here][r : r + 1], (8, W))
                 for p in range(1, len(heads)):
-                    mine = jnp.broadcast_to(heads[p][j + r : j + r + 1], (8, W))
+                    mine = jnp.broadcast_to(heads[p][here][r : r + 1], (8, W))
                     rows = jnp.where(sublane == p, mine, rows)
                 stacked.append(rows)
             entry = [[None] * pivots for _ in range(pivots)]
@@ -489,20 +488,21 @@
                 for c in range(pivots):
                     total = jnp.where(lane_tile == j + c, entry[r][c], total)
                 fresh.append(-total)
-            for p, head in enumerate(heads):
-                rows = [
-                    jnp.concatenate([jnp.broadcast_to(row[p : p + 1], (8, W))] * (unit // 8), axis=0)
-                    for row in fresh
-                ]
-                after = jnp.where(lane_head // pivots == j // pivots, 0.0, head)
-                for r in range(pivots):
-                    after = after - jnp.broadcast_to(head[:, j + r : j + r + 1], (unit, W)) * rows[r]
-                for r in range(pivots):
-                    after = jnp.where(row_head == j + r, rows[r], after)
-                heads[p] = after
+            for p, tiles in enumerate(heads):
+                rows = [jnp.broadcast_to(row[p : p + 1], (8, W)) for row in fresh]
+                for t, tile in enumerate(tiles):
+                    if t == here:
+                        after = rows[0]
+                        for r in range(1, pivots):
+                            after = jnp.where(sublane == r, rows[r], after)
+                    else:
+                        after = jnp.where(lane_tile // pivots == here, 0.0, tile)
+                        for r in range(pivots):
+                            after = after - jnp.broadcast_to(tile[:, j + r : j + r + 1], (8, W)) * rows[r]
+                    tiles[t] = after
         turned = []
-        for head, m in zip(heads, held):
-            rest = m[unit:]
+        for tiles, m in zip(heads, held):
+            head, rest = jnp.concatenate(tiles, axis=0), m[unit:]
             rest = jnp.where(lane[unit:] < unit, 0.0, rest) - exact(rest[:, :unit], head)
             turned.append(pltpu.roll(jnp.concatenate([rest, head], axis=0), W - unit, 1))
         return tuple(turned)

time: 114 us -> 114 us (level)
  no operation moved by 1% of the time
where the time goes in v9:
time: 114 us; the launch traced here: 113 us
  blocking collectives  82.8 us (73%)
  Pallas kernels  26.8 us (24%)
  waiting for transfers between devices  1.62 us (1%)
  starting transfers between devices  1.33 us (1%)
    all_to_all x5, blocking collectives, exchange(): lax.all_to_all(value, 'tm', 0, 0, axis_index_groups=groups, tiled=True)  69.5 us
    pallas_call x10, Pallas kernels, placed(): return run(*scalars, *near)  26.8 us
    all_to_all x1, blocking collectives, on_device(): gathered = lax.all_to_all(shift, ('tm', 'sens'), 0, 0, tiled=True)  13.3 us
  transfers between devices with their start and end apart: 6, of which 2 were waited for; matrix products, arithmetic and copies ran while one was open for 0% of the time, Pallas kernels for 6%

profile of v9, /device:TPU:0, one launch (start us, length us, event | category | flops | bytes accessed | tf_op | source)
XLA Modules:
  0.0 113.4 jit_solution(17212393105985433502)
XLA Ops:
  0.6 0.1 collective-permute-start
  0.7 0.5 collective-permute-start.3
  1.2 0.1 collective-permute-start.2
  1.3 0.1 pad_add_fusion.where
  1.4 0.7 collective-permute-done.unused.flags_other
  2.1 1.7 %shard_map.94 = (f32[256,128]{1,0:T(8,128)S(1)}, f32[256,128]{1,0:T(8,128)S(1)}) custom-call(s32[2]{0:T(128)S(1)} %pad_add_fusion.where, f32[512,256]{1,0:T(8,128)} %tel.3, s32[4,32]{1,0:T(4,128)} %bitcast.32, f32[128,256]{1,0:T(8,128)} %gain_own.1, s32[4,32]{1,0:T(4,128)S(1)} %collective-permute-done.unused.flags_other), custom_call_target="tpu_custom_call" | custom-call | tf_op jit(solution)/shard_map/pallas_call | solution.py:80
  3.8 0.0 copy-start.1
  3.8 0.0 copy-start.3
  3.8 0.3 collective-permute-start.1
  4.0 0.0 collective-permute-done.3.sense_other
  4.0 0.0 collective-permute-done.2.gain_other
  4.0 5.3 %shard_map.95 = (bf16[16,5,128,256]{3,2,1,0:T(8,128)(2,1)S(1)}, f32[16,128,128]{2,1,0:T(8,128)S(1)}, bf16[16,128,256]{2,1,0:T(8,128)(2,1)S(1)}, bf16[8,128,256]{2,1,0:T(8,128)(2,1)S(1)}, bf16[128,256]{1,0:T(8,128)(2,1)S(1)}) custom-call(s32[2]{0:T(128)S(1)} %pad_add_fusion.where, s32[4,32]{1,0:T(4,128)} %bitcast.33, ...), custom_call_target="tpu_custom_call" | custom-call | tf_op jit(solution)/shard_map/pallas_call | solution.py:80
  9.3 0.0 collective-permute-done.1.received
  9.4 2.0 %shard_map.96 = (f32[256,128]{1,0:T(8,128)S(1)}, f32[32,128]{1,0:T(8,128)S(1)}, f32[136,128]{1,0:T(8,128)S(1)}, bf16[15,128,256]{2,1,0:T(8,128)(2,1)S(1)}) custom-call(f32[256,128]{1,0:T(8,128)S(1)} %get-tuple-element.22.mine, f32[256,128]{1,0:T(8,128)S(1)} %collective-permute-done.1.received, bf16[16,5,128,256]{3,2,1,0:T(8,128)(2,1)S(1)} %get-tuple-element.24.powers, ...), custom_call_target="tpu_custom_call" | custom-call | tf_op jit(solution)/shard_map/pallas_call | solution.py:80
  11.4 0.4 collective-permute-start.4
  11.7 0.9 collective-permute-done.4.other.c1
  12.7 0.7 shard_map.97
  13.4 16.7 %all_to_all.66 = f32[8,136,128]{2,1,0:T(8,128)S(1)} all-to-all(f32[8,136,128]{2,1,0:T(8,128)S(1)} %bitcast.21), channel_id=1, replica_groups={{0,2,4,6,8,10,12,14},{16,18,20,22,24,26,28,30},{32,34,36,38,40,42,44,46..., dimensions={0} | all-to-all | bytes 1114112 | tf_op jit(solution)/shard_map/all_to_all | solution.py:554
  30.1 0.7 shard_map.98
  30.7 0.0 copy-start
  30.7 0.0 copy-start.2
  30.8 19.1 %all_to_all.67 = f32[8,136,128]{2,1,0:T(8,128)S(1)} all-to-all(f32[8,136,128]{2,1,0:T(8,128)S(1)} %bitcast.25), channel_id=1, replica_groups={{0,16,32,48,64,80,96,112},{2,18,34,50,66,82,98,114},{4,20,36,52,68,84,1..., dimensions={0} | all-to-all | bytes 1114112 | tf_op jit(solution)/shard_map/all_to_all | solution.py:554
  49.9 0.0 copy-done.1
  49.9 0.0 copy-done.3
  49.9 4.2 %shard_map.99 = (f32[264,128]{1,0:T(8,128)S(1)}, f32[128,128]{1,0:T(8,128)S(1)}) custom-call(s32[2]{0:T(128)S(1)} %pad_add_fusion.where, f32[1088,128]{1,0:T(8,128)S(1)} %bitcast.20, f32[1088,128]{1,0:T(8,128)S(1)} %bitcast.19, f32[3,136,128]{2,1,0:T(8,128)S(1)} %get-tuple-element.28.early, f32[136,128]{1,0:T(8,128)S(1)} %collective-permute-done.4.other.c1, ...), custom_call_target="tpu_custom_call" | custom-call | tf_op jit(solution)/shard_map/pallas_call | solution.py:80
  54.1 0.0 collective-permute-start.5
  54.2 13.3 %all_to_all.68 = f32[128,1,128]{2,1,0:T(1,128)S(1)} all-to-all(f32[128,1,128]{2,1,0:T(1,128)S(1)} %bitcast.30), channel_id=1, replica_groups=mesh['tm'=64,'sens'=2] {'tm','sens'}, dimensions={0} | all-to-all | bytes 131072 | tf_op jit(solution)/shard_map/all_to_all | solution.py:595
  67.4 0.0 collective-permute-done.5.other
  67.5 0.0 copy-done
  67.5 0.0 copy-done.2
  67.5 4.0 %shard_map.100 = (f32[512,128]{1,0:T(8,128)}, f32[768,128]{1,0:T(8,128)S(1)}) custom-call(s32[2]{0:T(128)S(1)} %pad_add_fusion.where, f32[128,128]{1,0:T(8,128)S(1)} %bitcast.29, f32[264,128]{1,0:T(8,128)S(1)} %get-tuple-element.36.own, f32[264,128]{1,0:T(8,128)S(1)} %collective-permute-done.5.other, ...), custom_call_target="tpu_custom_call" | custom-call | tf_op jit(solution)/shard_map/pallas_call | solution.py:80
  71.5 13.3 %all_to_all.69 = f32[16,48,128]{2,1,0:T(8,128)S(1)} all-to-all(f32[16,48,128]{2,1,0:T(8,128)S(1)} %bitcast.26), channel_id=1, replica_groups={{0,2,4,6,8,10,12,14,16,18,20,22,24,26,28,30},{32,34,36,38,40,42,44,46,4..., dimensions={0} | all-to-all | bytes 786432 | tf_op jit(solution)/shard_map/all_to_all | solution.py:554
  84.8 8.2 %all_to_all.70 = f32[4,48,128]{2,1,0:T(8,128)S(1)} all-to-all(f32[4,48,128]{2,1,0:T(8,128)S(1)} %bitcast.27), channel_id=1, replica_groups={{0,32,64,96},{2,34,66,98},{4,36,68,100},{6,38,70,102},{8,40,72,104},{10..., dimensions={0} | all-to-all | bytes 196608 | tf_op jit(solution)/shard_map/all_to_all | solution.py:554
  93.0 12.3 %all_to_all.71 = f32[16,48,128]{2,1,0:T(8,128)S(1)} all-to-all(f32[16,48,128]{2,1,0:T(8,128)S(1)} %bitcast.24), channel_id=1, replica_groups={{0,2,4,6,8,10,12,14,16,18,20,22,24,26,28,30},{32,34,36,38,40,42,44,46,4..., dimensions={0} | all-to-all | bytes 786432 | tf_op jit(solution)/shard_map/all_to_all | solution.py:554
  105.3 8.1 %shard_map.103 = (f32[128,128]{1,0:T(8,128)}, f32[256,128]{1,0:T(8,128)}) custom-call(f32[768,128]{1,0:T(8,128)S(1)} %bitcast.22), custom_call_target="tpu_custom_call" | custom-call | tf_op jit(solution)/shard_map/pallas_call | solution.py:80
  (2 shorter events, 0.1 us)
Async XLA Ops:
  0.6 1.4 %collective-permute-start = (s32[4,32]{1,0:T(4,128)}, s32[4,32]{1,0:T(4,128)S(1)}, u32[]{:S(2)}, u32[]{:S(2)}) collective-permute-start(s32[4,32]{1,0:T(4,128)} %bitcast.31), channel_id=1, source_target_pairs={{0,1},{1,0},{2,3},{3,2},{4,5},{5,4},{6,7},{7,6},{8,9},{9,8},{10,11... | collective-permute-start | bytes 1544 | tf_op jit(solution)/shard_map/ppermute | solution.py:545
  0.7 3.3 %collective-permute-start.3 = (f32[256,128]{1,0:T(8,128)}, f32[256,128]{1,0:T(8,128)S(1)}, u32[]{:S(2)}, u32[]{:S(2)}) collective-permute-start(f32[256,128]{1,0:T(8,128)} %sense_own.1), channel_id=1, source_target_pairs={{0,1},{1,0},{2,3},{3,2},{4,5},{5,4},{6,7},{7,6},{8,9},{9,8},{10,11... | collective-permute-start | bytes 393224 | tf_op jit(solution)/shard_map/ppermute | solution.py:545
  1.2 2.8 %collective-permute-start.2 = (f32[128,256]{1,0:T(8,128)}, f32[128,256]{1,0:T(8,128)S(1)}, u32[]{:S(2)}, u32[]{:S(2)}) collective-permute-start(f32[128,256]{1,0:T(8,128)} %gain_own.1), channel_id=1, source_target_pairs={{0,1},{1,0},{2,3},{3,2},{4,5},{5,4},{6,7},{7,6},{8,9},{9,8},{10,11... | collective-permute-start | bytes 393224 | tf_op jit(solution)/shard_map/ppermute | solution.py:545
  3.8 46.1 %copy-start.1 = (f32[128,128]{1,0:T(8,128)S(1)}, f32[128,128]{1,0:T(8,128)}, u32[]{:S(2)}) copy-start(f32[128,128]{1,0:T(8,128)} %trans.3) | copy-start | bytes 196612
  3.8 46.1 %copy-start.3 = (f32[128]{0:T(128)S(1)}, f32[128]{0:T(128)}, u32[]{:S(2)}) copy-start(f32[128]{0:T(128)} %param.13) | copy-start | bytes 1540
  3.8 5.6 %collective-permute-start.1 = (f32[256,128]{1,0:T(8,128)S(1)}, f32[256,128]{1,0:T(8,128)S(1)}, u32[]{:S(2)}, u32[]{:S(2)}) collective-permute-start(f32[256,128]{1,0:T(8,128)S(1)} %get-tuple-element.23), channel_id=1, source_target_pairs={{0,1},{1,0},{2,3},{3,2},{4,5},{5,4},{6,7},{7,6},{8,9},{9,8},{10,11... | collective-permute-start | bytes 393224 | tf_op jit(solution)/shard_map/ppermute | solution.py:545
  11.4 1.3 %collective-permute-start.4 = (f32[136,128]{1,0:T(8,128)S(1)}, f32[136,128]{1,0:T(8,128)S(1)}, u32[]{:S(2)}, u32[]{:S(2)}) collective-permute-start(f32[136,128]{1,0:T(8,128)S(1)} %get-tuple-element.26.own), channel_id=1, source_target_pairs={{0,1},{1,0},{2,3},{3,2},{4,5},{5,4},{6,7},{7,6},{8,9},{9,8},{10,11... | collective-permute-start | bytes 208904 | tf_op jit(solution)/shard_map/ppermute | solution.py:545
  30.7 36.7 %copy-start = (f32[512,256]{1,0:T(8,128)S(1)}, f32[512,256]{1,0:T(8,128)}, u32[]{:S(2)}) copy-start(f32[512,256]{1,0:T(8,128)} %tel.3) | copy-start | bytes 1572868
  30.7 36.7 %copy-start.2 = (s32[32,4]{0,1:T(4,128)S(1)}, s32[32,4]{0,1:T(4,128)}, u32[]{:S(2)}) copy-start(s32[32,4]{0,1:T(4,128)} %param.8) | copy-start | bytes 1540
  54.1 13.3 %collective-permute-start.5 = (f32[264,128]{1,0:T(8,128)S(1)}, f32[264,128]{1,0:T(8,128)S(1)}, u32[]{:S(2)}, u32[]{:S(2)}) collective-permute-start(f32[264,128]{1,0:T(8,128)S(1)} %get-tuple-element.36.own), channel_id=1, source_target_pairs={{0,1},{1,0},{2,3},{3,2},{4,5},{5,4},{6,7},{7,6},{8,9},{9,8},{10,11... | collective-permute-start | bytes 405512 | tf_op jit(solution)/shard_map/ppermute | solution.py:545

commit v10 on v9

--- a/solution.py
+++ b/solution.py
@@ -314,15 +314,17 @@
     device, core = where[0], where[1]
     level = split_maps(far)
     pairs = [joined(level[2 * p], level[2 * p + 1]) for p in range(3)]
+    inner = stages(device % NEAR, near, early)
+    inner.append(masked(core == 1, c1[...]))
+    inner = joined(inner[0], inner[1]), joined(inner[2], inner[3])
     for slot, (dev, row) in enumerate((joined(pairs[0], pairs[1]), pairs[0], pairs[2])):
         far_early[slot, 0:W] = dev
         far_early[slot, W:PACK] = row
+    inner = joined(*inner)
     state = jnp.broadcast_to(initial[...], (8, W))
     for stage in stages(device // NEAR, far, far_early):
         state = after_map(state, stage)
-    inner = stages(device % NEAR, near, early)
-    inner.append(masked(core == 1, c1[...]))
-    state = after_map(state, joined(joined(inner[0], inner[1]), joined(inner[2], inner[3])))
+    state = after_map(state, inner)
     starts = {0: state}
     for span, maps_at, ends_at in ((8, 12, 28), (4, 8, 24), (2, 0, 16), (1, -1, 0)):
         for begin in range(0, SEGS, 2 * span):

time: 114 us -> 114 us (level)
  no operation moved by 1% of the time
where the time goes in v10:
time: 114 us; the launch traced here: 113 us
  blocking collectives  82.8 us (73%)
  Pallas kernels  26.7 us (23%)
  waiting for transfers between devices  1.62 us (1%)
  starting transfers between devices  1.33 us (1%)
    all_to_all x5, blocking collectives, exchange(): lax.all_to_all(value, 'tm', 0, 0, axis_index_groups=groups, tiled=True)  69.5 us
    pallas_call x10, Pallas kernels, placed(): return run(*scalars, *near)  26.7 us
    all_to_all x1, blocking collectives, on_device(): gathered = lax.all_to_all(shift, ('tm', 'sens'), 0, 0, tiled=True)  13.3 us
  transfers between devices with their start and end apart: 6, of which 2 were waited for; matrix products, arithmetic and copies ran while one was open for 0% of the time, Pallas kernels for 6%

profile of v10, /device:TPU:0, one launch (start us, length us, event | category | flops | bytes accessed | tf_op | source)
XLA Modules:
  0.0 113.3 jit_solution(10102277916903806168)
XLA Ops:
  0.6 0.1 collective-permute-start
  0.7 0.5 collective-permute-start.3
  1.2 0.1 collective-permute-start.2
  1.3 0.1 pad_add_fusion.where
  1.4 0.7 collective-permute-done.unused.flags_other
  2.1 1.7 %shard_map.94 = (f32[256,128]{1,0:T(8,128)S(1)}, f32[256,128]{1,0:T(8,128)S(1)}) custom-call(s32[2]{0:T(128)S(1)} %pad_add_fusion.where, f32[512,256]{1,0:T(8,128)} %tel.3, s32[4,32]{1,0:T(4,128)} %bitcast.32, f32[128,256]{1,0:T(8,128)} %gain_own.1, s32[4,32]{1,0:T(4,128)S(1)} %collective-permute-done.unused.flags_other), custom_call_target="tpu_custom_call" | custom-call | tf_op jit(solution)/shard_map/pallas_call | solution.py:80
  3.8 0.0 copy-start.1
  3.8 0.0 copy-start.3
  3.8 0.3 collective-permute-start.1
  4.0 0.0 collective-permute-done.3.sense_other
  4.0 0.0 collective-permute-done.2.gain_other
  4.0 5.3 %shard_map.95 = (bf16[16,5,128,256]{3,2,1,0:T(8,128)(2,1)S(1)}, f32[16,128,128]{2,1,0:T(8,128)S(1)}, bf16[16,128,256]{2,1,0:T(8,128)(2,1)S(1)}, bf16[8,128,256]{2,1,0:T(8,128)(2,1)S(1)}, bf16[128,256]{1,0:T(8,128)(2,1)S(1)}) custom-call(s32[2]{0:T(128)S(1)} %pad_add_fusion.where, s32[4,32]{1,0:T(4,128)} %bitcast.33, ...), custom_call_target="tpu_custom_call" | custom-call | tf_op jit(solution)/shard_map/pallas_call | solution.py:80
  9.3 0.0 collective-permute-done.1.received
  9.4 2.0 %shard_map.96 = (f32[256,128]{1,0:T(8,128)S(1)}, f32[32,128]{1,0:T(8,128)S(1)}, f32[136,128]{1,0:T(8,128)S(1)}, bf16[15,128,256]{2,1,0:T(8,128)(2,1)S(1)}) custom-call(f32[256,128]{1,0:T(8,128)S(1)} %get-tuple-element.22.mine, f32[256,128]{1,0:T(8,128)S(1)} %collective-permute-done.1.received, bf16[16,5,128,256]{3,2,1,0:T(8,128)(2,1)S(1)} %get-tuple-element.24.powers, ...), custom_call_target="tpu_custom_call" | custom-call | tf_op jit(solution)/shard_map/pallas_call | solution.py:80
  11.4 0.4 collective-permute-start.4
  11.7 0.9 collective-permute-done.4.other.c1
  12.7 0.7 shard_map.97
  13.4 16.7 %all_to_all.66 = f32[8,136,128]{2,1,0:T(8,128)S(1)} all-to-all(f32[8,136,128]{2,1,0:T(8,128)S(1)} %bitcast.21), channel_id=1, replica_groups={{0,2,4,6,8,10,12,14},{16,18,20,22,24,26,28,30},{32,34,36,38,40,42,44,46..., dimensions={0} | all-to-all | bytes 1114112 | tf_op jit(solution)/shard_map/all_to_all | solution.py:556
  30.1 0.7 shard_map.98
  30.7 0.0 copy-start
  30.7 0.0 copy-start.2
  30.8 19.1 %all_to_all.67 = f32[8,136,128]{2,1,0:T(8,128)S(1)} all-to-all(f32[8,136,128]{2,1,0:T(8,128)S(1)} %bitcast.25), channel_id=1, replica_groups={{0,16,32,48,64,80,96,112},{2,18,34,50,66,82,98,114},{4,20,36,52,68,84,1..., dimensions={0} | all-to-all | bytes 1114112 | tf_op jit(solution)/shard_map/all_to_all | solution.py:556
  49.9 0.0 copy-done.1
  49.9 0.0 copy-done.3
  49.9 4.1 %shard_map.99 = (f32[264,128]{1,0:T(8,128)S(1)}, f32[128,128]{1,0:T(8,128)S(1)}) custom-call(s32[2]{0:T(128)S(1)} %pad_add_fusion.where, f32[1088,128]{1,0:T(8,128)S(1)} %bitcast.20, f32[1088,128]{1,0:T(8,128)S(1)} %bitcast.19, f32[3,136,128]{2,1,0:T(8,128)S(1)} %get-tuple-element.28.early, f32[136,128]{1,0:T(8,128)S(1)} %collective-permute-done.4.other.c1, ...), custom_call_target="tpu_custom_call" | custom-call | tf_op jit(solution)/shard_map/pallas_call | solution.py:80
  54.0 0.0 collective-permute-start.5
  54.0 13.3 %all_to_all.68 = f32[128,1,128]{2,1,0:T(1,128)S(1)} all-to-all(f32[128,1,128]{2,1,0:T(1,128)S(1)} %bitcast.30), channel_id=1, replica_groups=mesh['tm'=64,'sens'=2] {'tm','sens'}, dimensions={0} | all-to-all | bytes 131072 | tf_op jit(solution)/shard_map/all_to_all | solution.py:597
  67.3 0.0 collective-permute-done.5.other
  67.3 0.0 copy-done
  67.3 0.0 copy-done.2
  67.3 4.0 %shard_map.100 = (f32[512,128]{1,0:T(8,128)}, f32[768,128]{1,0:T(8,128)S(1)}) custom-call(s32[2]{0:T(128)S(1)} %pad_add_fusion.where, f32[128,128]{1,0:T(8,128)S(1)} %bitcast.29, f32[264,128]{1,0:T(8,128)S(1)} %get-tuple-element.36.own, f32[264,128]{1,0:T(8,128)S(1)} %collective-permute-done.5.other, ...), custom_call_target="tpu_custom_call" | custom-call | tf_op jit(solution)/shard_map/pallas_call | solution.py:80
  71.3 13.3 %all_to_all.69 = f32[16,48,128]{2,1,0:T(8,128)S(1)} all-to-all(f32[16,48,128]{2,1,0:T(8,128)S(1)} %bitcast.26), channel_id=1, replica_groups={{0,2,4,6,8,10,12,14,16,18,20,22,24,26,28,30},{32,34,36,38,40,42,44,46,4..., dimensions={0} | all-to-all | bytes 786432 | tf_op jit(solution)/shard_map/all_to_all | solution.py:556
  84.6 8.2 %all_to_all.70 = f32[4,48,128]{2,1,0:T(8,128)S(1)} all-to-all(f32[4,48,128]{2,1,0:T(8,128)S(1)} %bitcast.27), channel_id=1, replica_groups={{0,32,64,96},{2,34,66,98},{4,36,68,100},{6,38,70,102},{8,40,72,104},{10..., dimensions={0} | all-to-all | bytes 196608 | tf_op jit(solution)/shard_map/all_to_all | solution.py:556
  92.8 12.3 %all_to_all.71 = f32[16,48,128]{2,1,0:T(8,128)S(1)} all-to-all(f32[16,48,128]{2,1,0:T(8,128)S(1)} %bitcast.24), channel_id=1, replica_groups={{0,2,4,6,8,10,12,14,16,18,20,22,24,26,28,30},{32,34,36,38,40,42,44,46,4..., dimensions={0} | all-to-all | bytes 786432 | tf_op jit(solution)/shard_map/all_to_all | solution.py:556
  105.1 8.1 %shard_map.103 = (f32[128,128]{1,0:T(8,128)}, f32[256,128]{1,0:T(8,128)}) custom-call(f32[768,128]{1,0:T(8,128)S(1)} %bitcast.22), custom_call_target="tpu_custom_call" | custom-call | tf_op jit(solution)/shard_map/pallas_call | solution.py:80
  (2 shorter events, 0.1 us)
Async XLA Ops:
  0.6 1.4 %collective-permute-start = (s32[4,32]{1,0:T(4,128)}, s32[4,32]{1,0:T(4,128)S(1)}, u32[]{:S(2)}, u32[]{:S(2)}) collective-permute-start(s32[4,32]{1,0:T(4,128)} %bitcast.31), channel_id=1, source_target_pairs={{0,1},{1,0},{2,3},{3,2},{4,5},{5,4},{6,7},{7,6},{8,9},{9,8},{10,11... | collective-permute-start | bytes 1544 | tf_op jit(solution)/shard_map/ppermute | solution.py:547
  0.7 3.3 %collective-permute-start.3 = (f32[256,128]{1,0:T(8,128)}, f32[256,128]{1,0:T(8,128)S(1)}, u32[]{:S(2)}, u32[]{:S(2)}) collective-permute-start(f32[256,128]{1,0:T(8,128)} %sense_own.1), channel_id=1, source_target_pairs={{0,1},{1,0},{2,3},{3,2},{4,5},{5,4},{6,7},{7,6},{8,9},{9,8},{10,11... | collective-permute-start | bytes 393224 | tf_op jit(solution)/shard_map/ppermute | solution.py:547
  1.2 2.8 %collective-permute-start.2 = (f32[128,256]{1,0:T(8,128)}, f32[128,256]{1,0:T(8,128)S(1)}, u32[]{:S(2)}, u32[]{:S(2)}) collective-permute-start(f32[128,256]{1,0:T(8,128)} %gain_own.1), channel_id=1, source_target_pairs={{0,1},{1,0},{2,3},{3,2},{4,5},{5,4},{6,7},{7,6},{8,9},{9,8},{10,11... | collective-permute-start | bytes 393224 | tf_op jit(solution)/shard_map/ppermute | solution.py:547
  3.8 46.1 %copy-start.1 = (f32[128,128]{1,0:T(8,128)S(1)}, f32[128,128]{1,0:T(8,128)}, u32[]{:S(2)}) copy-start(f32[128,128]{1,0:T(8,128)} %trans.3) | copy-start | bytes 196612
  3.8 46.1 %copy-start.3 = (f32[128]{0:T(128)S(1)}, f32[128]{0:T(128)}, u32[]{:S(2)}) copy-start(f32[128]{0:T(128)} %param.13) | copy-start | bytes 1540
  3.8 5.6 %collective-permute-start.1 = (f32[256,128]{1,0:T(8,128)S(1)}, f32[256,128]{1,0:T(8,128)S(1)}, u32[]{:S(2)}, u32[]{:S(2)}) collective-permute-start(f32[256,128]{1,0:T(8,128)S(1)} %get-tuple-element.23), channel_id=1, source_target_pairs={{0,1},{1,0},{2,3},{3,2},{4,5},{5,4},{6,7},{7,6},{8,9},{9,8},{10,11... | collective-permute-start | bytes 393224 | tf_op jit(solution)/shard_map/ppermute | solution.py:547
  11.4 1.3 %collective-permute-start.4 = (f32[136,128]{1,0:T(8,128)S(1)}, f32[136,128]{1,0:T(8,128)S(1)}, u32[]{:S(2)}, u32[]{:S(2)}) collective-permute-start(f32[136,128]{1,0:T(8,128)S(1)} %get-tuple-element.26.own), channel_id=1, source_target_pairs={{0,1},{1,0},{2,3},{3,2},{4,5},{5,4},{6,7},{7,6},{8,9},{9,8},{10,11... | collective-permute-start | bytes 208904 | tf_op jit(solution)/shard_map/ppermute | solution.py:547
  30.7 36.6 %copy-start = (f32[512,256]{1,0:T(8,128)S(1)}, f32[512,256]{1,0:T(8,128)}, u32[]{:S(2)}) copy-start(f32[512,256]{1,0:T(8,128)} %tel.3) | copy-start | bytes 1572868
  30.7 36.6 %copy-start.2 = (s32[32,4]{0,1:T(4,128)S(1)}, s32[32,4]{0,1:T(4,128)}, u32[]{:S(2)}) copy-start(s32[32,4]{0,1:T(4,128)} %param.8) | copy-start | bytes 1540
  54.0 13.3 %collective-permute-start.5 = (f32[264,128]{1,0:T(8,128)S(1)}, f32[264,128]{1,0:T(8,128)S(1)}, u32[]{:S(2)}, u32[]{:S(2)}) collective-permute-start(f32[264,128]{1,0:T(8,128)S(1)} %get-tuple-element.36.own), channel_id=1, source_target_pairs={{0,1},{1,0},{2,3},{3,2},{4,5},{5,4},{6,7},{7,6},{8,9},{9,8},{10,11... | collective-permute-start | bytes 405512 | tf_op jit(solution)/shard_map/ppermute | solution.py:547
